TPU v7x, 512 devices: a whole 4x8x8 slice. The times are simulated.
512 devices in a mesh: chain: 64 (over y, x, core), cols: 8 (over z).
Axes of the slice: x: 4, y: 8, z: 8, core: 2. Of those that a mesh axis runs over, the one named last changes fastest.
Arguments:
- start_vectors: float32 [1024, 256, 256], P('chain', 'cols'), may hold values from -6 to 6
- factors: float32 [1024, 256, 256], P('chain', 'cols'), may hold values from -1.2 to 1.2, as said below
Outputs:
- vectors: float32 [1024, 256, 256], P('chain', 'cols')
- log_growth: float32 [256], P('cols')
Inputs may be any that keep to these rules, and one draw needn't show every extreme that they name: `factors`: the factor blocks of the shifted operator; every product of consecutive factor blocks is bounded.
All inputs are finite; a program needn't handle non-finite values.
Results may differ from a plain program's by a relative error of at most 0.0003.
Values sent between devices are 32-bit elements; how exact they have to be, the bound alone decides.
No kernel may reach another device: no remote copies, remote signals or barrier semaphores. Data moves between devices by JAX's collectives and lax.ppermute only.
A program may use at most 128 MiB of HBM per device.

v0:
```python
import jax
import jax.numpy as jnp
from jax import lax
from jax.sharding import PartitionSpec as P

eps_value = 1e-06


def from_behind(block, axis, distance):
    devices = range(lax.axis_size(axis))
    route = [(i - distance, i) for i in devices if i - distance in devices]
    return lax.ppermute(block, axis, route)


def transform(matrix, vectors_in):
    return lax.dot_general(
        vectors_in,
        matrix,
        (((1,), (1,)), ((), ())),
        precision=lax.Precision.HIGHEST,
        preferred_element_type=jnp.float32,
    )


def compose(later, earlier):
    return jnp.dot(
        later, earlier, precision=lax.Precision.HIGHEST, preferred_element_type=jnp.float32
    )


def forward_rows(factors, right_side, incoming):

    def forward_advance(carried, element):
        matrix, source = element
        carried = transform(matrix, carried) + source
        return (carried, carried)

    return lax.scan(forward_advance, incoming, (factors, right_side))


def backward_rows(factors, forward, incoming):

    def backward_advance(carried, element):
        matrix, source = element
        carried = transform(matrix, source + carried)
        return (carried, carried)

    return lax.scan(backward_advance, incoming, (factors, forward), reverse=True)


def chain_operator(factors, reverse):
    identity_block = jnp.eye(factors.shape[1], dtype=jnp.float32)

    def chain_advance(running, matrix):
        return (compose(matrix, running), None)

    running, _ = lax.scan(chain_advance, identity_block, factors, reverse=reverse)
    return running


def section_count():
    return (lax.axis_size("chain") - 1).bit_length()


def enter_state(summary, direction):
    return from_behind(summary, "chain", direction)


def solve_system(factors, right_side, prefix_forward, prefix_backward):
    zero_state = jnp.zeros(right_side.shape[1:], jnp.float32)
    local_last, _ = forward_rows(factors, right_side, zero_state)
    incoming = enter_state(prefix_forward(local_last), 1)
    _, forward = forward_rows(factors, right_side, incoming)
    local_first, _ = backward_rows(factors, forward, zero_state)
    incoming_back = enter_state(prefix_backward(local_first), -1)
    _, solved = backward_rows(factors, forward, incoming_back)
    return solved


def shards(start_vectors, factors):
    full_factors = lax.all_gather(factors, "cols", axis=1, tiled=True)

    def pair_prefix(operator, summary, direction):
        sections = section_count()
        for section_index in range(sections):
            distance = direction * (1 << section_index)
            if section_index + 1 < sections:
                received_op, received_sum = from_behind((operator, summary), "chain", distance)
                summary = transform(operator, received_sum) + summary
                operator = compose(operator, received_op)
            else:
                received_sum = from_behind(summary, "chain", distance)
                summary = transform(operator, received_sum) + summary
        return summary

    def prefix_forward(summary):
        return pair_prefix(chain_operator(full_factors, False), summary, 1)

    def prefix_backward(summary):
        return pair_prefix(chain_operator(full_factors, True), summary, -1)

    cell_count = start_vectors.shape[0] * lax.axis_size("chain") * start_vectors.shape[2]
    first_solve = solve_system(full_factors, start_vectors, prefix_forward, prefix_backward)
    first_squares = lax.psum(jnp.sum(first_solve * first_solve, axis=(0, 2)), "chain")
    scale_one = jnp.sqrt(first_squares / cell_count + eps_value)
    second_solve = solve_system(
        full_factors, first_solve / scale_one[None, :, None], prefix_forward, prefix_backward
    )
    second_squares = lax.psum(jnp.sum(second_solve * second_solve, axis=(0, 2)), "chain")
    scale_two = jnp.sqrt(second_squares / cell_count + eps_value)
    result_vectors = second_solve / scale_two[None, :, None]
    return (result_vectors, jnp.log(scale_two))


def solution(mesh):
    return jax.shard_map(
        shards,
        mesh=mesh,
        in_specs=(P("chain", "cols", None), P("chain", "cols", None)),
        out_specs=(P("chain", "cols", None), P("cols")),
        check_vma=False,
    )
```

profile of v0, /device:TPU:1, one launch (start us, length us, event | category | flops | bytes accessed | tf_op | source)
XLA Modules:
  0.0 803.1 jit_solution(6026892274242298097)
XLA Ops:
  8.0 65.9 %all-gather.2.cloned.1.call-done = f32[16,256,256]{2,1,0:T(8,128)} async-done(((f32[16,32,256]{2,1,0:T(8,128)}), f32[16,256,256]{2,1,0:T(8,128)}) %all-gather.2.cloned.1.call-update) | async-done | bytes 4194320 | tf_op jit(solution)/shard_map/all_gather | solution.py:81
  73.9 21.4 %while.146 = (s32[]{:T(128)}, f32[32,256]{1,0:T(8,128)S(1)}, f32[16,256,256]{2,1,0:T(8,128)}, f32[16,32,256]{2,1,0:T(8,128)}, s32[]{:T(128)}, /*index=5*/s32[]{:T(128)}) while((s32[]{:T(128)}, f32[32,256]{1,0:T(8,128)S(1)}, f32[16,256,256]{2,1,0:T(8,128)}, f32[16,32,256]{2,1,0:T(8,128)}, s32[]{:T(128)}, /*index=5*/s32[]{:T(128)}) %tuple.241), condition=%wide.region_1.2_spmd.clone, body=%wide.region_0.1_spmd.clone.sunk | while | flops 25182212 | bytes 427087 | solution.py:38
  99.0 22.1 %while.138 = (s32[]{:T(128)}, f32[256,256]{1,0:T(8,128)S(1)}, f32[16,256,256]{2,1,0:T(8,128)}, s32[]{:T(128)}) while((s32[]{:T(128)}, f32[256,256]{1,0:T(8,128)S(1)}, f32[16,256,256]{2,1,0:T(8,128)}, s32[]{:T(128)}) %tuple.273), condition=%wide.region_3.4_spmd, body=%wide.region_2.3_spmd.sunk | while | flops 201326592 | bytes 1311285 | solution.py:57
  130.2 4.5 collective-permute-start.3
  135.0 4.7 collective-permute-start.6
  143.6 5.9 collective-permute-start.8
  154.3 6.5 collective-permute-start.10
  161.2 6.0 collective-permute-start.9
  168.5 10.4 %collective-permute-start.11 = (f32[32,256]{1,0:T(8,128)S(1)}, f32[32,256]{1,0:T(8,128)S(1)}, u32[]{:S(2)}, u32[]{:S(2)}) collective-permute-start(f32[32,256]{1,0:T(8,128)S(1)} %convolution_add_fusion.18), channel_id=1, source_target_pairs={{0,8},{8,16},{16,24},{24,32},{32,40},{40,48},{48,56},{56,64},{64,7... | collective-permute-start | bytes 98312 | tf_op jit(solution)/shard_map/ppermute | solution.py:12
  178.9 6.2 collective-permute-done.11
  185.2 21.4 %while.139 = (s32[]{:T(128)}, f32[32,256]{1,0:T(8,128)S(1)}, f32[16,32,256]{2,1,0:T(8,128)S(1)}, f32[16,256,256]{2,1,0:T(8,128)}, f32[16,32,256]{2,1,0:T(8,128)}, /*index=5*/s32[]{:T(128)}) while((s32[]{:T(128)}, f32[32,256]{1,0:T(8,128)S(1)}, f32[16,32,256]{2,1,0:T(8,128)S(1)}, f32[16,256,256]{2,1,0:T(8,128)}, f32[16,32,256]{2,1,0:T(8,128)}, ...), condition=%wide.region_5.6_spmd, body=%wide.region_4.5_spmd.sunk | while | flops 25174016 | bytes 459845 | solution.py:38
  206.7 21.3 %while.140 = (s32[]{:T(128)}, f32[32,256]{1,0:T(8,128)S(1)}, f32[16,32,256]{2,1,0:T(8,128)S(1)}, f32[16,256,256]{2,1,0:T(8,128)}, s32[]{:T(128)}, /*index=5*/s32[]{:T(128)}) while((s32[]{:T(128)}, f32[32,256]{1,0:T(8,128)S(1)}, f32[16,32,256]{2,1,0:T(8,128)S(1)}, f32[16,256,256]{2,1,0:T(8,128)}, s32[]{:T(128)}, /*index=5*/s32[]{:T(128)}) %tuple.275), condition=%wide.region_7.8_spmd, body=%wide.region_6.7_spmd.sunk | while | flops 25174020 | bytes 427089 | solution.py:48
  230.1 22.1 %while.141 = (s32[]{:T(128)}, f32[256,256]{1,0:T(8,128)S(1)}, f32[16,256,256]{2,1,0:T(8,128)}, s32[]{:T(128)}, s32[]{:T(128)}) while((s32[]{:T(128)}, f32[256,256]{1,0:T(8,128)S(1)}, f32[16,256,256]{2,1,0:T(8,128)}, s32[]{:T(128)}, s32[]{:T(128)}) %tuple.276), condition=%wide.region_9.10_spmd, body=%wide.region_8.9_spmd.sunk | while | flops 201326592 | bytes 1310797 | solution.py:57
  255.8 4.4 collective-permute-done.14
  263.6 5.6 collective-permute-done.16
  272.6 8.3 %collective-permute-done.18 = f32[256,256]{1,0:T(8,128)S(1)} collective-permute-done((f32[256,256]{1,0:T(8,128)S(1)}, f32[256,256]{1,0:T(8,128)S(1)}, u32[]{:S(2)}, u32[]{:S(2)}) %collective-permute-start.18) | collective-permute-done | bytes 262176 | tf_op jit(solution)/shard_map/ppermute | solution.py:12
  285.2 10.0 %collective-permute-done.20 = f32[256,256]{1,0:T(8,128)S(1)} collective-permute-done((f32[256,256]{1,0:T(8,128)S(1)}, f32[256,256]{1,0:T(8,128)S(1)}, u32[]{:S(2)}, u32[]{:S(2)}) %collective-permute-start.20) | collective-permute-done | bytes 262176 | tf_op jit(solution)/shard_map/ppermute | solution.py:12
  298.5 9.3 %collective-permute-done.22 = f32[256,256]{1,0:T(8,128)S(1)} collective-permute-done((f32[256,256]{1,0:T(8,128)S(1)}, f32[256,256]{1,0:T(8,128)S(1)}, u32[]{:S(2)}, u32[]{:S(2)}) %collective-permute-start.22) | collective-permute-done | bytes 262176 | tf_op jit(solution)/shard_map/ppermute | solution.py:12
  314.9 21.6 %while.142 = (s32[]{:T(128)}, f32[32,256]{1,0:T(8,128)S(1)}, f32[16,32,256]{2,1,0:T(8,128)S(1)}, f32[16,32,256]{2,1,0:T(8,128)}, f32[16,256,256]{2,1,0:T(8,128)}, /*index=5*/s32[]{:T(128)}, s32[]{:T(128)}) while((s32[]{:T(128)}, f32[32,256]{1,0:T(8,128)S(1)}, f32[16,32,256]{2,1,0:T(8,128)S(1)}, f32[16,32,256]{2,1,0:T(8,128)}, ...), condition=%wide.region_11.12_spmd, body=%wide.region_10.11_spmd.sunk | while | flops 25174020 | bytes 460377 | solution.py:48
  336.7 123.3 %psum.14 = f32[32]{0:T(128)S(1)} all-reduce(f32[32]{0:T(128)S(1)} %multiply_reduce_fusion.1), channel_id=1, replica_groups=mesh['chain'=64,'cols'=8] {'chain'}, use_global_device_ids=true, to_apply=%region_13.14 | all-reduce | flops 32 | bytes 256 | tf_op jit(solution)/shard_map/psum | solution.py:104
  460.9 21.5 %while.147 = (s32[]{:T(128)}, f32[32,256]{1,0:T(8,128)S(1)}, f32[16,256,256]{2,1,0:T(8,128)}, f32[16,32,256]{2,1,0:T(8,128)}, s32[]{:T(128)}, /*index=5*/s32[]{:T(128)}) while((s32[]{:T(128)}, f32[32,256]{1,0:T(8,128)S(1)}, f32[16,256,256]{2,1,0:T(8,128)}, f32[16,32,256]{2,1,0:T(8,128)}, s32[]{:T(128)}, ...), condition=%wide.region_15.16_spmd.clone, body=%wide.region_14.15_spmd.clone.sunk | while | flops 25182212 | bytes 427087 | solution.py:38
  500.2 21.9 %collective-permute-start.28 = (f32[32,256]{1,0:T(8,128)S(1)}, f32[32,256]{1,0:T(8,128)S(1)}, u32[]{:S(2)}, u32[]{:S(2)}) collective-permute-start(f32[32,256]{1,0:T(8,128)S(1)} %convolution_add_fusion.8), channel_id=1, source_target_pairs={{0,128},{8,136},{16,144},{24,152},{32,160},{40,168},{48,176},{56,1... | collective-permute-start | bytes 98312 | tf_op jit(solution)/shard_map/ppermute | solution.py:12
  523.5 15.5 %collective-permute-start.29 = (f32[32,256]{1,0:T(8,128)S(1)}, f32[32,256]{1,0:T(8,128)S(1)}, u32[]{:S(2)}, u32[]{:S(2)}) collective-permute-start(f32[32,256]{1,0:T(8,128)S(1)} %convolution_add_fusion.7), channel_id=1, source_target_pairs={{0,256},{8,264},{16,272},{24,280},{32,288},{40,296},{48,304},{56,3... | collective-permute-start | bytes 98312 | tf_op jit(solution)/shard_map/ppermute | solution.py:12
  540.2 9.5 %collective-permute-start.30 = (f32[32,256]{1,0:T(8,128)S(1)}, f32[32,256]{1,0:T(8,128)S(1)}, u32[]{:S(2)}, u32[]{:S(2)}) collective-permute-start(f32[32,256]{1,0:T(8,128)S(1)} %convolution_add_fusion.6), channel_id=1, source_target_pairs={{0,8},{8,16},{16,24},{24,32},{32,40},{40,48},{48,56},{56,64},{64,7... | collective-permute-start | bytes 98312 | tf_op jit(solution)/shard_map/ppermute | solution.py:12
  553.1 21.4 %while.143 = (s32[]{:T(128)}, f32[32,256]{1,0:T(8,128)S(1)}, f32[16,32,256]{2,1,0:T(8,128)S(1)}, f32[16,256,256]{2,1,0:T(8,128)}, f32[16,32,256]{2,1,0:T(8,128)}, /*index=5*/s32[]{:T(128)}) while((s32[]{:T(128)}, f32[32,256]{1,0:T(8,128)S(1)}, f32[16,32,256]{2,1,0:T(8,128)S(1)}, f32[16,256,256]{2,1,0:T(8,128)}, f32[16,32,256]{2,1,0:T(8,128)}, ...), condition=%wide.region_17.18_spmd, body=%wide.region_16.17_spmd.sunk | while | flops 25174016 | bytes 459845 | solution.py:38
  574.5 21.3 %while.144 = (s32[]{:T(128)}, f32[32,256]{1,0:T(8,128)S(1)}, f32[16,32,256]{2,1,0:T(8,128)S(1)}, f32[16,256,256]{2,1,0:T(8,128)}, s32[]{:T(128)}, /*index=5*/s32[]{:T(128)}) while((s32[]{:T(128)}, f32[32,256]{1,0:T(8,128)S(1)}, f32[16,32,256]{2,1,0:T(8,128)S(1)}, f32[16,256,256]{2,1,0:T(8,128)}, s32[]{:T(128)}, /*index=5*/s32[]{:T(128)}) %tuple.280), condition=%wide.region_19.20_spmd, body=%wide.region_18.19_spmd.sunk | while | flops 25174020 | bytes 427089 | solution.py:48
  607.7 6.1 collective-permute-done.33
  615.5 5.0 collective-permute-done.34
  622.1 8.0 collective-permute-done.35
  631.8 8.9 %collective-permute-done.36 = f32[32,256]{1,0:T(8,128)S(1)} collective-permute-done((f32[32,256]{1,0:T(8,128)S(1)}, f32[32,256]{1,0:T(8,128)S(1)}, u32[]{:S(2)}, u32[]{:S(2)}) %collective-permute-start.36) | collective-permute-done | bytes 32800 | tf_op jit(solution)/shard_map/ppermute | solution.py:12
  647.0 21.3 %while.145 = (s32[]{:T(128)}, f32[32,256]{1,0:T(8,128)S(1)}, f32[16,32,256]{2,1,0:T(8,128)S(1)}, f32[16,32,256]{2,1,0:T(8,128)S(1)}, f32[16,256,256]{2,1,0:T(8,128)}, /*index=5*/s32[]{:T(128)}, s32[]{:T(128)}) while((s32[]{:T(128)}, f32[32,256]{1,0:T(8,128)S(1)}, f32[16,32,256]{2,1,0:T(8,128)S(1)}, f32[16,32,256]{2,1,0:T(8,128)S(1)}, ...), condition=%wide.region_21.22_spmd, body=%wide.region_20.21_spmd.sunk | while | flops 25174020 | bytes 460377 | solution.py:48
  668.4 126.4 %psum.15 = f32[32]{0:T(128)S(1)} all-reduce(f32[32]{0:T(128)S(1)} %multiply_reduce_fusion), channel_id=1, replica_groups=mesh['chain'=64,'cols'=8] {'chain'}, use_global_device_ids=true, to_apply=%region_23.24 | all-reduce | flops 32 | bytes 256 | tf_op jit(solution)/shard_map/psum | solution.py:109
  (435 shorter events, 311.0 us)
Async XLA Ops:
  7.2 66.7 %all-gather.2.cloned.1.call-start = ((), (), s32[]{:S(2)}) async-start(), calls=%async_computation | async-start | bytes 4718592 | tf_op jit(solution)/shard_map/all_gather | solution.py:81
  95.3 27.7 %collective-permute-start = (f32[32,256]{1,0:T(8,128)S(1)}, f32[32,256]{1,0:T(8,128)S(1)}, u32[]{:S(2)}, u32[]{:S(2)}) collective-permute-start(f32[32,256]{1,0:T(8,128)S(1)} %get-tuple-element.568), channel_id=1, source_target_pairs={{0,8},{8,16},{16,24},{24,32},{32,40},{40,48},{48,56},{56,64},{64,7... | collective-permute-start | bytes 98312 | tf_op jit(solution)/shard_map/ppermute | solution.py:12
  123.4 6.4 collective-permute-start.1
  126.9 7.8 collective-permute-start.4
  130.2 9.6 %collective-permute-start.3 = (f32[32,256]{1,0:T(8,128)S(1)}, f32[32,256]{1,0:T(8,128)S(1)}, u32[]{:S(2)}, u32[]{:S(2)}) collective-permute-start(f32[32,256]{1,0:T(8,128)S(1)} %convolution_add_fusion.22), channel_id=1, source_target_pairs={{0,32},{8,40},{16,48},{24,56},{32,64},{40,72},{48,80},{56,88},{64,... | collective-permute-start | bytes 98312 | tf_op jit(solution)/shard_map/ppermute | solution.py:12
  135.0 8.2 %collective-permute-start.6 = (f32[256,256]{1,0:T(8,128)S(1)}, f32[256,256]{1,0:T(8,128)S(1)}, u32[]{:S(2)}, u32[]{:S(2)}) collective-permute-start(f32[256,256]{1,0:T(8,128)S(1)} %fusion.55), channel_id=1, source_target_pairs={{0,32},{8,40},{16,48},{24,56},{32,64},{40,72},{48,80},{56,88},{64,... | collective-permute-start | bytes 786440 | tf_op jit(solution)/shard_map/ppermute | solution.py:12
  140.1 9.4 %collective-permute-start.5 = (f32[32,256]{1,0:T(8,128)S(1)}, f32[32,256]{1,0:T(8,128)S(1)}, u32[]{:S(2)}, u32[]{:S(2)}) collective-permute-start(f32[32,256]{1,0:T(8,128)S(1)} %convolution_add_fusion.21), channel_id=1, source_target_pairs={{0,64},{8,72},{16,80},{24,88},{32,96},{40,104},{48,112},{56,120},{... | collective-permute-start | bytes 98312 | tf_op jit(solution)/shard_map/ppermute | solution.py:12
  143.6 10.3 %collective-permute-start.8 = (f32[256,256]{1,0:T(8,128)S(1)}, f32[256,256]{1,0:T(8,128)S(1)}, u32[]{:S(2)}, u32[]{:S(2)}) collective-permute-start(f32[256,256]{1,0:T(8,128)S(1)} %fusion.56), channel_id=1, source_target_pairs={{0,64},{8,72},{16,80},{24,88},{32,96},{40,104},{48,112},{56,120},{... | collective-permute-start | bytes 786440 | tf_op jit(solution)/shard_map/ppermute | solution.py:12
  149.9 10.9 %collective-permute-start.7 = (f32[32,256]{1,0:T(8,128)S(1)}, f32[32,256]{1,0:T(8,128)S(1)}, u32[]{:S(2)}, u32[]{:S(2)}) collective-permute-start(f32[32,256]{1,0:T(8,128)S(1)} %convolution_add_fusion.20), channel_id=1, source_target_pairs={{0,128},{8,136},{16,144},{24,152},{32,160},{40,168},{48,176},{56,1... | collective-permute-start | bytes 98312 | tf_op jit(solution)/shard_map/ppermute | solution.py:12
  154.3 12.9 %collective-permute-start.10 = (f32[256,256]{1,0:T(8,128)S(1)}, f32[256,256]{1,0:T(8,128)S(1)}, u32[]{:S(2)}, u32[]{:S(2)}) collective-permute-start(f32[256,256]{1,0:T(8,128)S(1)} %fusion.57), channel_id=1, source_target_pairs={{0,128},{8,136},{16,144},{24,152},{32,160},{40,168},{48,176},{56,1... | collective-permute-start | bytes 786440 | tf_op jit(solution)/shard_map/ppermute | solution.py:12
  161.2 7.0 collective-permute-start.9
  168.5 16.6 %collective-permute-start.11 = (f32[32,256]{1,0:T(8,128)S(1)}, f32[32,256]{1,0:T(8,128)S(1)}, u32[]{:S(2)}, u32[]{:S(2)}) collective-permute-start(f32[32,256]{1,0:T(8,128)S(1)} %convolution_add_fusion.18), channel_id=1, source_target_pairs={{0,8},{8,16},{16,24},{24,32},{32,40},{40,48},{48,56},{56,64},{64,7... | collective-permute-start | bytes 98312 | tf_op jit(solution)/shard_map/ppermute | solution.py:12
  228.0 26.2 %collective-permute-start.12 = (f32[32,256]{1,0:T(8,128)S(1)}, f32[32,256]{1,0:T(8,128)S(1)}, u32[]{:S(2)}, u32[]{:S(2)}) collective-permute-start(f32[32,256]{1,0:T(8,128)S(1)} %get-tuple-element.571), channel_id=1, source_target_pairs={{8,0},{16,8},{24,16},{32,24},{40,32},{48,40},{56,48},{64,56},{72,6... | collective-permute-start | bytes 98312 | tf_op jit(solution)/shard_map/ppermute | solution.py:12
  252.2 8.0 %collective-permute-start.14 = (f32[256,256]{1,0:T(8,128)S(1)}, f32[256,256]{1,0:T(8,128)S(1)}, u32[]{:S(2)}, u32[]{:S(2)}) collective-permute-start(f32[256,256]{1,0:T(8,128)S(1)} %get-tuple-element.572), channel_id=1, source_target_pairs={{8,0},{16,8},{24,16},{32,24},{40,32},{48,40},{56,48},{64,56},{72,6... | collective-permute-start | bytes 786440 | tf_op jit(solution)/shard_map/ppermute | solution.py:12
  254.5 7.4 collective-permute-start.13
  260.6 8.6 %collective-permute-start.16 = (f32[256,256]{1,0:T(8,128)S(1)}, f32[256,256]{1,0:T(8,128)S(1)}, u32[]{:S(2)}, u32[]{:S(2)}) collective-permute-start(f32[256,256]{1,0:T(8,128)S(1)} %fusion.59), channel_id=1, source_target_pairs={{16,0},{24,8},{32,16},{40,24},{48,32},{56,40},{64,48},{72,56},{80,... | collective-permute-start | bytes 786440 | tf_op jit(solution)/shard_map/ppermute | solution.py:12
  262.3 8.6 %collective-permute-start.15 = (f32[32,256]{1,0:T(8,128)S(1)}, f32[32,256]{1,0:T(8,128)S(1)}, u32[]{:S(2)}, u32[]{:S(2)}) collective-permute-start(f32[32,256]{1,0:T(8,128)S(1)} %convolution_add_fusion.16), channel_id=1, source_target_pairs={{32,0},{40,8},{48,16},{56,24},{64,32},{72,40},{80,48},{88,56},{96,... | collective-permute-start | bytes 98312 | tf_op jit(solution)/shard_map/ppermute | solution.py:12
  269.6 11.2 %collective-permute-start.18 = (f32[256,256]{1,0:T(8,128)S(1)}, f32[256,256]{1,0:T(8,128)S(1)}, u32[]{:S(2)}, u32[]{:S(2)}) collective-permute-start(f32[256,256]{1,0:T(8,128)S(1)} %fusion.60), channel_id=1, source_target_pairs={{32,0},{40,8},{48,16},{56,24},{64,32},{72,40},{80,48},{88,56},{96,... | collective-permute-start | bytes 786440 | tf_op jit(solution)/shard_map/ppermute | solution.py:12
  271.3 12.3 %collective-permute-start.17 = (f32[32,256]{1,0:T(8,128)S(1)}, f32[32,256]{1,0:T(8,128)S(1)}, u32[]{:S(2)}, u32[]{:S(2)}) collective-permute-start(f32[32,256]{1,0:T(8,128)S(1)} %convolution_add_fusion.15), channel_id=1, source_target_pairs={{64,0},{72,8},{80,16},{88,24},{96,32},{104,40},{112,48},{120,56},{... | collective-permute-start | bytes 98312 | tf_op jit(solution)/shard_map/ppermute | solution.py:12
  281.2 13.9 %collective-permute-start.20 = (f32[256,256]{1,0:T(8,128)S(1)}, f32[256,256]{1,0:T(8,128)S(1)}, u32[]{:S(2)}, u32[]{:S(2)}) collective-permute-start(f32[256,256]{1,0:T(8,128)S(1)} %fusion.61), channel_id=1, source_target_pairs={{64,0},{72,8},{80,16},{88,24},{96,32},{104,40},{112,48},{120,56},{... | collective-permute-start | bytes 786440 | tf_op jit(solution)/shard_map/ppermute | solution.py:12
  283.9 12.9 %collective-permute-start.19 = (f32[32,256]{1,0:T(8,128)S(1)}, f32[32,256]{1,0:T(8,128)S(1)}, u32[]{:S(2)}, u32[]{:S(2)}) collective-permute-start(f32[32,256]{1,0:T(8,128)S(1)} %convolution_add_fusion.14), channel_id=1, source_target_pairs={{128,0},{136,8},{144,16},{152,24},{160,32},{168,40},{176,48},{184,... | collective-permute-start | bytes 98312 | tf_op jit(solution)/shard_map/ppermute | solution.py:12
  295.5 12.3 %collective-permute-start.22 = (f32[256,256]{1,0:T(8,128)S(1)}, f32[256,256]{1,0:T(8,128)S(1)}, u32[]{:S(2)}, u32[]{:S(2)}) collective-permute-start(f32[256,256]{1,0:T(8,128)S(1)} %fusion.62), channel_id=1, source_target_pairs={{128,0},{136,8},{144,16},{152,24},{160,32},{168,40},{176,48},{184,... | collective-permute-start | bytes 786440 | tf_op jit(solution)/shard_map/ppermute | solution.py:12
  297.2 11.6 %collective-permute-start.21 = (f32[32,256]{1,0:T(8,128)S(1)}, f32[32,256]{1,0:T(8,128)S(1)}, u32[]{:S(2)}, u32[]{:S(2)}) collective-permute-start(f32[32,256]{1,0:T(8,128)S(1)} %convolution_add_fusion.13), channel_id=1, source_target_pairs={{256,0},{264,8},{272,16},{280,24},{288,32},{296,40},{304,48},{312,... | collective-permute-start | bytes 98312 | tf_op jit(solution)/shard_map/ppermute | solution.py:12
  482.4 6.9 collective-permute-start.24
  500.2 22.9 %collective-permute-start.28 = (f32[32,256]{1,0:T(8,128)S(1)}, f32[32,256]{1,0:T(8,128)S(1)}, u32[]{:S(2)}, u32[]{:S(2)}) collective-permute-start(f32[32,256]{1,0:T(8,128)S(1)} %convolution_add_fusion.8), channel_id=1, source_target_pairs={{0,128},{8,136},{16,144},{24,152},{32,160},{40,168},{48,176},{56,1... | collective-permute-start | bytes 98312 | tf_op jit(solution)/shard_map/ppermute | solution.py:12
  523.5 16.3 %collective-permute-start.29 = (f32[32,256]{1,0:T(8,128)S(1)}, f32[32,256]{1,0:T(8,128)S(1)}, u32[]{:S(2)}, u32[]{:S(2)}) collective-permute-start(f32[32,256]{1,0:T(8,128)S(1)} %convolution_add_fusion.7), channel_id=1, source_target_pairs={{0,256},{8,264},{16,272},{24,280},{32,288},{40,296},{48,304},{56,3... | collective-permute-start | bytes 98312 | tf_op jit(solution)/shard_map/ppermute | solution.py:12
  540.2 12.9 %collective-permute-start.30 = (f32[32,256]{1,0:T(8,128)S(1)}, f32[32,256]{1,0:T(8,128)S(1)}, u32[]{:S(2)}, u32[]{:S(2)}) collective-permute-start(f32[32,256]{1,0:T(8,128)S(1)} %convolution_add_fusion.6), channel_id=1, source_target_pairs={{0,8},{8,16},{16,24},{24,32},{32,40},{40,48},{48,56},{56,64},{64,7... | collective-permute-start | bytes 98312 | tf_op jit(solution)/shard_map/ppermute | solution.py:12
  606.4 7.4 collective-permute-start.33
  614.2 6.3 collective-permute-start.34
  620.8 9.3 %collective-permute-start.35 = (f32[32,256]{1,0:T(8,128)S(1)}, f32[32,256]{1,0:T(8,128)S(1)}, u32[]{:S(2)}, u32[]{:S(2)}) collective-permute-start(f32[32,256]{1,0:T(8,128)S(1)} %convolution_add_fusion.2), channel_id=1, source_target_pairs={{128,0},{136,8},{144,16},{152,24},{160,32},{168,40},{176,48},{184,... | collective-permute-start | bytes 98312 | tf_op jit(solution)/shard_map/ppermute | solution.py:12
  630.5 10.2 %collective-permute-start.36 = (f32[32,256]{1,0:T(8,128)S(1)}, f32[32,256]{1,0:T(8,128)S(1)}, u32[]{:S(2)}, u32[]{:S(2)}) collective-permute-start(f32[32,256]{1,0:T(8,128)S(1)} %convolution_add_fusion.1), channel_id=1, source_target_pairs={{256,0},{264,8},{272,16},{280,24},{288,32},{296,40},{304,48},{312,... | collective-permute-start | bytes 98312 | tf_op jit(solution)/shard_map/ppermute | solution.py:12
  641.0 5.9 collective-permute-start.37
  (10 other events, 211.4 us)
Sparse Core Ops, SparseCore 0:
  10.1 63.7 all-gather.1
where the time goes:
time: 818 us; the launch traced here: 803 us
  blocking collectives  250 us (31%)
  matrix products  221 us (27%)
  waiting for transfers between devices  163 us (20%)
  starting transfers between devices  145 us (18%)
  between operations  14.9 us (2%)
    dot_general x152, matrix products, transform(): lax.dot_general(vectors_in, matrix, (((1,), (1,)), ((), ())), precision=l...  175 us
    ppermute x38, starting transfers between devices, from_behind(): return lax.ppermute(block, axis, route)  145 us
    psum x1, blocking collectives, shards(): lax.psum(jnp.sum(second_solve * second_solve, axis=(0, 2)), 'chain')  126 us
    psum x1, blocking collectives, shards(): lax.psum(jnp.sum(first_solve * first_solve, axis=(0, 2)), 'chain')  123 us
    ppermute x38, waiting for transfers between devices, from_behind(): return lax.ppermute(block, axis, route)  96.4 us
    all_gather x1, waiting for transfers between devices, shards(): full_factors = lax.all_gather(factors, 'cols', axis=1, tiled=True)  65.9 us
    dot_general x42, matrix products, compose(): jnp.dot(later, earlier, precision=lax.Precision.HIGHEST, preferred_elemen...  46.4 us
  transfers between devices with their start and end apart: 39, of which 25 were waited for; matrix products, arithmetic and copies ran while one was open for 6% of the time, Pallas kernels for 0%

commit v1 on v0

v1 whole, which is shorter than its diff:
```python
import functools

import jax
import jax.numpy as jnp
from jax import lax
from jax.experimental import pallas as pl
from jax.experimental.pallas import tpu as pltpu
from jax.sharding import Mesh, PartitionSpec as P

eps_value = 1e-06
VMEM_BYTES = 56 * 1024 * 1024


def split(value):
    high = value.astype(jnp.bfloat16)
    low = (value - high.astype(jnp.float32)).astype(jnp.bfloat16)
    return high, low


def apply_split(state, high, low):
    rows = state.shape[0]
    state_high, state_low = split(state)
    both = jnp.dot(
        jnp.concatenate([state_high, state_low], axis=0),
        high,
        preferred_element_type=jnp.float32,
    )
    return (both[:rows] + both[rows:]) + jnp.dot(
        state_high, low, preferred_element_type=jnp.float32
    )


def matmul(left, right):
    return jnp.dot(
        left, right, precision=lax.Precision.HIGHEST, preferred_element_type=jnp.float32
    )


def call(body, out_shapes, scratch, flops, *operands):
    vmem = pl.BlockSpec(memory_space=pltpu.VMEM)
    touched = sum(x.size * x.dtype.itemsize for x in (*operands, *out_shapes))
    return pl.pallas_call(
        body,
        out_shape=tuple(out_shapes),
        in_specs=[vmem] * len(operands),
        out_specs=tuple([vmem] * len(out_shapes)),
        scratch_shapes=scratch,
        compiler_params=pltpu.CompilerParams(vmem_limit_bytes=VMEM_BYTES),
        cost_estimate=pl.CostEstimate(flops=flops, bytes_accessed=touched, transcendentals=0),
    )(*operands)


def shape(*dims, dtype=jnp.float32):
    return jax.ShapeDtypeStruct(dims, dtype)


def prepare_body(factors, source, high, low, forward, prefix, suffix, ahead, behind):
    rows, width, _ = factors.shape
    count = source.shape[1]

    def turn(i, _):
        turned = factors[i].T
        high[i], low[i] = split(turned)
        return 0

    lax.fori_loop(0, rows, turn, 0)
    eye = (
        lax.broadcasted_iota(jnp.int32, (width, width), 0)
        == lax.broadcasted_iota(jnp.int32, (width, width), 1)
    ).astype(jnp.float32)
    ahead[:count] = jnp.zeros((count, width), jnp.float32)
    ahead[count:] = eye
    behind[...] = eye

    def step(i, _):
        j = rows - 1 - i
        moved = apply_split(ahead[...], high[i], low[i])
        back = apply_split(behind[...], high[j], low[j])
        state = moved[:count] + source[i]
        forward[i] = state
        prefix[i] = moved[count:]
        ahead[:count] = state
        ahead[count:] = moved[count:]
        suffix[j] = back
        behind[...] = back
        return 0

    lax.fori_loop(0, rows, step, 0)


def prepare(factors, source):
    rows, width, _ = factors.shape
    count = source.shape[1]
    square = (rows, width, width)
    return call(
        prepare_body,
        [
            shape(*square, dtype=jnp.bfloat16),
            shape(*square, dtype=jnp.bfloat16),
            shape(*source.shape),
            shape(*square),
            shape(*square),
        ],
        [pltpu.VMEM((count + width, width), jnp.float32), pltpu.VMEM((width, width), jnp.float32)],
        rows * 6 * (count + 2 * width) * width * width,
        factors,
        source,
    )


def couple_body(high, low, forward, prefix, suffix, first_end, cross, turn, behind, ahead):
    rows, count, width = forward.shape
    ahead[...] = jnp.zeros_like(ahead)
    behind[...] = jnp.zeros_like(behind)

    def step(i, _):
        j = rows - 1 - i
        entering = jnp.concatenate([forward[j], prefix[j]], axis=0) + behind[...]
        behind[...] = apply_split(entering, high[j], low[j])
        ahead[...] = apply_split(ahead[...], high[i], low[i]) + suffix[i]
        return 0

    lax.fori_loop(0, rows, step, 0)
    first_end[...] = behind[:count]
    cross[...] = behind[count:]
    turn[...] = ahead[...]


def couple(high, low, forward, prefix, suffix):
    rows, count, width = forward.shape
    return call(
        couple_body,
        [shape(count, width), shape(width, width), shape(width, width)],
        [pltpu.VMEM((count + width, width), jnp.float32), pltpu.VMEM((width, width), jnp.float32)],
        rows * 6 * (count + 2 * width) * width * width,
        high,
        low,
        forward,
        prefix,
        suffix,
    )


def sweep_body(reverse, high, low, source, entering, result):
    rows = source.shape[0]

    def step(i, state):
        if reverse:
            j = rows - 1 - i
            state = apply_split(source[j] + state, high[j], low[j])
        else:
            j = i
            state = apply_split(state, high[j], low[j]) + source[j]
        result[j] = state
        return state

    lax.fori_loop(0, rows, step, entering[...], unroll=2)


def sweep(high, low, source, entering, reverse):
    rows, count, width = source.shape
    return call(
        functools.partial(sweep_body, reverse),
        [shape(*source.shape)],
        [],
        rows * 6 * count * width * width,
        high,
        low,
        source,
        entering,
    )[0]


def exchange(value, level):
    size = lax.axis_size("chain")
    return lax.ppermute(value, "chain", [(i, i ^ (1 << level)) for i in range(size)])


def levels():
    return (lax.axis_size("chain") - 1).bit_length()


def upper_at(level):
    return (lax.axis_index("chain") >> level) & 1 == 1


def compose_levels(operator, reverse):
    passing, leading = [], []
    lead = None
    for level in range(levels()):
        after = ~upper_at(level) if reverse else upper_at(level)
        leading.append(lead)
        if level + 1 == levels():
            passing.append(None)
            break
        received = exchange(operator, level)
        first = jnp.where(after, received, operator)
        second = jnp.where(after, operator, received)
        passing.append(second)
        if lead is None:
            eye = jnp.eye(operator.shape[0], dtype=jnp.float32)
            lead = jnp.where(after, received, eye)
        else:
            lead = jnp.where(after, matmul(received, lead), lead)
        operator = matmul(first, second)
    return passing, leading


def scan_blocks(total, passing, leading, reverse):
    entering = jnp.zeros_like(total)
    for level in range(levels()):
        after = ~upper_at(level) if reverse else upper_at(level)
        received = exchange(total, level)
        lead = leading[level]
        carried = received if lead is None else matmul(received, lead)
        entering = jnp.where(after, entering + carried, entering)
        if level + 1 < levels():
            first = jnp.where(after, received, total)
            second = jnp.where(after, total, received)
            total = matmul(first, passing[level]) + second
    return entering


def norm_body(middle, suffix, entering, scale, result, squares):
    rows, count, width = middle.shape
    state_high, state_low = split(entering[...])
    stacked = jnp.concatenate([state_high, state_low], axis=0)
    divide = 1.0 / scale[...]

    def step(i, total):
        high, low = split(suffix[i])
        both = jnp.dot(stacked, high, preferred_element_type=jnp.float32)
        moved = (both[:count] + both[count:]) + jnp.dot(
            state_high, low, preferred_element_type=jnp.float32
        )
        value = (middle[i] + moved) * divide
        result[i] = value
        return total + value * value

    total = lax.fori_loop(0, rows, step, jnp.zeros((count, width), jnp.float32), unroll=2)
    squares[...] = jnp.broadcast_to(jnp.sum(total, axis=1, keepdims=True), squares.shape)


def finish(middle, suffix, entering, scale):
    rows, count, width = middle.shape
    return call(
        norm_body,
        [shape(*middle.shape), shape(count, 128)],
        [],
        rows * 6 * count * width * width,
        middle,
        suffix,
        entering,
        scale,
    )


def scale_body(vectors, scale, result):
    result[...] = vectors[...] * (1.0 / scale[...])[None]


def rescale(vectors, scale):
    return call(scale_body, [shape(*vectors.shape)], [], vectors.size, vectors, scale)[0]


def chain_total(value, groups):
    size = lax.axis_size("chain")
    for members in groups:
        n = len(members[0])
        copies = jnp.broadcast_to(value[None], (n, *value.shape))
        got = lax.all_to_all(copies, "chain", 0, 0, axis_index_groups=members, tiled=True)
        value = jnp.sum(got, axis=0)
    return value


def chain_groups():
    size = lax.axis_size("chain")
    inner = 1 << (levels() // 2)
    outer = size // inner
    near = [[g * inner + j for j in range(inner)] for g in range(outer)]
    far = [[g * inner + j for g in range(outer)] for j in range(inner)]
    return near, far


def shards(start_vectors, factors):
    rows, count, width = start_vectors.shape
    cell_count = rows * lax.axis_size("chain") * width
    groups = chain_groups()
    whole = lax.all_gather(factors, "cols", axis=1, tiled=True)
    high, low, forward, prefix, suffix = prepare(whole, start_vectors)
    first_end, cross, turn = couple(high, low, forward, prefix, suffix)
    ahead = compose_levels(prefix[rows - 1], False)
    behind = compose_levels(suffix[0], True)
    zero = jnp.zeros((count, width), jnp.float32)

    entering = scan_blocks(forward[rows - 1], *ahead, False)
    end = first_end + matmul(entering, cross)
    forward = sweep(high, low, start_vectors, entering, False)
    middle = sweep(high, low, forward, zero, True)
    middle_end = sweep(high, low, middle, zero, False)[rows - 1]

    entering = scan_blocks(end, *behind, True)
    end = middle_end + matmul(entering, turn)
    first_solve = sweep(high, low, forward, entering, True)
    squares = jnp.sum(first_solve * first_solve, axis=(0, 2))
    forward = sweep(high, low, first_solve, zero, False)
    middle_end = sweep(high, low, forward, zero, True)[0]

    entering = scan_blocks(end, *ahead, False)
    end = middle_end + matmul(entering, cross)
    forward = sweep(high, low, first_solve, entering, False)
    middle = sweep(high, low, forward, zero, True)

    entering = scan_blocks(end, *behind, True)
    padded = jnp.broadcast_to(squares[:, None], (count, 128))
    scale_one = jnp.sqrt(chain_total(padded, groups) / cell_count + eps_value)
    second, squares = finish(middle, suffix, entering, scale_one[:, :1])
    scale_two = jnp.sqrt(chain_total(squares, groups) / cell_count + eps_value)
    return rescale(second, scale_two[:, :1]), jnp.log(scale_two[:, 0])


def solution(mesh):
    return jax.shard_map(
        shards,
        mesh=mesh,
        in_specs=(P("chain", "cols", None), P("chain", "cols", None)),
        out_specs=(P("chain", "cols", None), P("cols")),
        check_vma=False,
    )
```

time: 818 us -> 409 us (0.50); the launches traced: 803 us -> 407 us
  blocking collectives: 250 us -> 29.4 us
  matrix products: 221 us -> 26.5 us
  Pallas kernels: 0 us -> 81.5 us
  waiting for transfers between devices: 163 us -> 101 us
    psum x2 -> x0, blocking collectives: 250 us -> none  [the longest x1 126 us: shards(): lax.psum(jnp.sum(second_solve * second_solve, axis=(0, 2)), 'chain')]
    dot_general x194 -> x59, matrix products: 221 us -> 26.5 us  [matmul(): jnp.dot(left, right, precision=lax.Precision.HIGHEST, preferred_element_t...]
    pallas_call x0 -> x12, Pallas kernels: none -> 81.5 us  [call(): pl.pallas_call(body, out_shape=tuple(out_shapes), in_specs=[vmem] * len(o...]
    ppermute x38 -> x34, waiting for transfers between devices: 96.4 us -> 34.3 us  [exchange(): lax.ppermute(value, 'chain', [(i, i ^ 1 << level) for i in range(size)])]
    all_to_all x0 -> x2, blocking collectives: none -> 29.4 us  [chain_total(): lax.all_to_all(copies, 'chain', 0, 0, axis_index_groups=members, tiled=True)]
    ppermute x38 -> x34, starting transfers between devices: 145 us -> 135 us  [exchange(): lax.ppermute(value, 'chain', [(i, i ^ 1 << level) for i in range(size)])]
    all_to_all x0 -> x2, starting transfers between devices: none -> 10.2 us  [chain_total(): lax.all_to_all(copies, 'chain', 0, 0, axis_index_groups=members, tiled=True)]
  transfers between devices with their start and end apart: 39 -> 37, of which waited for: 25 -> 19; matrix products, arithmetic and copies ran while one was open for 6% -> 7% of each run, Pallas kernels for 0% -> 13%
where the time goes in v1:
time: 409 us; the launch traced here: 407 us
  starting transfers between devices  145 us (35%)
  waiting for transfers between devices  101 us (25%)
  Pallas kernels  81.5 us (20%)
  blocking collectives  29.4 us (7%)
  matrix products  26.5 us (6%)
  between operations  15.3 us (4%)
  local copies, waits for them, and re-layouts  5.58 us (1%)
    ppermute x34, starting transfers between devices, exchange(): lax.ppermute(value, 'chain', [(i, i ^ 1 << level) for i in range(size)])  135 us
    pallas_call x12, Pallas kernels, call(): pl.pallas_call(body, out_shape=tuple(out_shapes), in_specs=[vmem] * len(o...  81.5 us
    all_gather x1, waiting for transfers between devices, shards(): whole = lax.all_gather(factors, 'cols', axis=1, tiled=True)  65.9 us
    ppermute x34, waiting for transfers between devices, exchange(): lax.ppermute(value, 'chain', [(i, i ^ 1 << level) for i in range(size)])  34.3 us
    all_to_all x2, blocking collectives, chain_total(): lax.all_to_all(copies, 'chain', 0, 0, axis_index_groups=members, tiled=True)  29.4 us
    dot_general x59, matrix products, matmul(): jnp.dot(left, right, precision=lax.Precision.HIGHEST, preferred_element_t...  26.5 us
    all_to_all x2, starting transfers between devices, chain_total(): lax.all_to_all(copies, 'chain', 0, 0, axis_index_groups=members, tiled=True)  10.2 us
  transfers between devices with their start and end apart: 37, of which 19 were waited for; matrix products, arithmetic and copies ran while one was open for 7% of the time, Pallas kernels for 13%

profile of v1, /device:TPU:1, one launch (start us, length us, event | category | flops | bytes accessed | tf_op | source)
XLA Modules:
  0.0 407.3 jit_solution(5802809974489770374)
XLA Ops:
  7.9 65.9 %all-gather.2.cloned.1.call-done.factors = f32[16,256,256]{2,1,0:T(8,128)} async-done(((f32[16,32,256]{2,1,0:T(8,128)}), f32[16,256,256]{2,1,0:T(8,128)}) %all-gather.2.cloned.1.call-update) | async-done | bytes 4194320 | tf_op jit(solution)/shard_map/all_gather | solution.py:289
  73.9 15.3 %shard_map.41 = (bf16[16,256,256]{2,1,0:T(8,128)(2,1)}, bf16[16,256,256]{2,1,0:T(8,128)(2,1)}, f32[16,32,256]{2,1,0:T(8,128)}, f32[16,256,256]{2,1,0:T(8,128)}, f32[16,256,256]{2,1,0:T(8,128)}) custom-call(f32[16,256,256]{2,1,0:T(8,128)} %all-gather.2.cloned.1.call-done.factors, f32[16,32,256]{2,1,0:T(8,128)} %source.3), custom_call_target="tpu_custom_call" | custom-call | flops 3422552064 | bytes 17825792 | tf_op jit(solution)/shard_map/pallas_call | solution.py:42
  98.8 12.1 %shard_map.43 = (f32[32,256]{1,0:T(8,128)}, f32[256,256]{1,0:T(8,128)}, f32[256,256]{1,0:T(8,128)}) custom-call(bf16[16,256,256]{2,1,0:T(8,128)(2,1)} %get-tuple-element.12.high, bf16[16,256,256]{2,1,0:T(8,128)(2,1)} %get-tuple-element.13.low, f32[16,32,256]{2,1,0:T(8,128)} %get-tuple-element.14.forward, f32[16,256,256]{2,1,0:T(8,128)} %get-tuple-element.15.prefix, ...), custom_call_target="tpu_custom_call" | custom-call | flops 3422552064 | bytes 13664256 | tf_op jit(solution)/shard_map/pallas_call | solution.py:42
  124.1 4.3 %collective-permute-start.16 = (f32[256,256]{1,0:T(8,128)S(1)}, f32[256,256]{1,0:T(8,128)S(1)}, u32[]{:S(2)}, u32[]{:S(2)}) collective-permute-start(f32[256,256]{1,0:T(8,128)S(1)} %fusion.24), channel_id=1, source_target_pairs={{0,32},{8,40},{16,48},{24,56},{32,0},{40,8},{48,16},{56,24},{64,96... | collective-permute-start | bytes 786440 | tf_op jit(solution)/shard_map/ppermute | solution.py:176
  129.7 4.6 %collective-permute-start.4 = (f32[32,256]{1,0:T(8,128)S(1)}, f32[32,256]{1,0:T(8,128)S(1)}, u32[]{:S(2)}, u32[]{:S(2)}) collective-permute-start(f32[32,256]{1,0:T(8,128)S(1)} %convolution_add_fusion.40), channel_id=1, source_target_pairs={{0,32},{8,40},{16,48},{24,56},{32,0},{40,8},{48,16},{56,24},{64,96... | collective-permute-start | bytes 98312 | tf_op jit(solution)/shard_map/ppermute | solution.py:176
  150.8 4.0 collective-permute-start.20
  163.5 14.3 %collective-permute-done.9 = f32[256,256]{1,0:T(8,128)S(1)} collective-permute-done((f32[256,256]{1,0:T(8,128)S(1)}, f32[256,256]{1,0:T(8,128)S(1)}, u32[]{:S(2)}, u32[]{:S(2)}) %collective-permute-start.9) | collective-permute-done | bytes 262176 | tf_op jit(solution)/shard_map/ppermute | solution.py:176
  178.0 7.3 %collective-permute-start.10 = (f32[32,256]{1,0:T(8,128)S(1)}, f32[32,256]{1,0:T(8,128)S(1)}, u32[]{:S(2)}, u32[]{:S(2)}) collective-permute-start(f32[32,256]{1,0:T(8,128)S(1)} %convolution_add_fusion.34), channel_id=1, source_target_pairs={{0,256},{8,264},{16,272},{24,280},{32,288},{40,296},{48,304},{56,3... | collective-permute-start | bytes 98312 | tf_op jit(solution)/shard_map/ppermute | solution.py:176
  187.2 5.8 %collective-permute-start.11 = (f32[32,256]{1,0:T(8,128)S(1)}, f32[32,256]{1,0:T(8,128)S(1)}, u32[]{:S(2)}, u32[]{:S(2)}) collective-permute-start(f32[32,256]{1,0:T(8,128)S(1)} %convolution_add_fusion.32), channel_id=1, source_target_pairs={{0,8},{8,0},{16,24},{24,16},{32,40},{40,32},{48,56},{56,48},{64,72... | collective-permute-start | bytes 98312 | tf_op jit(solution)/shard_map/ppermute | solution.py:176
  193.4 6.0 %shard_map.42.source = f32[16,32,256]{2,1,0:T(8,128)} custom-call(bf16[16,256,256]{2,1,0:T(8,128)(2,1)} %get-tuple-element.12.high, bf16[16,256,256]{2,1,0:T(8,128)(2,1)} %get-tuple-element.13.low, f32[16,32,256]{2,1,0:T(8,128)} %source.3, f32[32,256]{1,0:T(8,128)} %copy-done.29), custom_call_target="tpu_custom_call" | custom-call | flops 201326592 | bytes 5275648 | tf_op jit(solution)/shard_map/pallas_call | solution.py:42
  203.4 5.9 %shard_map.45.source = f32[16,32,256]{2,1,0:T(8,128)} custom-call(bf16[16,256,256]{2,1,0:T(8,128)(2,1)} %get-tuple-element.12.high, bf16[16,256,256]{2,1,0:T(8,128)(2,1)} %get-tuple-element.13.low, f32[16,32,256]{2,1,0:T(8,128)} %shard_map.42.source, f32[32,256]{1,0:T(8,128)} %broadcast_5_entering.2.entering), custom_call_target="tpu_custom_call" | custom-call | flops 201326592 | bytes 5275648 | tf_op jit(solution)/shard_map/pallas_call | solution.py:42
  209.3 5.9 %shard_map.46 = f32[16,32,256]{2,1,0:T(8,128)} custom-call(bf16[16,256,256]{2,1,0:T(8,128)(2,1)} %get-tuple-element.12.high, bf16[16,256,256]{2,1,0:T(8,128)(2,1)} %get-tuple-element.13.low, f32[16,32,256]{2,1,0:T(8,128)} %shard_map.45.source, f32[32,256]{1,0:T(8,128)} %broadcast_5_entering.2.entering), custom_call_target="tpu_custom_call" | custom-call | flops 201326592 | bytes 5275648 | tf_op jit(solution)/shard_map/pallas_call | solution.py:42
  215.4 4.1 %collective-permute-start.15 = (f32[32,256]{1,0:T(8,128)S(1)}, f32[32,256]{1,0:T(8,128)S(1)}, u32[]{:S(2)}, u32[]{:S(2)}) collective-permute-start(f32[32,256]{1,0:T(8,128)S(1)} %convolution_add_fusion.29), channel_id=1, source_target_pairs={{0,32},{8,40},{16,48},{24,56},{32,0},{40,8},{48,16},{56,24},{64,96... | collective-permute-start | bytes 98312 | tf_op jit(solution)/shard_map/ppermute | solution.py:176
  226.7 3.9 collective-permute-start.19
  232.5 7.2 %collective-permute-start.21 = (f32[32,256]{1,0:T(8,128)S(1)}, f32[32,256]{1,0:T(8,128)S(1)}, u32[]{:S(2)}, u32[]{:S(2)}) collective-permute-start(f32[32,256]{1,0:T(8,128)S(1)} %convolution_add_fusion.23), channel_id=1, source_target_pairs={{0,256},{8,264},{16,272},{24,280},{32,288},{40,296},{48,304},{56,3... | collective-permute-start | bytes 98312 | tf_op jit(solution)/shard_map/ppermute | solution.py:176
  242.1 5.9 %shard_map.44.source = f32[16,32,256]{2,1,0:T(8,128)} custom-call(bf16[16,256,256]{2,1,0:T(8,128)(2,1)} %get-tuple-element.12.high, bf16[16,256,256]{2,1,0:T(8,128)(2,1)} %get-tuple-element.13.low, f32[16,32,256]{2,1,0:T(8,128)} %shard_map.42.source, f32[32,256]{1,0:T(8,128)} %fusion.10.entering), custom_call_target="tpu_custom_call" | custom-call | flops 201326592 | bytes 5275648 | tf_op jit(solution)/shard_map/pallas_call | solution.py:42
  249.5 6.7 %collective-permute-start.22 = (f32[32,256]{1,0:T(8,128)}, f32[32,256]{1,0:T(8,128)}, u32[]{:S(2)}, u32[]{:S(2)}) collective-permute-start(f32[32,256]{1,0:T(8,128)} %convolution_add_fusion.21), channel_id=1, source_target_pairs={{0,8},{8,0},{16,24},{24,16},{32,40},{40,32},{48,56},{56,48},{64,72... | collective-permute-start | bytes 98312 | tf_op jit(solution)/shard_map/ppermute | solution.py:176
  258.2 3.9 all-to-all-start
  266.6 5.9 %shard_map.49.source = f32[16,32,256]{2,1,0:T(8,128)} custom-call(bf16[16,256,256]{2,1,0:T(8,128)(2,1)} %get-tuple-element.12.high, bf16[16,256,256]{2,1,0:T(8,128)(2,1)} %get-tuple-element.13.low, f32[16,32,256]{2,1,0:T(8,128)} %shard_map.44.source, f32[32,256]{1,0:T(8,128)} %broadcast_5_entering.2.entering), custom_call_target="tpu_custom_call" | custom-call | flops 201326592 | bytes 5275648 | tf_op jit(solution)/shard_map/pallas_call | solution.py:42
  272.5 6.0 %shard_map.50 = f32[16,32,256]{2,1,0:T(8,128)} custom-call(bf16[16,256,256]{2,1,0:T(8,128)(2,1)} %get-tuple-element.12.high, bf16[16,256,256]{2,1,0:T(8,128)(2,1)} %get-tuple-element.13.low, f32[16,32,256]{2,1,0:T(8,128)} %shard_map.49.source, f32[32,256]{1,0:T(8,128)} %broadcast_5_entering.2.entering), custom_call_target="tpu_custom_call" | custom-call | flops 201326592 | bytes 5275648 | tf_op jit(solution)/shard_map/pallas_call | solution.py:42
  278.8 4.3 %collective-permute-start.24 = (f32[32,256]{1,0:T(8,128)S(1)}, f32[32,256]{1,0:T(8,128)S(1)}, u32[]{:S(2)}, u32[]{:S(2)}) collective-permute-start(f32[32,256]{1,0:T(8,128)S(1)} %convolution_add_fusion.18), channel_id=1, source_target_pairs={{0,32},{8,40},{16,48},{24,56},{32,0},{40,8},{48,16},{56,24},{64,96... | collective-permute-start | bytes 98312 | tf_op jit(solution)/shard_map/ppermute | solution.py:176
  295.9 7.0 %collective-permute-start.27 = (f32[32,256]{1,0:T(8,128)S(1)}, f32[32,256]{1,0:T(8,128)S(1)}, u32[]{:S(2)}, u32[]{:S(2)}) collective-permute-start(f32[32,256]{1,0:T(8,128)S(1)} %convolution_add_fusion.12), channel_id=1, source_target_pairs={{0,256},{8,264},{16,272},{24,280},{32,288},{40,296},{48,304},{56,3... | collective-permute-start | bytes 98312 | tf_op jit(solution)/shard_map/ppermute | solution.py:176
  305.8 7.1 %collective-permute-start.28 = (f32[32,256]{1,0:T(8,128)S(1)}, f32[32,256]{1,0:T(8,128)S(1)}, u32[]{:S(2)}, u32[]{:S(2)}) collective-permute-start(f32[32,256]{1,0:T(8,128)S(1)} %convolution_add_fusion.10), channel_id=1, source_target_pairs={{0,8},{8,0},{16,24},{24,16},{32,40},{40,32},{48,56},{56,48},{64,72... | collective-permute-start | bytes 98312 | tf_op jit(solution)/shard_map/ppermute | solution.py:176
  313.6 6.3 %all-to-all-start.1 = ((f32[8,32,128]{2,1,0:T(8,128)}), f32[8,32,128]{2,1,0:T(8,128)S(1)}, u32[]{:S(2)}, u32[]{:S(2)}) async-start(f32[8,32,128]{2,1,0:T(8,128)} %broadcast_in_dim.6), calls=%async_computation.1 | async-start | bytes 262144 | tf_op jit(solution)/shard_map/all_to_all | solution.py:271
  323.1 5.9 %shard_map.47.source = f32[16,32,256]{2,1,0:T(8,128)} custom-call(bf16[16,256,256]{2,1,0:T(8,128)(2,1)} %get-tuple-element.12.high, bf16[16,256,256]{2,1,0:T(8,128)(2,1)} %get-tuple-element.13.low, f32[16,32,256]{2,1,0:T(8,128)} %shard_map.44.source, f32[32,256]{1,0:T(8,128)} %copy-done.28), custom_call_target="tpu_custom_call" | custom-call | flops 201326592 | bytes 5275648 | tf_op jit(solution)/shard_map/pallas_call | solution.py:42
  329.0 6.0 %shard_map.48.middle = f32[16,32,256]{2,1,0:T(8,128)} custom-call(bf16[16,256,256]{2,1,0:T(8,128)(2,1)} %get-tuple-element.12.high, bf16[16,256,256]{2,1,0:T(8,128)(2,1)} %get-tuple-element.13.low, f32[16,32,256]{2,1,0:T(8,128)} %shard_map.47.source, f32[32,256]{1,0:T(8,128)} %broadcast_5_entering.2.entering), custom_call_target="tpu_custom_call" | custom-call | flops 201326592 | bytes 5275648 | tf_op jit(solution)/shard_map/pallas_call | solution.py:42
  335.2 4.9 %collective-permute-start.30 = (f32[32,256]{1,0:T(8,128)S(1)}, f32[32,256]{1,0:T(8,128)S(1)}, u32[]{:S(2)}, u32[]{:S(2)}) collective-permute-start(f32[32,256]{1,0:T(8,128)S(1)} %convolution_add_fusion.7), channel_id=1, source_target_pairs={{0,32},{8,40},{16,48},{24,56},{32,0},{40,8},{48,16},{56,24},{64,96... | collective-permute-start | bytes 98312 | tf_op jit(solution)/shard_map/ppermute | solution.py:176
  346.6 4.3 %collective-permute-start.32 = (f32[32,256]{1,0:T(8,128)S(1)}, f32[32,256]{1,0:T(8,128)S(1)}, u32[]{:S(2)}, u32[]{:S(2)}) collective-permute-start(f32[32,256]{1,0:T(8,128)S(1)} %convolution_add_fusion.3), channel_id=1, source_target_pairs={{0,128},{8,136},{16,144},{24,152},{32,160},{40,168},{48,176},{56,1... | collective-permute-start | bytes 98312 | tf_op jit(solution)/shard_map/ppermute | solution.py:176
  352.4 7.6 %collective-permute-start.33 = (f32[32,256]{1,0:T(8,128)S(1)}, f32[32,256]{1,0:T(8,128)S(1)}, u32[]{:S(2)}, u32[]{:S(2)}) collective-permute-start(f32[32,256]{1,0:T(8,128)S(1)} %convolution_add_fusion.1), channel_id=1, source_target_pairs={{0,256},{8,264},{16,272},{24,280},{32,288},{40,296},{48,304},{56,3... | collective-permute-start | bytes 98312 | tf_op jit(solution)/shard_map/ppermute | solution.py:176
  362.2 4.8 %shard_map.51 = (f32[16,32,256]{2,1,0:T(8,128)}, f32[32,128]{1,0:T(8,128)}) custom-call(f32[16,32,256]{2,1,0:T(8,128)} %shard_map.48.middle, f32[16,256,256]{2,1,0:T(8,128)} %get-tuple-element.16.suffix, f32[32,256]{1,0:T(8,128)} %fusion.entering, f32[32,1]{1,0:T(8,128)} %fusion.73.scale), custom_call_target="tpu_custom_call" | custom-call | flops 201326592 | bytes 5292160 | tf_op jit(solution)/shard_map/pallas_call | solution.py:42
  367.8 14.7 %all_to_all.20 = f32[8,32,128]{2,1,0:T(8,128)S(1)} all-to-all(f32[8,32,128]{2,1,0:T(8,128)S(1)} %broadcast_in_dim.7), channel_id=1, replica_groups={{0,8,16,24,32,40,48,56},{64,72,80,88,96,104,112,120},{128,136,144,152,1..., dimensions={0} | all-to-all | bytes 262144 | tf_op jit(solution)/shard_map/all_to_all | solution.py:271
  382.5 14.7 %all_to_all.21 = f32[8,32,128]{2,1,0:T(8,128)S(1)} all-to-all(f32[8,32,128]{2,1,0:T(8,128)S(1)} %broadcast_in_dim.8), channel_id=1, replica_groups={{0,64,128,192,256,320,384,448},{8,72,136,200,264,328,392,456},{16,80,14..., dimensions={0} | all-to-all | bytes 262144 | tf_op jit(solution)/shard_map/all_to_all | solution.py:271
  (197 shorter events, 109.4 us)
Async XLA Ops:
  7.2 66.7 %all-gather.2.cloned.1.call-start = ((), (), s32[]{:S(2)}) async-start(), calls=%async_computation.4 | async-start | bytes 4718592 | tf_op jit(solution)/shard_map/all_gather | solution.py:289
  89.9 25.5 %collective-permute-start = (f32[32,256]{1,0:T(8,128)S(1)}, f32[32,256]{1,0:T(8,128)S(1)}, u32[]{:S(2)}, u32[]{:S(2)}) collective-permute-start(f32[32,256]{1,0:T(8,128)S(1)} %slice_bitcast_fusion.4), channel_id=1, source_target_pairs={{0,8},{8,0},{16,24},{24,16},{32,40},{40,32},{48,56},{56,48},{64,72... | collective-permute-start | bytes 98312 | tf_op jit(solution)/shard_map/ppermute | solution.py:176
  94.4 16.5 %collective-permute-start.12 = (f32[256,256]{1,0:T(8,128)S(1)}, f32[256,256]{1,0:T(8,128)S(1)}, u32[]{:S(2)}, u32[]{:S(2)}) collective-permute-start(f32[256,256]{1,0:T(8,128)S(1)} %slice_bitcast_fusion), channel_id=1, source_target_pairs={{0,8},{8,0},{16,24},{24,16},{32,40},{40,32},{48,56},{56,48},{64,72... | collective-permute-start | bytes 786440 | tf_op jit(solution)/shard_map/ppermute | solution.py:176
  96.4 19.1 %collective-permute-start.1 = (f32[256,256]{1,0:T(8,128)S(1)}, f32[256,256]{1,0:T(8,128)S(1)}, u32[]{:S(2)}, u32[]{:S(2)}) collective-permute-start(f32[256,256]{1,0:T(8,128)S(1)} %slice_bitcast_fusion.1), channel_id=1, source_target_pairs={{0,8},{8,0},{16,24},{24,16},{32,40},{40,32},{48,56},{56,48},{64,72... | collective-permute-start | bytes 786440 | tf_op jit(solution)/shard_map/ppermute | solution.py:176
  112.3 11.3 %collective-permute-start.14 = (f32[256,256]{1,0:T(8,128)S(1)}, f32[256,256]{1,0:T(8,128)S(1)}, u32[]{:S(2)}, u32[]{:S(2)}) collective-permute-start(f32[256,256]{1,0:T(8,128)S(1)} %fusion.26), channel_id=1, source_target_pairs={{0,16},{8,24},{16,0},{24,8},{32,48},{40,56},{48,32},{56,40},{64,80... | collective-permute-start | bytes 786440 | tf_op jit(solution)/shard_map/ppermute | solution.py:176
  116.6 6.7 %collective-permute-start.2 = (f32[32,256]{1,0:T(8,128)S(1)}, f32[32,256]{1,0:T(8,128)S(1)}, u32[]{:S(2)}, u32[]{:S(2)}) collective-permute-start(f32[32,256]{1,0:T(8,128)S(1)} %convolution_add_fusion.42), channel_id=1, source_target_pairs={{0,16},{8,24},{16,0},{24,8},{32,48},{40,56},{48,32},{56,40},{64,80... | collective-permute-start | bytes 98312 | tf_op jit(solution)/shard_map/ppermute | solution.py:176
  120.3 9.2 %collective-permute-start.3 = (f32[256,256]{1,0:T(8,128)S(1)}, f32[256,256]{1,0:T(8,128)S(1)}, u32[]{:S(2)}, u32[]{:S(2)}) collective-permute-start(f32[256,256]{1,0:T(8,128)S(1)} %fusion.34), channel_id=1, source_target_pairs={{0,16},{8,24},{16,0},{24,8},{32,48},{40,56},{48,32},{56,40},{64,80... | collective-permute-start | bytes 786440 | tf_op jit(solution)/shard_map/ppermute | solution.py:176
  124.1 14.1 %collective-permute-start.16 = (f32[256,256]{1,0:T(8,128)S(1)}, f32[256,256]{1,0:T(8,128)S(1)}, u32[]{:S(2)}, u32[]{:S(2)}) collective-permute-start(f32[256,256]{1,0:T(8,128)S(1)} %fusion.24), channel_id=1, source_target_pairs={{0,32},{8,40},{16,48},{24,56},{32,0},{40,8},{48,16},{56,24},{64,96... | collective-permute-start | bytes 786440 | tf_op jit(solution)/shard_map/ppermute | solution.py:176
  129.7 8.2 %collective-permute-start.4 = (f32[32,256]{1,0:T(8,128)S(1)}, f32[32,256]{1,0:T(8,128)S(1)}, u32[]{:S(2)}, u32[]{:S(2)}) collective-permute-start(f32[32,256]{1,0:T(8,128)S(1)} %convolution_add_fusion.40), channel_id=1, source_target_pairs={{0,32},{8,40},{16,48},{24,56},{32,0},{40,8},{48,16},{56,24},{64,96... | collective-permute-start | bytes 98312 | tf_op jit(solution)/shard_map/ppermute | solution.py:176
  134.7 8.6 %collective-permute-start.5 = (f32[256,256]{1,0:T(8,128)S(1)}, f32[256,256]{1,0:T(8,128)S(1)}, u32[]{:S(2)}, u32[]{:S(2)}) collective-permute-start(f32[256,256]{1,0:T(8,128)S(1)} %fusion.32), channel_id=1, source_target_pairs={{0,32},{8,40},{16,48},{24,56},{32,0},{40,8},{48,16},{56,24},{64,96... | collective-permute-start | bytes 786440 | tf_op jit(solution)/shard_map/ppermute | solution.py:176
  138.6 11.8 %collective-permute-start.18 = (f32[256,256]{1,0:T(8,128)S(1)}, f32[256,256]{1,0:T(8,128)S(1)}, u32[]{:S(2)}, u32[]{:S(2)}) collective-permute-start(f32[256,256]{1,0:T(8,128)S(1)} %fusion.22), channel_id=1, source_target_pairs={{0,64},{8,72},{16,80},{24,88},{32,96},{40,104},{48,112},{56,120},{... | collective-permute-start | bytes 786440 | tf_op jit(solution)/shard_map/ppermute | solution.py:176
  143.6 6.5 %collective-permute-start.6 = (f32[32,256]{1,0:T(8,128)S(1)}, f32[32,256]{1,0:T(8,128)S(1)}, u32[]{:S(2)}, u32[]{:S(2)}) collective-permute-start(f32[32,256]{1,0:T(8,128)S(1)} %convolution_add_fusion.38), channel_id=1, source_target_pairs={{0,64},{8,72},{16,80},{24,88},{32,96},{40,104},{48,112},{56,120},{... | collective-permute-start | bytes 98312 | tf_op jit(solution)/shard_map/ppermute | solution.py:176
  147.1 7.7 %collective-permute-start.7 = (f32[256,256]{1,0:T(8,128)S(1)}, f32[256,256]{1,0:T(8,128)S(1)}, u32[]{:S(2)}, u32[]{:S(2)}) collective-permute-start(f32[256,256]{1,0:T(8,128)S(1)} %fusion.30), channel_id=1, source_target_pairs={{0,64},{8,72},{16,80},{24,88},{32,96},{40,104},{48,112},{56,120},{... | collective-permute-start | bytes 786440 | tf_op jit(solution)/shard_map/ppermute | solution.py:176
  150.8 42.2 %collective-permute-start.20 = (f32[256,256]{1,0:T(8,128)S(1)}, f32[256,256]{1,0:T(8,128)S(1)}, u32[]{:S(2)}, u32[]{:S(2)}) collective-permute-start(f32[256,256]{1,0:T(8,128)S(1)} %fusion.20), channel_id=1, source_target_pairs={{0,128},{8,136},{16,144},{24,152},{32,160},{40,168},{48,176},{56,1... | collective-permute-start | bytes 786440 | tf_op jit(solution)/shard_map/ppermute | solution.py:176
  155.1 8.2 %collective-permute-start.8 = (f32[32,256]{1,0:T(8,128)S(1)}, f32[32,256]{1,0:T(8,128)S(1)}, u32[]{:S(2)}, u32[]{:S(2)}) collective-permute-start(f32[32,256]{1,0:T(8,128)S(1)} %convolution_add_fusion.36), channel_id=1, source_target_pairs={{0,128},{8,136},{16,144},{24,152},{32,160},{40,168},{48,176},{56,1... | collective-permute-start | bytes 98312 | tf_op jit(solution)/shard_map/ppermute | solution.py:176
  159.3 18.5 %collective-permute-start.9 = (f32[256,256]{1,0:T(8,128)S(1)}, f32[256,256]{1,0:T(8,128)S(1)}, u32[]{:S(2)}, u32[]{:S(2)}) collective-permute-start(f32[256,256]{1,0:T(8,128)S(1)} %fusion.28), channel_id=1, source_target_pairs={{0,128},{8,136},{16,144},{24,152},{32,160},{40,168},{48,176},{56,1... | collective-permute-start | bytes 786440 | tf_op jit(solution)/shard_map/ppermute | solution.py:176
  178.0 8.6 %collective-permute-start.10 = (f32[32,256]{1,0:T(8,128)S(1)}, f32[32,256]{1,0:T(8,128)S(1)}, u32[]{:S(2)}, u32[]{:S(2)}) collective-permute-start(f32[32,256]{1,0:T(8,128)S(1)} %convolution_add_fusion.34), channel_id=1, source_target_pairs={{0,256},{8,264},{16,272},{24,280},{32,288},{40,296},{48,304},{56,3... | collective-permute-start | bytes 98312 | tf_op jit(solution)/shard_map/ppermute | solution.py:176
  187.2 12.2 %collective-permute-start.11 = (f32[32,256]{1,0:T(8,128)S(1)}, f32[32,256]{1,0:T(8,128)S(1)}, u32[]{:S(2)}, u32[]{:S(2)}) collective-permute-start(f32[32,256]{1,0:T(8,128)S(1)} %convolution_add_fusion.32), channel_id=1, source_target_pairs={{0,8},{8,0},{16,24},{24,16},{32,40},{40,32},{48,56},{56,48},{64,72... | collective-permute-start | bytes 98312 | tf_op jit(solution)/shard_map/ppermute | solution.py:176
  200.6 14.6 %collective-permute-start.13 = (f32[32,256]{1,0:T(8,128)S(1)}, f32[32,256]{1,0:T(8,128)S(1)}, u32[]{:S(2)}, u32[]{:S(2)}) collective-permute-start(f32[32,256]{1,0:T(8,128)S(1)} %convolution_add_fusion.31), channel_id=1, source_target_pairs={{0,16},{8,24},{16,0},{24,8},{32,48},{40,56},{48,32},{56,40},{64,80... | collective-permute-start | bytes 98312 | tf_op jit(solution)/shard_map/ppermute | solution.py:176
  215.4 6.2 %collective-permute-start.15 = (f32[32,256]{1,0:T(8,128)S(1)}, f32[32,256]{1,0:T(8,128)S(1)}, u32[]{:S(2)}, u32[]{:S(2)}) collective-permute-start(f32[32,256]{1,0:T(8,128)S(1)} %convolution_add_fusion.29), channel_id=1, source_target_pairs={{0,32},{8,40},{16,48},{24,56},{32,0},{40,8},{48,16},{56,24},{64,96... | collective-permute-start | bytes 98312 | tf_op jit(solution)/shard_map/ppermute | solution.py:176
  232.5 8.7 %collective-permute-start.21 = (f32[32,256]{1,0:T(8,128)S(1)}, f32[32,256]{1,0:T(8,128)S(1)}, u32[]{:S(2)}, u32[]{:S(2)}) collective-permute-start(f32[32,256]{1,0:T(8,128)S(1)} %convolution_add_fusion.23), channel_id=1, source_target_pairs={{0,256},{8,264},{16,272},{24,280},{32,288},{40,296},{48,304},{56,3... | collective-permute-start | bytes 98312 | tf_op jit(solution)/shard_map/ppermute | solution.py:176
  249.5 12.5 %collective-permute-start.22 = (f32[32,256]{1,0:T(8,128)}, f32[32,256]{1,0:T(8,128)}, u32[]{:S(2)}, u32[]{:S(2)}) collective-permute-start(f32[32,256]{1,0:T(8,128)} %convolution_add_fusion.21), channel_id=1, source_target_pairs={{0,8},{8,0},{16,24},{24,16},{32,40},{40,32},{48,56},{56,48},{64,72... | collective-permute-start | bytes 98312 | tf_op jit(solution)/shard_map/ppermute | solution.py:176
  258.2 54.8 %all-to-all-start = ((f32[8,32,128]{2,1,0:T(8,128)}), f32[8,32,128]{2,1,0:T(8,128)S(1)}, u32[]{:S(2)}, u32[]{:S(2)}) async-start(f32[8,32,128]{2,1,0:T(8,128)} %broadcast_in_dim_broadcast_in_dim_broadcast_in_dim.2), calls=%async_computation | async-start | bytes 262144 | tf_op jit(solution)/shard_map/all_to_all | solution.py:271
  263.3 15.2 %collective-permute-start.23 = (f32[32,256]{1,0:T(8,128)S(1)}, f32[32,256]{1,0:T(8,128)S(1)}, u32[]{:S(2)}, u32[]{:S(2)}) collective-permute-start(f32[32,256]{1,0:T(8,128)S(1)} %convolution_add_fusion.20), channel_id=1, source_target_pairs={{0,16},{8,24},{16,0},{24,8},{32,48},{40,56},{48,32},{56,40},{64,80... | collective-permute-start | bytes 98312 | tf_op jit(solution)/shard_map/ppermute | solution.py:176
  278.8 6.2 %collective-permute-start.24 = (f32[32,256]{1,0:T(8,128)S(1)}, f32[32,256]{1,0:T(8,128)S(1)}, u32[]{:S(2)}, u32[]{:S(2)}) collective-permute-start(f32[32,256]{1,0:T(8,128)S(1)} %convolution_add_fusion.18), channel_id=1, source_target_pairs={{0,32},{8,40},{16,48},{24,56},{32,0},{40,8},{48,16},{56,24},{64,96... | collective-permute-start | bytes 98312 | tf_op jit(solution)/shard_map/ppermute | solution.py:176
  295.9 8.6 %collective-permute-start.27 = (f32[32,256]{1,0:T(8,128)S(1)}, f32[32,256]{1,0:T(8,128)S(1)}, u32[]{:S(2)}, u32[]{:S(2)}) collective-permute-start(f32[32,256]{1,0:T(8,128)S(1)} %convolution_add_fusion.12), channel_id=1, source_target_pairs={{0,256},{8,264},{16,272},{24,280},{32,288},{40,296},{48,304},{56,3... | collective-permute-start | bytes 98312 | tf_op jit(solution)/shard_map/ppermute | solution.py:176
  305.8 14.2 %collective-permute-start.28 = (f32[32,256]{1,0:T(8,128)S(1)}, f32[32,256]{1,0:T(8,128)S(1)}, u32[]{:S(2)}, u32[]{:S(2)}) collective-permute-start(f32[32,256]{1,0:T(8,128)S(1)} %convolution_add_fusion.10), channel_id=1, source_target_pairs={{0,8},{8,0},{16,24},{24,16},{32,40},{40,32},{48,56},{56,48},{64,72... | collective-permute-start | bytes 98312 | tf_op jit(solution)/shard_map/ppermute | solution.py:176
  313.6 37.5 %all-to-all-start.1 = ((f32[8,32,128]{2,1,0:T(8,128)}), f32[8,32,128]{2,1,0:T(8,128)S(1)}, u32[]{:S(2)}, u32[]{:S(2)}) async-start(f32[8,32,128]{2,1,0:T(8,128)} %broadcast_in_dim.6), calls=%async_computation.1 | async-start | bytes 262144 | tf_op jit(solution)/shard_map/all_to_all | solution.py:271
  321.2 13.8 %collective-permute-start.29 = (f32[32,256]{1,0:T(8,128)S(1)}, f32[32,256]{1,0:T(8,128)S(1)}, u32[]{:S(2)}, u32[]{:S(2)}) collective-permute-start(f32[32,256]{1,0:T(8,128)S(1)} %convolution_add_fusion.9), channel_id=1, source_target_pairs={{0,16},{8,24},{16,0},{24,8},{32,48},{40,56},{48,32},{56,40},{64,80... | collective-permute-start | bytes 98312 | tf_op jit(solution)/shard_map/ppermute | solution.py:176
  335.2 6.2 %collective-permute-start.30 = (f32[32,256]{1,0:T(8,128)S(1)}, f32[32,256]{1,0:T(8,128)S(1)}, u32[]{:S(2)}, u32[]{:S(2)}) collective-permute-start(f32[32,256]{1,0:T(8,128)S(1)} %convolution_add_fusion.7), channel_id=1, source_target_pairs={{0,32},{8,40},{16,48},{24,56},{32,0},{40,8},{48,16},{56,24},{64,96... | collective-permute-start | bytes 98312 | tf_op jit(solution)/shard_map/ppermute | solution.py:176
  346.6 5.6 %collective-permute-start.32 = (f32[32,256]{1,0:T(8,128)S(1)}, f32[32,256]{1,0:T(8,128)S(1)}, u32[]{:S(2)}, u32[]{:S(2)}) collective-permute-start(f32[32,256]{1,0:T(8,128)S(1)} %convolution_add_fusion.3), channel_id=1, source_target_pairs={{0,128},{8,136},{16,144},{24,152},{32,160},{40,168},{48,176},{56,1... | collective-permute-start | bytes 98312 | tf_op jit(solution)/shard_map/ppermute | solution.py:176
  352.4 8.9 %collective-permute-start.33 = (f32[32,256]{1,0:T(8,128)S(1)}, f32[32,256]{1,0:T(8,128)S(1)}, u32[]{:S(2)}, u32[]{:S(2)}) collective-permute-start(f32[32,256]{1,0:T(8,128)S(1)} %convolution_add_fusion.1), channel_id=1, source_target_pairs={{0,256},{8,264},{16,272},{24,280},{32,288},{40,296},{48,304},{56,3... | collective-permute-start | bytes 98312 | tf_op jit(solution)/shard_map/ppermute | solution.py:176
  (38 other events, 1089.9 us)
Sparse Core Ops, SparseCore 0:
  10.1 63.7 all-gather.1

commit v2 on v1

v2 whole, which is shorter than its diff:
```python
import functools

import jax
import jax.numpy as jnp
from jax import lax
from jax.experimental import pallas as pl
from jax.experimental.pallas import tpu as pltpu
from jax.sharding import Mesh, PartitionSpec as P

eps_value = 1e-06
VMEM_BYTES = 56 * 1024 * 1024
CHAIN = ("outer", "inner")


def split(value):
    high = value.astype(jnp.bfloat16)
    low = (value - high.astype(jnp.float32)).astype(jnp.bfloat16)
    return high, low


def apply_split(state, high, low):
    rows = state.shape[0]
    state_high, state_low = split(state)
    both = jnp.dot(
        jnp.concatenate([state_high, state_low], axis=0),
        high,
        preferred_element_type=jnp.float32,
    )
    return (both[:rows] + both[rows:]) + jnp.dot(
        state_high, low, preferred_element_type=jnp.float32
    )


def matmul(left, right):
    return jnp.dot(
        left, right, precision=lax.Precision.HIGHEST, preferred_element_type=jnp.float32
    )


def call(body, out_shapes, scratch, flops, *operands, after=None, position=None):
    vmem = pl.BlockSpec(memory_space=pltpu.VMEM)
    touched = sum(x.size * x.dtype.itemsize for x in (*operands, *out_shapes))
    specs = [vmem] * len(operands)
    if position is not None:
        specs = [pl.BlockSpec(memory_space=pltpu.SMEM), *specs]
        operands = (position, *operands)
    kernel = body
    if after is not None:
        specs = [pl.BlockSpec(memory_space=pl.ANY), *specs]
        operands = (after, *operands)

        def kernel(_, *refs):
            body(*refs)

    return pl.pallas_call(
        kernel,
        out_shape=tuple(out_shapes),
        in_specs=specs,
        out_specs=tuple([vmem] * len(out_shapes)),
        scratch_shapes=scratch,
        compiler_params=pltpu.CompilerParams(vmem_limit_bytes=VMEM_BYTES),
        cost_estimate=pl.CostEstimate(flops=flops, bytes_accessed=touched, transcendentals=0),
    )(*operands)


def shape(*dims, dtype=jnp.float32):
    return jax.ShapeDtypeStruct(dims, dtype)


def prepare_body(factors, source, high, low, forward, prefix, suffix, ahead, behind):
    rows, width, _ = factors.shape
    count = source.shape[1]

    def turn(i, _):
        turned = factors[i].T
        high[i], low[i] = split(turned)
        return 0

    lax.fori_loop(0, rows, turn, 0)
    eye = (
        lax.broadcasted_iota(jnp.int32, (width, width), 0)
        == lax.broadcasted_iota(jnp.int32, (width, width), 1)
    ).astype(jnp.float32)
    ahead[:count] = jnp.zeros((count, width), jnp.float32)
    ahead[count:] = eye
    behind[...] = eye

    def step(i, _):
        j = rows - 1 - i
        moved = apply_split(ahead[...], high[i], low[i])
        back = apply_split(behind[...], high[j], low[j])
        state = moved[:count] + source[i]
        forward[i] = state
        prefix[i] = moved[count:]
        ahead[:count] = state
        ahead[count:] = moved[count:]
        suffix[j] = back
        behind[...] = back
        return 0

    lax.fori_loop(0, rows, step, 0)


def prepare(factors, source):
    rows, width, _ = factors.shape
    count = source.shape[1]
    square = (rows, width, width)
    return call(
        prepare_body,
        [
            shape(*square, dtype=jnp.bfloat16),
            shape(*square, dtype=jnp.bfloat16),
            shape(*source.shape),
            shape(*square),
            shape(*square),
        ],
        [pltpu.VMEM((count + width, width), jnp.float32), pltpu.VMEM((width, width), jnp.float32)],
        rows * 6 * (count + 2 * width) * width * width,
        factors,
        source,
    )


def couple_body(high, low, forward, prefix, suffix, first_end, cross, turn, twist, behind, ahead, kept):
    rows, count, width = forward.shape
    ahead[...] = jnp.zeros_like(ahead)
    behind[...] = jnp.zeros_like(behind)

    def step(i, _):
        j = rows - 1 - i
        entering = jnp.concatenate([forward[j], prefix[j]], axis=0) + behind[...]
        behind[...] = apply_split(entering, high[j], low[j])
        state = apply_split(ahead[...], high[i], low[i]) + suffix[i]
        ahead[...] = state
        kept[i] = state
        return 0

    lax.fori_loop(0, rows, step, 0)
    first_end[...] = behind[:count]
    cross[...] = behind[count:]
    turn[...] = ahead[...]
    ahead[...] = jnp.zeros_like(ahead)

    def back(i, _):
        j = rows - 1 - i
        ahead[...] = apply_split(kept[j] + ahead[...], high[j], low[j])
        return 0

    lax.fori_loop(0, rows, back, 0)
    twist[...] = ahead[...]


def couple(high, low, forward, prefix, suffix):
    rows, count, width = forward.shape
    square = (width, width)
    return call(
        couple_body,
        [shape(count, width), shape(*square), shape(*square), shape(*square)],
        [
            pltpu.VMEM((count + width, width), jnp.float32),
            pltpu.VMEM(square, jnp.float32),
            pltpu.VMEM((rows, *square), jnp.float32),
        ],
        rows * 6 * (count + 3 * width) * width * width,
        high,
        low,
        forward,
        prefix,
        suffix,
    )


def sweep_body(reverse, high, low, source, entering, result):
    rows = source.shape[0]

    def step(i, state):
        if reverse:
            j = rows - 1 - i
            state = apply_split(source[j] + state, high[j], low[j])
        else:
            j = i
            state = apply_split(state, high[j], low[j]) + source[j]
        result[j] = state
        return state

    lax.fori_loop(0, rows, step, entering[...], unroll=2)


def sweep(high, low, source, entering, reverse, after=None):
    rows, count, width = source.shape
    return call(
        functools.partial(sweep_body, reverse),
        [shape(*source.shape)],
        [],
        rows * 6 * count * width * width,
        high,
        low,
        source,
        entering,
        after=after,
    )[0]


def exchange(value, level):
    size = lax.axis_size(CHAIN)
    return lax.ppermute(value, CHAIN, [(i, i ^ (1 << level)) for i in range(size)])


def scan_spans(operator, total, reverse):
    width = operator.shape[0]
    count = total.shape[0]
    levels = (lax.axis_size(CHAIN) - 1).bit_length()
    span = jnp.concatenate([operator, total], axis=0)
    lead = None
    entering = jnp.zeros_like(total)
    arrivals = []
    for level in range(levels):
        after = (lax.axis_index(CHAIN) >> level) & 1 == (0 if reverse else 1)
        if level + 1 == levels:
            received = exchange(span[width:], level)
            return jnp.where(after, entering + matmul(received, lead), entering), arrivals
        received = exchange(span, level)
        first = jnp.where(after, received, span)
        second = jnp.where(after, span, received)
        source = jnp.concatenate([jnp.zeros_like(operator), second[width:]], axis=0)
        span = matmul(first, second[:width]) + source
        carried = received if lead is None else matmul(received, lead)
        base = jnp.eye(width, dtype=jnp.float32) if lead is None else lead
        lead = jnp.where(after, carried[:width], base)
        entering = jnp.where(after, entering + carried[width:], entering)
        arrivals.append(entering)


def join_body(position, spans, own, whole, reach, crossing):
    members, _, width, _ = spans.shape
    eye = (
        lax.broadcasted_iota(jnp.int32, (width, width), 0)
        == lax.broadcasted_iota(jnp.int32, (width, width), 1)
    ).astype(jnp.float32)
    reach[0] = eye
    reach[1] = eye
    mine = position[0]

    def outward(e, _):
        @pl.when(e == mine)
        def _():
            own[0] = reach[0]

        back = members - 1 - e

        @pl.when(back == mine)
        def _():
            own[1] = reach[1]

        ahead = reach[0]
        crossing[e] = apply_split(ahead, *split(spans[e, 2]))
        reach[1] = apply_split(reach[1], *split(spans[back, 1]))
        reach[0] = apply_split(ahead, *split(spans[e, 0]))
        return 0

    lax.fori_loop(0, members, outward, 0)
    whole[0] = reach[0]
    whole[1] = reach[1]
    reach[0] = jnp.zeros((width, width), jnp.float32)

    def inward(i, _):
        e = members - 1 - i

        @pl.when(e == mine)
        def _():
            own[2] = reach[0]

        reach[0] = apply_split(reach[0], *split(spans[e, 1])) + crossing[e]
        return 0

    lax.fori_loop(0, members, inward, 0)
    whole[2] = reach[0]


def join(position, spans, after):
    members, parts, width, _ = spans.shape
    return call(
        join_body,
        [shape(parts, width, width), shape(parts, width, width)],
        [pltpu.VMEM((2, width, width), jnp.float32), pltpu.VMEM((members, width, width), jnp.float32)],
        members * 6 * 4 * width**3,
        spans,
        after=after,
        position=position,
    )


def relay(mine, spans, ends, entered):
    members, _, width, _ = spans.shape
    count = (ends.shape[1] - 8) // 2
    state = jnp.zeros((count, width), jnp.float32)
    states = []
    for e in range(members):
        states.append(state)

        @pl.when(mine == e)
        def _(state=state):
            entered[0] = state

        end = ends[e, :count]
        state = end if e == 0 else apply_split(state, *split(spans[e, 0])) + end
    ahead = state
    state = jnp.zeros((count, width), jnp.float32)
    for e in reversed(range(members)):

        @pl.when(mine == e)
        def _(state=state):
            entered[1] = state

        end = ends[e, count : 2 * count]
        if e > 0:
            end = end + apply_split(states[e], *split(spans[e, 2]))
        state = end if e == members - 1 else apply_split(state, *split(spans[e, 1])) + end
    return ahead, state


def total_of(ends):
    count = (ends.shape[1] - 8) // 2
    total = ends[0, 2 * count :]
    for e in range(1, ends.shape[0]):
        total = total + ends[e, 2 * count :]
    return total


def near_body(position, spans, ends, entered, whole):
    count = entered.shape[1]
    ahead, behind = relay(position[0], spans, ends, entered)
    whole[:count] = ahead
    whole[count : 2 * count] = behind
    whole[2 * count :] = total_of(ends)


def near(position, spans, ends):
    members, length, width = ends.shape
    count = (length - 8) // 2
    return call(
        near_body,
        [shape(2, count, width), shape(length, width)],
        [],
        members * 6 * 3 * count * width * width,
        spans,
        ends,
        position=position,
    )


def far_body(position, spans, ends, own, inner, entering, squares, entered):
    relay(position[0], spans, ends, entered)
    ahead, behind = entered[0], entered[1]
    entering[0] = apply_split(ahead, *split(own[0])) + inner[0]
    entering[1] = (
        apply_split(behind, *split(own[1])) + apply_split(ahead, *split(own[2])) + inner[1]
    )
    squares[...] = total_of(ends)


def far(position, spans, ends, own, inner):
    members, length, width = ends.shape
    count = (length - 8) // 2
    return call(
        far_body,
        [shape(2, count, width), shape(8, width)],
        [pltpu.VMEM((2, count, width), jnp.float32)],
        members * 6 * 3 * count * width * width,
        spans,
        ends,
        own,
        inner,
        position=position,
    )


def row_sums(total):
    ones = jnp.ones((8, total.shape[1]), jnp.float32)
    return lax.dot_general(
        ones,
        total,
        (((1,), (1,)), ((), ())),
        precision=lax.Precision.HIGHEST,
        preferred_element_type=jnp.float32,
    )


def first_body(high, low, forward, entering, middle_ends, turn, twist, solved, message):
    rows, count, width = forward.shape

    def step(i, carry):
        state, total = carry
        j = rows - 1 - i
        state = apply_split(forward[j] + state, high[j], low[j])
        solved[j] = state
        return state, total + state * state

    start = entering[...]
    zero = jnp.zeros((count, width), jnp.float32)
    _, total = lax.fori_loop(0, rows, step, (start, zero), unroll=2)
    message[:count] = middle_ends[0] + apply_split(start, *split(turn[...]))
    message[count : 2 * count] = middle_ends[1] + apply_split(start, *split(twist[...]))
    message[2 * count :] = jnp.zeros((8, width), jnp.float32)
    message[2 * count :, :count] = row_sums(total)


def first_rows(high, low, forward, entering, middle_ends, turn, twist):
    rows, count, width = forward.shape
    return call(
        first_body,
        [shape(*forward.shape), shape(2 * count + 8, width)],
        [],
        rows * 6 * count * width * width,
        high,
        low,
        forward,
        entering,
        middle_ends,
        turn,
        twist,
    )


def second_body(high, low, source, entering, scale, result, squares, forward):
    rows, count, width = source.shape
    inverse = 1.0 / scale[...]

    def ahead(i, state):
        state = apply_split(state, high[i], low[i]) + source[i]
        forward[i] = state
        return state

    lax.fori_loop(0, rows, ahead, entering[0], unroll=2)

    def behind(i, carry):
        state, total = carry
        j = rows - 1 - i
        state = apply_split(forward[j] + state, high[j], low[j])
        value = state * inverse
        result[j] = value
        return state, total + value * value

    zero = jnp.zeros((count, width), jnp.float32)
    _, total = lax.fori_loop(0, rows, behind, (entering[1], zero), unroll=2)
    squares[...] = jnp.zeros(squares.shape, jnp.float32)
    squares[:, :count] = row_sums(total)


def second_rows(high, low, source, entering, scale):
    rows, count, width = source.shape
    return call(
        second_body,
        [shape(*source.shape), shape(8, 128)],
        [pltpu.VMEM(source.shape, jnp.float32)],
        2 * rows * 6 * count * width * width,
        high,
        low,
        source,
        entering,
        scale,
    )


def scale_body(vectors, scale, result):
    result[...] = vectors[...] * (1.0 / scale[...])[None]


def rescale(vectors, scale):
    return call(scale_body, [shape(*vectors.shape)], [], vectors.size, vectors, scale)[0]


def to_all(value, axis):
    copies = jnp.broadcast_to(value[None], (lax.axis_size(axis), *value.shape))
    return lax.all_to_all(copies, axis, 0, 0, tiled=True)


def shards(start_vectors, factors):
    rows, count, width = start_vectors.shape
    cell_count = rows * lax.axis_size(CHAIN) * width
    whole = lax.all_gather(factors, "cols", axis=1, tiled=True)
    high, low, forward, prefix, suffix = prepare(whole, start_vectors)
    first_end, cross, turn, twist = couple(high, low, forward, prefix, suffix)
    operators = jnp.stack([prefix[rows - 1], suffix[0], cross])
    near_spans = lax.all_gather(operators, "inner")
    near_position = lax.axis_index("inner").astype(jnp.int32)[None]
    far_position = lax.axis_index("outer").astype(jnp.int32)[None]
    zero = jnp.zeros((count, width), jnp.float32)

    entering, early = scan_spans(prefix[rows - 1], forward[rows - 1], False)
    end = first_end + matmul(entering, cross)
    own, composed = join(near_position, near_spans, early[-1])
    far_spans = lax.all_gather(composed, "outer")
    leaving, arrivals = scan_spans(suffix[0], end, True)
    forward = sweep(high, low, start_vectors, entering, False, arrivals[0])
    middle = sweep(high, low, forward, zero, True, arrivals[1])
    middle = sweep(high, low, middle, zero, False, arrivals[2])
    middle_ahead = middle[rows - 1]
    middle_behind = sweep(high, low, middle, zero, True, arrivals[-2])[0]
    entering = leaving

    middle_ends = jnp.stack([middle_ahead, middle_behind])
    first_solve, message = first_rows(high, low, forward, entering, middle_ends, turn, twist)
    inner, message = near(near_position, near_spans, to_all(message, "inner"))
    entering, squares = far(far_position, far_spans, to_all(message, "outer"), own, inner)
    scale_one = jnp.sqrt(squares[0, :count] / cell_count + eps_value)
    second, squares = second_rows(high, low, first_solve, entering, scale_one[:, None])
    squares = jnp.sum(to_all(squares, "inner"), axis=0)
    squares = jnp.sum(to_all(squares, "outer"), axis=0)
    scale_two = jnp.sqrt(squares[0, :count] / cell_count + eps_value)
    return rescale(second, scale_two[:, None]), jnp.log(scale_two)


def solution(mesh):
    size = mesh.shape["chain"]
    inner = 1 << ((size - 1).bit_length() // 2)
    devices = mesh.devices.reshape(size // inner, inner, mesh.shape["cols"])
    placed = P(CHAIN, "cols", None)
    return jax.shard_map(
        shards,
        mesh=Mesh(devices, (*CHAIN, "cols")),
        in_specs=(placed, placed),
        out_specs=(placed, P("cols")),
        check_vma=False,
    )
```

time: 409 us -> 392 us (0.958)
  starting transfers between devices: 145 us -> 50 us
  waiting for transfers between devices: 101 us -> 149 us
  blocking collectives: 29.4 us -> 59 us
  matrix products: 26.5 us -> 8.75 us
  Pallas kernels: 81.5 us -> 95.9 us
    ppermute x34 -> x12, starting transfers between devices: 135 us -> 49.9 us  [exchange(): lax.ppermute(value, CHAIN, [(i, i ^ 1 << level) for i in range(size)])]
    ppermute x34 -> x12, waiting for transfers between devices: 34.3 us -> 82.2 us  [exchange(): lax.ppermute(value, CHAIN, [(i, i ^ 1 << level) for i in range(size)])]
    all_to_all x2 -> x4, blocking collectives: 29.4 us -> 59 us  [to_all(): return lax.all_to_all(copies, axis, 0, 0, tiled=True)]
    dot_general x59 -> x21, matrix products: 26.5 us -> 8.75 us  [matmul(): jnp.dot(left, right, precision=lax.Precision.HIGHEST, preferred_element_t...]
    pallas_call x12, Pallas kernels: 81.5 us -> 95.9 us  [call(): pl.pallas_call(kernel, out_shape=tuple(out_shapes), in_specs=specs, out_s...]
    all_to_all x2 -> x0, starting transfers between devices: 10.2 us -> none  [chain_total(): lax.all_to_all(copies, 'chain', 0, 0, axis_index_groups=members, tiled=True)]
  transfers between devices with their start and end apart: 37 -> 15, of which waited for: 19 -> 13; matrix products, arithmetic and copies ran while one was open for 7% -> 4% of each run, Pallas kernels for 13% -> 9%
where the time goes in v2:
time: 392 us; the launch traced here: 391 us
  waiting for transfers between devices  149 us (38%)
  Pallas kernels  95.9 us (24%)
  blocking collectives  59 us (15%)
  starting transfers between devices  50 us (13%)
  between operations  14.3 us (4%)
  matrix products  8.75 us (2%)
  local copies, waits for them, and re-layouts  8.08 us (2%)
  other arithmetic  5.68 us (1%)
    pallas_call x12, Pallas kernels, call(): pl.pallas_call(kernel, out_shape=tuple(out_shapes), in_specs=specs, out_s...  95.9 us
    ppermute x12, waiting for transfers between devices, exchange(): lax.ppermute(value, CHAIN, [(i, i ^ 1 << level) for i in range(size)])  82.2 us
    all_gather x1, waiting for transfers between devices, shards(): whole = lax.all_gather(factors, 'cols', axis=1, tiled=True)  65.9 us
    all_to_all x4, blocking collectives, to_all(): return lax.all_to_all(copies, axis, 0, 0, tiled=True)  59 us
    ppermute x12, starting transfers between devices, exchange(): lax.ppermute(value, CHAIN, [(i, i ^ 1 << level) for i in range(size)])  49.9 us
    dot_general x21, matrix products, matmul(): jnp.dot(left, right, precision=lax.Precision.HIGHEST, preferred_element_t...  8.75 us
  transfers between devices with their start and end apart: 15, of which 13 were waited for; matrix products, arithmetic and copies ran while one was open for 4% of the time, Pallas kernels for 9%

profile of v2, /device:TPU:1, one launch (start us, length us, event | category | flops | bytes accessed | tf_op | source)
XLA Modules:
  0.0 390.6 jit_solution(11663958422083124514)
XLA Ops:
  7.9 65.9 %all-gather.6.cloned.1.call-done.factors = f32[16,256,256]{2,1,0:T(8,128)} async-done(((f32[16,32,256]{2,1,0:T(8,128)}), f32[16,256,256]{2,1,0:T(8,128)}) %all-gather.6.cloned.1.call-update) | async-done | bytes 4194320 | tf_op jit(solution)/shard_map/all_gather | solution.py:481
  73.9 15.3 %shard_map.41 = (bf16[16,256,256]{2,1,0:T(8,128)(2,1)}, bf16[16,256,256]{2,1,0:T(8,128)(2,1)}, f32[16,32,256]{2,1,0:T(8,128)}, f32[16,256,256]{2,1,0:T(8,128)}, f32[16,256,256]{2,1,0:T(8,128)}) custom-call(f32[16,256,256]{2,1,0:T(8,128)} %all-gather.6.cloned.1.call-done.factors, f32[16,32,256]{2,1,0:T(8,128)} %refs_2_.1), custom_call_target="tpu_custom_call" | custom-call | flops 3422552064 | bytes 17825792 | tf_op jit(solution)/shard_map/pallas_call | solution.py:55
  91.2 16.4 %shard_map.42 = (f32[32,256]{1,0:T(8,128)}, f32[256,256]{1,0:T(8,128)}, f32[256,256]{1,0:T(8,128)}, f32[256,256]{1,0:T(8,128)}) custom-call(bf16[16,256,256]{2,1,0:T(8,128)(2,1)} %get-tuple-element.21.high.refs_0_, bf16[16,256,256]{2,1,0:T(8,128)(2,1)} %get-tuple-element.22.low.refs_1_, f32[16,32,256]{2,1,0:T(8,128)} %get-tuple-element.24.forward, ...), custom_call_target="tpu_custom_call" | custom-call | flops 5033164800 | bytes 13926400 | tf_op jit(solution)/shard_map/pallas_call | solution.py:55
  117.7 7.0 %collective-permute-done.1 = f32[288,256]{1,0:T(8,128)S(1)} collective-permute-done((f32[288,256]{1,0:T(8,128)S(1)}, f32[288,256]{1,0:T(8,128)S(1)}, u32[]{:S(2)}, u32[]{:S(2)}) %collective-permute-start.1) | collective-permute-done | bytes 294944 | tf_op jit(solution)/shard_map/ppermute | solution.py:206
  125.1 4.6 %collective-permute-start.2 = (f32[288,256]{1,0:T(8,128)S(1)}, f32[288,256]{1,0:T(8,128)S(1)}, u32[]{:S(2)}, u32[]{:S(2)}) collective-permute-start(f32[288,256]{1,0:T(8,128)S(1)} %convolution_add_fusion.6), channel_id=1, source_target_pairs={{0,32},{8,40},{16,48},{24,56},{32,0},{40,8},{48,16},{56,24},{64,96... | collective-permute-start | bytes 884744 | tf_op jit(solution)/shard_map/ppermute | solution.py:206
  130.2 13.1 %collective-permute-done.2 = f32[288,256]{1,0:T(8,128)S(1)} collective-permute-done((f32[288,256]{1,0:T(8,128)S(1)}, f32[288,256]{1,0:T(8,128)S(1)}, u32[]{:S(2)}, u32[]{:S(2)}) %collective-permute-start.2) | collective-permute-done | bytes 294944 | tf_op jit(solution)/shard_map/ppermute | solution.py:206
  143.8 3.1 collective-permute-start.3
  147.4 4.9 %collective-permute-done.3 = f32[288,256]{1,0:T(8,128)S(1)} collective-permute-done((f32[288,256]{1,0:T(8,128)S(1)}, f32[288,256]{1,0:T(8,128)S(1)}, u32[]{:S(2)}, u32[]{:S(2)}) %collective-permute-start.3) | collective-permute-done | bytes 294944 | tf_op jit(solution)/shard_map/ppermute | solution.py:206
  152.7 4.0 %collective-permute-start.4 = (f32[288,256]{1,0:T(8,128)S(1)}, f32[288,256]{1,0:T(8,128)S(1)}, u32[]{:S(2)}, u32[]{:S(2)}) collective-permute-start(f32[288,256]{1,0:T(8,128)S(1)} %convolution_add_fusion.4), channel_id=1, source_target_pairs={{0,128},{8,136},{16,144},{24,152},{32,160},{40,168},{48,176},{56,1... | collective-permute-start | bytes 884744 | tf_op jit(solution)/shard_map/ppermute | solution.py:206
  157.2 12.5 %collective-permute-done.4 = f32[288,256]{1,0:T(8,128)S(1)} collective-permute-done((f32[288,256]{1,0:T(8,128)S(1)}, f32[288,256]{1,0:T(8,128)S(1)}, u32[]{:S(2)}, u32[]{:S(2)}) %collective-permute-start.4) | collective-permute-done | bytes 294944 | tf_op jit(solution)/shard_map/ppermute | solution.py:206
  170.8 10.0 %shard_map.48 = (f32[3,256,256]{2,1,0:T(8,128)}, f32[3,256,256]{2,1,0:T(8,128)}) custom-call(f32[32,256]{1,0:T(8,128)} %add_select_fusion.4._, s32[1]{0:T(128)} %bitcast.4.refs_0_.position, f32[8,3,256,256]{3,2,1,0:T(8,128)} %bitcast.33), custom_call_target="tpu_custom_call" | custom-call | flops 3221225472 | bytes 7864320 | tf_op jit(solution)/shard_map/pallas_call | solution.py:55
  181.4 8.0 %collective-permute-start.5 = (f32[32,256]{1,0:T(8,128)S(1)}, f32[32,256]{1,0:T(8,128)S(1)}, u32[]{:S(2)}, u32[]{:S(2)}) collective-permute-start(f32[32,256]{1,0:T(8,128)S(1)} %pad_add_fusion.1), channel_id=1, source_target_pairs={{0,256},{8,264},{16,272},{24,280},{32,288},{40,296},{48,304},{56,3... | collective-permute-start | bytes 98312 | tf_op jit(solution)/shard_map/ppermute | solution.py:206
  191.2 3.9 collective-permute-start.6
  199.0 8.0 %collective-permute-done.7 = f32[288,256]{1,0:T(8,128)S(1)} collective-permute-done((f32[288,256]{1,0:T(8,128)S(1)}, f32[288,256]{1,0:T(8,128)S(1)}, u32[]{:S(2)}, u32[]{:S(2)}) %collective-permute-start.7) | collective-permute-done | bytes 294944 | tf_op jit(solution)/shard_map/ppermute | solution.py:206
  207.4 4.6 %collective-permute-start.8 = (f32[288,256]{1,0:T(8,128)S(1)}, f32[288,256]{1,0:T(8,128)S(1)}, u32[]{:S(2)}, u32[]{:S(2)}) collective-permute-start(f32[288,256]{1,0:T(8,128)S(1)} %convolution_add_fusion.2), channel_id=1, source_target_pairs={{0,32},{8,40},{16,48},{24,56},{32,0},{40,8},{48,16},{56,24},{64,96... | collective-permute-start | bytes 884744 | tf_op jit(solution)/shard_map/ppermute | solution.py:206
  212.5 5.8 %collective-permute-done.8 = f32[288,256]{1,0:T(8,128)S(1)} collective-permute-done((f32[288,256]{1,0:T(8,128)S(1)}, f32[288,256]{1,0:T(8,128)S(1)}, u32[]{:S(2)}, u32[]{:S(2)}) %collective-permute-start.8) | collective-permute-done | bytes 294944 | tf_op jit(solution)/shard_map/ppermute | solution.py:206
  221.2 13.9 %collective-permute-done.9 = f32[288,256]{1,0:T(8,128)S(1)} collective-permute-done((f32[288,256]{1,0:T(8,128)S(1)}, f32[288,256]{1,0:T(8,128)S(1)}, u32[]{:S(2)}, u32[]{:S(2)}) %collective-permute-start.9) | collective-permute-done | bytes 294944 | tf_op jit(solution)/shard_map/ppermute | solution.py:206
  236.3 5.9 %shard_map.43.refs_2_.forward = f32[16,32,256]{2,1,0:T(8,128)} custom-call(f32[32,256]{1,0:T(8,128)} %get-tuple-element.43._, bf16[16,256,256]{2,1,0:T(8,128)(2,1)} %get-tuple-element.21.high.refs_0_, bf16[16,256,256]{2,1,0:T(8,128)(2,1)} %get-tuple-element.22.low.refs_1_, f32[16,32,256]{2,1,0:T(8,128)} %refs_2_.1, f32[32,256]{1,0:T(8,128)} %copy-done.1), custom_call_target="tpu_custom_call" | custom-call | flops 201326592 | bytes 5275648 | tf_op jit(solution)/shard_map/pallas_call | solution.py:55
  242.8 5.9 %shard_map.44.refs_2_ = f32[16,32,256]{2,1,0:T(8,128)} custom-call(f32[32,256]{1,0:T(8,128)} %get-tuple-element.42._, bf16[16,256,256]{2,1,0:T(8,128)(2,1)} %get-tuple-element.21.high.refs_0_, bf16[16,256,256]{2,1,0:T(8,128)(2,1)} %get-tuple-element.22.low.refs_1_, f32[16,32,256]{2,1,0:T(8,128)} %shard_map.43.refs_2_.forward, ...), custom_call_target="tpu_custom_call" | custom-call | flops 201326592 | bytes 5275648 | tf_op jit(solution)/shard_map/pallas_call | solution.py:55
  248.7 5.9 %shard_map.45.refs_2_ = f32[16,32,256]{2,1,0:T(8,128)} custom-call(f32[32,256]{1,0:T(8,128)} %get-tuple-element.41._, bf16[16,256,256]{2,1,0:T(8,128)(2,1)} %get-tuple-element.21.high.refs_0_, bf16[16,256,256]{2,1,0:T(8,128)(2,1)} %get-tuple-element.22.low.refs_1_, f32[16,32,256]{2,1,0:T(8,128)} %shard_map.44.refs_2_, f32[32,256]{1,0:T(8,128)} %broadcast_7_refs_3_.2.refs_3_), custom_call_target="tpu_custom_call" | custom-call | flops 201326592 | bytes 5275648 | tf_op jit(solution)/shard_map/pallas_call | solution.py:55
  254.6 5.9 %shard_map.46 = f32[16,32,256]{2,1,0:T(8,128)} custom-call(f32[32,256]{1,0:T(8,128)} %get-tuple-element.40._, bf16[16,256,256]{2,1,0:T(8,128)(2,1)} %get-tuple-element.21.high.refs_0_, bf16[16,256,256]{2,1,0:T(8,128)(2,1)} %get-tuple-element.22.low.refs_1_, f32[16,32,256]{2,1,0:T(8,128)} %shard_map.45.refs_2_, f32[32,256]{1,0:T(8,128)} %broadcast_7_refs_3_.2.refs_3_), custom_call_target="tpu_custom_call" | custom-call | flops 201326592 | bytes 5275648 | tf_op jit(solution)/shard_map/pallas_call | solution.py:55
  261.8 3.9 collective-permute-start.10
  266.4 12.7 %collective-permute-done.10 = f32[288,256]{1,0:T(8,128)S(1)} collective-permute-done((f32[288,256]{1,0:T(8,128)S(1)}, f32[288,256]{1,0:T(8,128)S(1)}, u32[]{:S(2)}, u32[]{:S(2)}) %collective-permute-start.10) | collective-permute-done | bytes 294944 | tf_op jit(solution)/shard_map/ppermute | solution.py:206
  279.6 7.8 %collective-permute-start.11 = (f32[32,256]{1,0:T(8,128)S(1)}, f32[32,256]{1,0:T(8,128)S(1)}, u32[]{:S(2)}, u32[]{:S(2)}) collective-permute-start(f32[32,256]{1,0:T(8,128)S(1)} %pad_add_fusion), channel_id=1, source_target_pairs={{0,256},{8,264},{16,272},{24,280},{32,288},{40,296},{48,304},{56,3... | collective-permute-start | bytes 98312 | tf_op jit(solution)/shard_map/ppermute | solution.py:206
  289.4 6.1 %shard_map.47 = (f32[16,32,256]{2,1,0:T(8,128)}, f32[72,256]{1,0:T(8,128)}) custom-call(bf16[16,256,256]{2,1,0:T(8,128)(2,1)} %get-tuple-element.21.high.refs_0_, bf16[16,256,256]{2,1,0:T(8,128)(2,1)} %get-tuple-element.22.low.refs_1_, f32[16,32,256]{2,1,0:T(8,128)} %shard_map.43.refs_2_.forward, f32[32,256]{1,0:T(8,128)} %fusion.entering, ...), custom_call_target="tpu_custom_call" | custom-call | flops 201326592 | bytes 5939200 | tf_op jit(solution)/shard_map/pallas_call | solution.py:55
  296.4 16.6 %all_to_all.20.ends = f32[8,72,256]{2,1,0:T(8,128)} all-to-all(f32[8,72,256]{2,1,0:T(8,128)S(1)} %broadcast_in_dim.14), channel_id=1, replica_groups=mesh['outer'=8,'inner'=8,'cols'=8] {'inner'}, dimensions={0} | all-to-all | bytes 1179648 | tf_op jit(solution)/shard_map/all_to_all | solution.py:475
  313.1 6.8 %shard_map.49 = (f32[2,32,256]{2,1,0:T(8,128)}, f32[72,256]{1,0:T(8,128)}) custom-call(s32[1]{0:T(128)} %bitcast.4.refs_0_.position, f32[8,3,256,256]{3,2,1,0:T(8,128)} %bitcast.34, f32[8,72,256]{2,1,0:T(8,128)} %all_to_all.20.ends), custom_call_target="tpu_custom_call" | custom-call | flops 301989888 | bytes 7020544 | tf_op jit(solution)/shard_map/pallas_call | solution.py:55
  320.8 23.5 %all_to_all.21.ends = f32[8,72,256]{2,1,0:T(8,128)} all-to-all(f32[8,72,256]{2,1,0:T(8,128)S(1)} %broadcast_in_dim.15), channel_id=1, replica_groups=mesh['outer'=8,'inner'=8,'cols'=8] {'outer'}, dimensions={0} | all-to-all | bytes 1179648 | tf_op jit(solution)/shard_map/all_to_all | solution.py:475
  344.3 6.9 %shard_map.50 = (f32[2,32,256]{2,1,0:T(8,128)}, f32[8,256]{1,0:T(8,128)}) custom-call(s32[1]{0:T(128)} %bitcast.3.position, f32[8,3,256,256]{3,2,1,0:T(8,128)} %bitcast.35, f32[8,72,256]{2,1,0:T(8,128)} %all_to_all.21.ends, f32[3,256,256]{2,1,0:T(8,128)} %get-tuple-element.34.own, f32[2,32,256]{2,1,0:T(8,128)} %get-tuple-element.35.inner), custom_call_target="tpu_custom_call" | custom-call | flops 301989888 | bytes 7806976 | tf_op jit(solution)/shard_map/pallas_call | solution.py:55
  352.6 8.7 %shard_map.51 = (f32[16,32,256]{2,1,0:T(8,128)}, f32[8,128]{1,0:T(8,128)}) custom-call(bf16[16,256,256]{2,1,0:T(8,128)(2,1)} %get-tuple-element.21.high.refs_0_, bf16[16,256,256]{2,1,0:T(8,128)(2,1)} %get-tuple-element.22.low.refs_1_, f32[16,32,256]{2,1,0:T(8,128)} %get-tuple-element.30.source, f32[2,32,256]{2,1,0:T(8,128)} %get-tuple-element.36.entering, ...), custom_call_target="tpu_custom_call" | custom-call | flops 402653184 | bytes 5312640 | tf_op jit(solution)/shard_map/pallas_call | solution.py:55
  362.0 9.6 %all_to_all.22 = f32[8,8,128]{2,1,0:T(8,128)S(1)} all-to-all(f32[8,8,128]{2,1,0:T(8,128)S(1)} %broadcast_in_dim.16), channel_id=1, replica_groups=mesh['outer'=8,'inner'=8,'cols'=8] {'inner'}, dimensions={0} | all-to-all | bytes 65536 | tf_op jit(solution)/shard_map/all_to_all | solution.py:475
  371.7 9.2 %all_to_all.23 = f32[8,8,128]{2,1,0:T(8,128)S(1)} all-to-all(f32[8,8,128]{2,1,0:T(8,128)S(1)} %broadcast_in_dim.17), channel_id=1, replica_groups=mesh['outer'=8,'inner'=8,'cols'=8] {'outer'}, dimensions={0} | all-to-all | bytes 65536 | tf_op jit(solution)/shard_map/all_to_all | solution.py:475
  (97 shorter events, 39.6 us)
Async XLA Ops:
  7.2 66.7 %all-gather.6.cloned.1.call-start = ((), (), s32[]{:S(2)}) async-start(), calls=%async_computation.4 | async-start | bytes 4718592 | tf_op jit(solution)/shard_map/all_gather | solution.py:481
  7.9 162.9 %all-gather.8.cloned.1.call-start = ((), (), s32[]{:S(2)}) async-start(), calls=%async_computation.5 | async-start | bytes 7077888 | tf_op jit(solution)/shard_map/all_gather | solution.py:485
  109.5 234.9 %all-gather.10.cloned.1.call-start = ((), (), s32[]{:S(2)}) async-start(), calls=%async_computation.6 | async-start | bytes 7077888 | tf_op jit(solution)/shard_map/all_gather | solution.py:493
  110.3 3.8 collective-permute-start
  114.5 10.1 %collective-permute-start.1 = (f32[288,256]{1,0:T(8,128)S(1)}, f32[288,256]{1,0:T(8,128)S(1)}, u32[]{:S(2)}, u32[]{:S(2)}) collective-permute-start(f32[288,256]{1,0:T(8,128)S(1)} %convolution_add_fusion.7), channel_id=1, source_target_pairs={{0,16},{8,24},{16,0},{24,8},{32,48},{40,56},{48,32},{56,40},{64,80... | collective-permute-start | bytes 884744 | tf_op jit(solution)/shard_map/ppermute | solution.py:206
  125.1 18.2 %collective-permute-start.2 = (f32[288,256]{1,0:T(8,128)S(1)}, f32[288,256]{1,0:T(8,128)S(1)}, u32[]{:S(2)}, u32[]{:S(2)}) collective-permute-start(f32[288,256]{1,0:T(8,128)S(1)} %convolution_add_fusion.6), channel_id=1, source_target_pairs={{0,32},{8,40},{16,48},{24,56},{32,0},{40,8},{48,16},{56,24},{64,96... | collective-permute-start | bytes 884744 | tf_op jit(solution)/shard_map/ppermute | solution.py:206
  143.8 8.5 %collective-permute-start.3 = (f32[288,256]{1,0:T(8,128)S(1)}, f32[288,256]{1,0:T(8,128)S(1)}, u32[]{:S(2)}, u32[]{:S(2)}) collective-permute-start(f32[288,256]{1,0:T(8,128)S(1)} %convolution_add_fusion.5), channel_id=1, source_target_pairs={{0,64},{8,72},{16,80},{24,88},{32,96},{40,104},{48,112},{56,120},{... | collective-permute-start | bytes 884744 | tf_op jit(solution)/shard_map/ppermute | solution.py:206
  152.7 17.0 %collective-permute-start.4 = (f32[288,256]{1,0:T(8,128)S(1)}, f32[288,256]{1,0:T(8,128)S(1)}, u32[]{:S(2)}, u32[]{:S(2)}) collective-permute-start(f32[288,256]{1,0:T(8,128)S(1)} %convolution_add_fusion.4), channel_id=1, source_target_pairs={{0,128},{8,136},{16,144},{24,152},{32,160},{40,168},{48,176},{56,1... | collective-permute-start | bytes 884744 | tf_op jit(solution)/shard_map/ppermute | solution.py:206
  170.8 19.8 %copy-start.3 = (f32[32,256]{1,0:T(8,128)S(1)}, f32[32,256]{1,0:T(8,128)}, u32[]{:S(2)}) copy-start(f32[32,256]{1,0:T(8,128)} %add_select_fusion.4._) | copy-start | bytes 98308
  170.8 20.1 %copy-start = (f32[256,256]{1,0:T(8,128)S(1)}, f32[256,256]{1,0:T(8,128)}, u32[]{:S(2)}) copy-start(f32[256,256]{1,0:T(8,128)} %get-tuple-element.27) | copy-start | bytes 786436
  170.8 20.1 %copy-start.4 = (f32[32,256]{1,0:T(8,128)S(1)}, f32[32,256]{1,0:T(8,128)}, u32[]{:S(2)}) copy-start(f32[32,256]{1,0:T(8,128)} %get-tuple-element.26) | copy-start | bytes 98308
  181.4 9.3 %collective-permute-start.5 = (f32[32,256]{1,0:T(8,128)S(1)}, f32[32,256]{1,0:T(8,128)S(1)}, u32[]{:S(2)}, u32[]{:S(2)}) collective-permute-start(f32[32,256]{1,0:T(8,128)S(1)} %pad_add_fusion.1), channel_id=1, source_target_pairs={{0,256},{8,264},{16,272},{24,280},{32,288},{40,296},{48,304},{56,3... | collective-permute-start | bytes 98312 | tf_op jit(solution)/shard_map/ppermute | solution.py:206
  190.9 29.9 %copy-start.1 = (f32[32,256]{1,0:T(8,128)}, f32[32,256]{1,0:T(8,128)S(1)}, u32[]{:S(2)}) copy-start(f32[32,256]{1,0:T(8,128)S(1)} %fusion.1.refs_3_) | copy-start | bytes 98308
  191.2 5.1 %collective-permute-start.6 = (f32[288,256]{1,0:T(8,128)S(1)}, f32[288,256]{1,0:T(8,128)S(1)}, u32[]{:S(2)}, u32[]{:S(2)}) collective-permute-start(f32[288,256]{1,0:T(8,128)S(1)} %pad_maximum_fusion.2), channel_id=1, source_target_pairs={{0,8},{8,0},{16,24},{24,16},{32,40},{40,32},{48,56},{56,48},{64,72... | collective-permute-start | bytes 884744 | tf_op jit(solution)/shard_map/ppermute | solution.py:206
  196.7 10.2 %collective-permute-start.7 = (f32[288,256]{1,0:T(8,128)S(1)}, f32[288,256]{1,0:T(8,128)S(1)}, u32[]{:S(2)}, u32[]{:S(2)}) collective-permute-start(f32[288,256]{1,0:T(8,128)S(1)} %convolution_add_fusion.3), channel_id=1, source_target_pairs={{0,16},{8,24},{16,0},{24,8},{32,48},{40,56},{48,32},{56,40},{64,80... | collective-permute-start | bytes 884744 | tf_op jit(solution)/shard_map/ppermute | solution.py:206
  207.4 10.8 %collective-permute-start.8 = (f32[288,256]{1,0:T(8,128)S(1)}, f32[288,256]{1,0:T(8,128)S(1)}, u32[]{:S(2)}, u32[]{:S(2)}) collective-permute-start(f32[288,256]{1,0:T(8,128)S(1)} %convolution_add_fusion.2), channel_id=1, source_target_pairs={{0,32},{8,40},{16,48},{24,56},{32,0},{40,8},{48,16},{56,24},{64,96... | collective-permute-start | bytes 884744 | tf_op jit(solution)/shard_map/ppermute | solution.py:206
  218.7 16.5 %collective-permute-start.9 = (f32[288,256]{1,0:T(8,128)S(1)}, f32[288,256]{1,0:T(8,128)S(1)}, u32[]{:S(2)}, u32[]{:S(2)}) collective-permute-start(f32[288,256]{1,0:T(8,128)S(1)} %convolution_add_fusion.1), channel_id=1, source_target_pairs={{0,64},{8,72},{16,80},{24,88},{32,96},{40,104},{48,112},{56,120},{... | collective-permute-start | bytes 884744 | tf_op jit(solution)/shard_map/ppermute | solution.py:206
  254.6 11.0 %slice-start = ((f32[16,32,256]{2,1,0:T(8,128)}), f32[1,32,256]{2,1,0:T(8,128)S(1)}, s32[]{:S(2)}) async-start(f32[16,32,256]{2,1,0:T(8,128)} %shard_map.45.refs_2_), calls=%async_computation.7 | async-start | bytes 65536 | tf_op jit(solution)/shard_map/slice | solution.py:498
  260.5 28.0 %copy-start.2 = (f32[32,256]{1,0:T(8,128)S(1)}, f32[32,256]{1,0:T(8,128)}, u32[]{:S(2)}) copy-start(f32[32,256]{1,0:T(8,128)} %get-tuple-element.40._) | copy-start | bytes 98308
  261.8 17.3 %collective-permute-start.10 = (f32[288,256]{1,0:T(8,128)S(1)}, f32[288,256]{1,0:T(8,128)S(1)}, u32[]{:S(2)}, u32[]{:S(2)}) collective-permute-start(f32[288,256]{1,0:T(8,128)S(1)} %convolution_add_fusion), channel_id=1, source_target_pairs={{0,128},{8,136},{16,144},{24,152},{32,160},{40,168},{48,176},{56,1... | collective-permute-start | bytes 884744 | tf_op jit(solution)/shard_map/ppermute | solution.py:206
  279.6 8.9 %collective-permute-start.11 = (f32[32,256]{1,0:T(8,128)S(1)}, f32[32,256]{1,0:T(8,128)S(1)}, u32[]{:S(2)}, u32[]{:S(2)}) collective-permute-start(f32[32,256]{1,0:T(8,128)S(1)} %pad_add_fusion), channel_id=1, source_target_pairs={{0,256},{8,264},{16,272},{24,280},{32,288},{40,296},{48,304},{56,3... | collective-permute-start | bytes 98312 | tf_op jit(solution)/shard_map/ppermute | solution.py:206
Sparse Core Ops, SparseCore 0:
  10.1 63.7 all-gather.5
  109.6 51.0 all-gather.7
  181.0 80.6 all-gather.9

commit v3 on v2

--- a/solution.py
+++ b/solution.py
@@ -31,13 +31,7 @@
     )
 
 
-def matmul(left, right):
-    return jnp.dot(
-        left, right, precision=lax.Precision.HIGHEST, preferred_element_type=jnp.float32
-    )
-
-
-def call(body, out_shapes, scratch, flops, *operands, after=None, position=None):
+def call(body, out_shapes, scratch, flops, *operands, after=(), position=None):
     vmem = pl.BlockSpec(memory_space=pltpu.VMEM)
     touched = sum(x.size * x.dtype.itemsize for x in (*operands, *out_shapes))
     specs = [vmem] * len(operands)
@@ -45,12 +39,12 @@
         specs = [pl.BlockSpec(memory_space=pltpu.SMEM), *specs]
         operands = (position, *operands)
     kernel = body
-    if after is not None:
-        specs = [pl.BlockSpec(memory_space=pl.ANY), *specs]
-        operands = (after, *operands)
-
-        def kernel(_, *refs):
-            body(*refs)
+    if after:
+        specs = [pl.BlockSpec(memory_space=pl.ANY)] * len(after) + specs
+        operands = (*after, *operands)
+
+        def kernel(*refs):
+            body(*refs[len(after) :])
 
     return pl.pallas_call(
         kernel,
@@ -67,20 +61,16 @@
     return jax.ShapeDtypeStruct(dims, dtype)
 
 
-def prepare_body(factors, source, high, low, forward, prefix, suffix, ahead, behind):
+def prepare_body(factors, source, high, low, suffix, cross, solved, operators, ends, prefix, forward, ahead, behind):
     rows, width, _ = factors.shape
     count = source.shape[1]
 
     def turn(i, _):
-        turned = factors[i].T
-        high[i], low[i] = split(turned)
+        high[i], low[i] = split(factors[i].T)
         return 0
 
     lax.fori_loop(0, rows, turn, 0)
-    eye = (
-        lax.broadcasted_iota(jnp.int32, (width, width), 0)
-        == lax.broadcasted_iota(jnp.int32, (width, width), 1)
-    ).astype(jnp.float32)
+    eye = identity(width)
     ahead[:count] = jnp.zeros((count, width), jnp.float32)
     ahead[count:] = eye
     behind[...] = eye
@@ -99,6 +89,24 @@
         return 0
 
     lax.fori_loop(0, rows, step, 0)
+    operators[0] = ahead[count:]
+    operators[1] = behind[...]
+    ends[:count] = ahead[:count]
+    ahead[...] = jnp.zeros_like(ahead)
+
+    def back(i, _):
+        j = rows - 1 - i
+        entering = jnp.concatenate([forward[j], prefix[j]], axis=0) + ahead[...]
+        state = apply_split(entering, high[j], low[j])
+        ahead[...] = state
+        solved[j] = state[:count]
+        cross[j] = state[count:]
+        return 0
+
+    lax.fori_loop(0, rows, back, 0)
+    operators[2] = ahead[count:]
+    ends[count : 2 * count] = ahead[:count]
+    ends[2 * count :] = jnp.zeros((8, width), jnp.float32)
 
 
 def prepare(factors, source):
@@ -110,133 +118,90 @@
         [
             shape(*square, dtype=jnp.bfloat16),
             shape(*square, dtype=jnp.bfloat16),
-            shape(*source.shape),
             shape(*square),
             shape(*square),
+            shape(*source.shape),
+            shape(3, width, width),
+            shape(2 * count + 8, width),
         ],
-        [pltpu.VMEM((count + width, width), jnp.float32), pltpu.VMEM((width, width), jnp.float32)],
-        rows * 6 * (count + 2 * width) * width * width,
+        [
+            pltpu.VMEM(square, jnp.float32),
+            pltpu.VMEM(source.shape, jnp.float32),
+            pltpu.VMEM((count + width, width), jnp.float32),
+            pltpu.VMEM((width, width), jnp.float32),
+        ],
+        rows * 6 * (2 * count + 3 * width) * width * width,
         factors,
         source,
     )
 
 
-def couple_body(high, low, forward, prefix, suffix, first_end, cross, turn, twist, behind, ahead, kept):
-    rows, count, width = forward.shape
-    ahead[...] = jnp.zeros_like(ahead)
-    behind[...] = jnp.zeros_like(behind)
+def ahead_body(high, low, cross, suffix, solved, rows_out, ends):
+    rows, count, width = solved.shape
+    ends[...] = jnp.zeros_like(ends)
+
+    def step(i, _):
+        source = jnp.concatenate([cross[i], suffix[i], solved[i]], axis=0)
+        state = apply_split(ends[...], high[i], low[i]) + source
+        ends[...] = state
+        rows_out[i] = state
+        return 0
+
+    lax.fori_loop(0, rows, step, 0)
+
+
+def behind_body(high, low, source, ends):
+    rows = source.shape[0]
+    ends[...] = jnp.zeros_like(ends)
 
     def step(i, _):
         j = rows - 1 - i
-        entering = jnp.concatenate([forward[j], prefix[j]], axis=0) + behind[...]
-        behind[...] = apply_split(entering, high[j], low[j])
-        state = apply_split(ahead[...], high[i], low[i]) + suffix[i]
-        ahead[...] = state
-        kept[i] = state
+        ends[...] = apply_split(source[j] + ends[...], high[j], low[j])
         return 0
 
     lax.fori_loop(0, rows, step, 0)
-    first_end[...] = behind[:count]
-    cross[...] = behind[count:]
-    turn[...] = ahead[...]
-    ahead[...] = jnp.zeros_like(ahead)
-
-    def back(i, _):
-        j = rows - 1 - i
-        ahead[...] = apply_split(kept[j] + ahead[...], high[j], low[j])
-        return 0
-
-    lax.fori_loop(0, rows, back, 0)
-    twist[...] = ahead[...]
-
-
-def couple(high, low, forward, prefix, suffix):
-    rows, count, width = forward.shape
-    square = (width, width)
-    return call(
-        couple_body,
-        [shape(count, width), shape(*square), shape(*square), shape(*square)],
-        [
-            pltpu.VMEM((count + width, width), jnp.float32),
-            pltpu.VMEM(square, jnp.float32),
-            pltpu.VMEM((rows, *square), jnp.float32),
-        ],
-        rows * 6 * (count + 3 * width) * width * width,
+
+
+def respond_ahead(high, low, cross, suffix, solved):
+    rows, count, width = solved.shape
+    length = 2 * width + count
+    return call(
+        ahead_body,
+        [shape(rows, length, width), shape(length, width)],
+        [],
+        rows * 6 * length * width * width,
         high,
         low,
-        forward,
-        prefix,
+        cross,
         suffix,
-    )
-
-
-def sweep_body(reverse, high, low, source, entering, result):
-    rows = source.shape[0]
-
-    def step(i, state):
-        if reverse:
-            j = rows - 1 - i
-            state = apply_split(source[j] + state, high[j], low[j])
-        else:
-            j = i
-            state = apply_split(state, high[j], low[j]) + source[j]
-        result[j] = state
-        return state
-
-    lax.fori_loop(0, rows, step, entering[...], unroll=2)
-
-
-def sweep(high, low, source, entering, reverse, after=None):
-    rows, count, width = source.shape
-    return call(
-        functools.partial(sweep_body, reverse),
-        [shape(*source.shape)],
+        solved,
+    )
+
+
+def respond_behind(high, low, source, after):
+    rows, length, width = source.shape
+    return call(
+        behind_body,
+        [shape(length, width)],
         [],
-        rows * 6 * count * width * width,
+        rows * 6 * length * width * width,
         high,
         low,
         source,
-        entering,
         after=after,
     )[0]
 
 
-def exchange(value, level):
-    size = lax.axis_size(CHAIN)
-    return lax.ppermute(value, CHAIN, [(i, i ^ (1 << level)) for i in range(size)])
-
-
-def scan_spans(operator, total, reverse):
-    width = operator.shape[0]
-    count = total.shape[0]
-    levels = (lax.axis_size(CHAIN) - 1).bit_length()
-    span = jnp.concatenate([operator, total], axis=0)
-    lead = None
-    entering = jnp.zeros_like(total)
-    arrivals = []
-    for level in range(levels):
-        after = (lax.axis_index(CHAIN) >> level) & 1 == (0 if reverse else 1)
-        if level + 1 == levels:
-            received = exchange(span[width:], level)
-            return jnp.where(after, entering + matmul(received, lead), entering), arrivals
-        received = exchange(span, level)
-        first = jnp.where(after, received, span)
-        second = jnp.where(after, span, received)
-        source = jnp.concatenate([jnp.zeros_like(operator), second[width:]], axis=0)
-        span = matmul(first, second[:width]) + source
-        carried = received if lead is None else matmul(received, lead)
-        base = jnp.eye(width, dtype=jnp.float32) if lead is None else lead
-        lead = jnp.where(after, carried[:width], base)
-        entering = jnp.where(after, entering + carried[width:], entering)
-        arrivals.append(entering)
-
-
-def join_body(position, spans, own, whole, reach, crossing):
-    members, _, width, _ = spans.shape
-    eye = (
+def identity(width):
+    return (
         lax.broadcasted_iota(jnp.int32, (width, width), 0)
         == lax.broadcasted_iota(jnp.int32, (width, width), 1)
     ).astype(jnp.float32)
+
+
+def join_body(position, spans, own, whole, reach, crossing):
+    members, _, width, _ = spans.shape
+    eye = identity(width)
     reach[0] = eye
     reach[1] = eye
     mine = position[0]
@@ -386,39 +351,48 @@
     )
 
 
-def first_body(high, low, forward, entering, middle_ends, turn, twist, solved, message):
-    rows, count, width = forward.shape
-
-    def step(i, carry):
+def first_body(high, low, source, entering, ahead_ends, behind_ends, solved, message, forward):
+    rows, count, width = source.shape
+
+    def ahead(i, state):
+        state = apply_split(state, high[i], low[i]) + source[i]
+        forward[i] = state
+        return state
+
+    lax.fori_loop(0, rows, ahead, entering[0], unroll=2)
+
+    def behind(i, carry):
         state, total = carry
         j = rows - 1 - i
         state = apply_split(forward[j] + state, high[j], low[j])
         solved[j] = state
         return state, total + state * state
 
-    start = entering[...]
     zero = jnp.zeros((count, width), jnp.float32)
-    _, total = lax.fori_loop(0, rows, step, (start, zero), unroll=2)
-    message[:count] = middle_ends[0] + apply_split(start, *split(turn[...]))
-    message[count : 2 * count] = middle_ends[1] + apply_split(start, *split(twist[...]))
+    _, total = lax.fori_loop(0, rows, behind, (entering[1], zero), unroll=2)
+    for place, ends in enumerate((ahead_ends, behind_ends)):
+        message[place * count : (place + 1) * count] = (
+            ends[2 * width :]
+            + apply_split(entering[0], *split(ends[:width]))
+            + apply_split(entering[1], *split(ends[width : 2 * width]))
+        )
     message[2 * count :] = jnp.zeros((8, width), jnp.float32)
     message[2 * count :, :count] = row_sums(total)
 
 
-def first_rows(high, low, forward, entering, middle_ends, turn, twist):
-    rows, count, width = forward.shape
+def first_rows(high, low, source, entering, ahead_ends, behind_ends):
+    rows, count, width = source.shape
     return call(
         first_body,
-        [shape(*forward.shape), shape(2 * count + 8, width)],
-        [],
-        rows * 6 * count * width * width,
+        [shape(*source.shape), shape(2 * count + 8, width)],
+        [pltpu.VMEM(source.shape, jnp.float32)],
+        2 * rows * 6 * count * width * width,
         high,
         low,
-        forward,
+        source,
         entering,
-        middle_ends,
-        turn,
-        twist,
+        ahead_ends,
+        behind_ends,
     )
 
 
@@ -479,28 +453,21 @@
     rows, count, width = start_vectors.shape
     cell_count = rows * lax.axis_size(CHAIN) * width
     whole = lax.all_gather(factors, "cols", axis=1, tiled=True)
-    high, low, forward, prefix, suffix = prepare(whole, start_vectors)
-    first_end, cross, turn, twist = couple(high, low, forward, prefix, suffix)
-    operators = jnp.stack([prefix[rows - 1], suffix[0], cross])
-    near_spans = lax.all_gather(operators, "inner")
+    high, low, suffix, cross, solved, operators, ends = prepare(whole, start_vectors)
     near_position = lax.axis_index("inner").astype(jnp.int32)[None]
     far_position = lax.axis_index("outer").astype(jnp.int32)[None]
-    zero = jnp.zeros((count, width), jnp.float32)
-
-    entering, early = scan_spans(prefix[rows - 1], forward[rows - 1], False)
-    end = first_end + matmul(entering, cross)
-    own, composed = join(near_position, near_spans, early[-1])
+    near_spans = lax.all_gather(operators, "inner")
+    near_ends = to_all(ends, "inner")
+    ahead_rows, ahead_ends = respond_ahead(high, low, cross, suffix, solved)
+    own, composed = join(near_position, near_spans, (ahead_ends, near_ends))
     far_spans = lax.all_gather(composed, "outer")
-    leaving, arrivals = scan_spans(suffix[0], end, True)
-    forward = sweep(high, low, start_vectors, entering, False, arrivals[0])
-    middle = sweep(high, low, forward, zero, True, arrivals[1])
-    middle = sweep(high, low, middle, zero, False, arrivals[2])
-    middle_ahead = middle[rows - 1]
-    middle_behind = sweep(high, low, middle, zero, True, arrivals[-2])[0]
-    entering = leaving
-
-    middle_ends = jnp.stack([middle_ahead, middle_behind])
-    first_solve, message = first_rows(high, low, forward, entering, middle_ends, turn, twist)
+    behind_ends = respond_behind(high, low, ahead_rows, (own,))
+
+    inner, message = near(near_position, near_spans, near_ends)
+    entering, _ = far(far_position, far_spans, to_all(message, "outer"), own, inner)
+    first_solve, message = first_rows(
+        high, low, start_vectors, entering, ahead_ends, behind_ends
+    )
     inner, message = near(near_position, near_spans, to_all(message, "inner"))
     entering, squares = far(far_position, far_spans, to_all(message, "outer"), own, inner)
     scale_one = jnp.sqrt(squares[0, :count] / cell_count + eps_value)

time: 392 us -> 347 us (0.89)
  starting transfers between devices: 50 us -> 11.5 us
  matrix products: 8.75 us -> 0 us
  Pallas kernels: 95.9 us -> 104 us
  other arithmetic: 5.68 us -> 1.22 us
  waiting for transfers between devices: 149 us -> 153 us
    ppermute x12 -> x0, waiting for transfers between devices: 82.2 us -> none  [exchange(): lax.ppermute(value, CHAIN, [(i, i ^ 1 << level) for i in range(size)])]
    ppermute x12 -> x0, starting transfers between devices: 49.9 us -> none  [exchange(): lax.ppermute(value, CHAIN, [(i, i ^ 1 << level) for i in range(size)])]
    all_gather x1, waiting for transfers between devices: 0.01 us -> 49 us  [shards(): far_spans = lax.all_gather(composed, 'outer')]
    all_gather x1, waiting for transfers between devices: 0.01 us -> 23.5 us  [shards(): near_spans = lax.all_gather(operators, 'inner')]
    all_to_all x0 -> x2, waiting for transfers between devices: none -> 13.3 us  [to_all(): return lax.all_to_all(copies, axis, 0, 0, tiled=True)]
    all_to_all x0 -> x2, starting transfers between devices: none -> 11.4 us  [to_all(): return lax.all_to_all(copies, axis, 0, 0, tiled=True)]
    dot_general x21 -> x0, matrix products: 8.75 us -> none  [matmul(): jnp.dot(left, right, precision=lax.Precision.HIGHEST, preferred_element_t...]
    pallas_call x12 -> x11, Pallas kernels: 95.9 us -> 104 us  [call(): pl.pallas_call(kernel, out_shape=tuple(out_shapes), in_specs=specs, out_s...]
  transfers between devices with their start and end apart: 15 -> 5, of which waited for: 13 -> 4; matrix products, arithmetic and copies ran while one was open for 4% -> 1% of each run, Pallas kernels for 9% -> 10%
where the time goes in v3:
time: 347 us; the launch traced here: 346 us
  waiting for transfers between devices  153 us (44%)
  Pallas kernels  104 us (30%)
  blocking collectives  55.4 us (16%)
  between operations  13.8 us (4%)
  starting transfers between devices  11.5 us (3%)
  local copies, waits for them, and re-layouts  7.4 us (2%)
    pallas_call x11, Pallas kernels, call(): pl.pallas_call(kernel, out_shape=tuple(out_shapes), in_specs=specs, out_s...  104 us
    all_gather x1, waiting for transfers between devices, shards(): whole = lax.all_gather(factors, 'cols', axis=1, tiled=True)  65.9 us
    all_to_all x4, blocking collectives, to_all(): return lax.all_to_all(copies, axis, 0, 0, tiled=True)  55.4 us
    all_gather x1, waiting for transfers between devices, shards(): far_spans = lax.all_gather(composed, 'outer')  49 us
    all_gather x1, waiting for transfers between devices, shards(): near_spans = lax.all_gather(operators, 'inner')  23.5 us
    all_to_all x2, waiting for transfers between devices, to_all(): return lax.all_to_all(copies, axis, 0, 0, tiled=True)  13.3 us
    all_to_all x2, starting transfers between devices, to_all(): return lax.all_to_all(copies, axis, 0, 0, tiled=True)  11.4 us
  transfers between devices with their start and end apart: 5, of which 4 were waited for; matrix products, arithmetic and copies ran while one was open for 1% of the time, Pallas kernels for 10%

profile of v3, /device:TPU:1, one launch (start us, length us, event | category | flops | bytes accessed | tf_op | source)
XLA Modules:
  0.0 345.8 jit_solution(14805903296048618205)
XLA Ops:
  7.2 0.7 all-gather.6.cloned.1.call-update
  7.9 0.0 all-gather.8.cloned.1.call-start
  7.9 65.9 %all-gather.6.cloned.1.call-done.factors = f32[16,256,256]{2,1,0:T(8,128)} async-done(((f32[16,32,256]{2,1,0:T(8,128)}), f32[16,256,256]{2,1,0:T(8,128)}) %all-gather.6.cloned.1.call-update) | async-done | bytes 4194320 | tf_op jit(solution)/shard_map/all_gather | solution.py:455
  73.9 20.1 %shard_map.41 = (bf16[16,256,256]{2,1,0:T(8,128)(2,1)}, bf16[16,256,256]{2,1,0:T(8,128)(2,1)}, f32[16,256,256]{2,1,0:T(8,128)}, f32[16,256,256]{2,1,0:T(8,128)},...) custom-call(f32[16,256,256]{2,1,0:T(8,128)} %all-gather.6.cloned.1.call-done.factors, ...), custom_call_target="tpu_custom_call" | custom-call | flops 5234491392 | bytes 18685952 | tf_op jit(solution)/shard_map/pallas_call | solution.py:49
  94.0 1.8 broadcast_in_dim.17
  95.8 4.9 %all-to-all-start = ((f32[8,72,256]{2,1,0:T(8,128)}), f32[8,72,256]{2,1,0:T(8,128)S(1)}, u32[]{:S(2)}, u32[]{:S(2)}) async-start(f32[8,72,256]{2,1,0:T(8,128)} %broadcast_in_dim.17), calls=%async_computation | async-start | bytes 1179648 | tf_op jit(solution)/shard_map/all_to_all | solution.py:449
  100.7 14.7 %shard_map.42 = (f32[16,544,256]{2,1,0:T(8,128)}, f32[544,256]{1,0:T(8,128)}) custom-call(bf16[16,256,256]{2,1,0:T(8,128)(2,1)} %get-tuple-element.24.high.refs_1_, bf16[16,256,256]{2,1,0:T(8,128)(2,1)} %get-tuple-element.25.low.refs_2_, f32[16,256,256]{2,1,0:T(8,128)} %get-tuple-element.26.cross, f32[16,256,256]{2,1,0:T(8,128)} %get-tuple-element.27.suffix, ...), custom_call_target="tpu_custom_call" | custom-call | flops 3422552064 | bytes 22577152 | tf_op jit(solution)/shard_map/pallas_call | solution.py:49
  115.4 23.5 %all-gather.8.cloned.1.call-done = f32[24,256,256]{2,1,0:T(8,128)} async-done(((f32[3,256,256]{2,1,0:T(8,128)}), f32[24,256,256]{2,1,0:T(8,128)}) %all-gather.8.cloned.1.call-update) | async-done | bytes 6291472 | tf_op jit(solution)/shard_map/all_gather | solution.py:459
  138.9 10.0 %shard_map.43 = (f32[3,256,256]{2,1,0:T(8,128)}, f32[3,256,256]{2,1,0:T(8,128)}) custom-call(f32[544,256]{1,0:T(8,128)} %get-tuple-element.29.refs_0_.ahead_ends, f32[8,72,256]{2,1,0:T(8,128)} %copy-done, s32[1]{0:T(128)} %bitcast.1.refs_2_.position, f32[8,3,256,256]{3,2,1,0:T(8,128)} %bitcast.10), custom_call_target="tpu_custom_call" | custom-call | flops 3221225472 | bytes 7864320 | tf_op jit(solution)/shard_map/pallas_call | solution.py:49
  148.9 6.8 %shard_map.44 = (f32[2,32,256]{2,1,0:T(8,128)}, f32[72,256]{1,0:T(8,128)}) custom-call(s32[1]{0:T(128)} %bitcast.1.refs_2_.position, f32[8,3,256,256]{3,2,1,0:T(8,128)} %bitcast.11, f32[8,72,256]{2,1,0:T(8,128)} %copy-done), custom_call_target="tpu_custom_call" | custom-call | flops 301989888 | bytes 7020544 | tf_op jit(solution)/shard_map/pallas_call | solution.py:49
  155.7 1.7 broadcast_in_dim.19
  157.5 6.5 %all-to-all-start.1 = ((f32[8,72,256]{2,1,0:T(8,128)}), f32[8,72,256]{2,1,0:T(8,128)S(1)}, u32[]{:S(2)}, u32[]{:S(2)}) async-start(f32[8,72,256]{2,1,0:T(8,128)} %broadcast_in_dim.19), calls=%async_computation.1 | async-start | bytes 1179648 | tf_op jit(solution)/shard_map/all_to_all | solution.py:449
  163.9 11.9 %shard_map.46.behind_ends = f32[544,256]{1,0:T(8,128)} custom-call(f32[3,256,256]{2,1,0:T(8,128)} %get-tuple-element.34.own.refs_0_, bf16[16,256,256]{2,1,0:T(8,128)(2,1)} %get-tuple-element.24.high.refs_1_, bf16[16,256,256]{2,1,0:T(8,128)(2,1)} %get-tuple-element.25.low.refs_2_, f32[16,544,256]{2,1,0:T(8,128)} %get-tuple-element.37.refs_3_), custom_call_target="tpu_custom_call" | custom-call | flops 3422552064 | bytes 13664256 | tf_op jit(solution)/shard_map/pallas_call | solution.py:49
  175.8 13.3 %all-to-all-done.1.ends = f32[8,72,256]{2,1,0:T(8,128)S(1)} async-done(((f32[8,72,256]{2,1,0:T(8,128)}), f32[8,72,256]{2,1,0:T(8,128)S(1)}, u32[]{:S(2)}, u32[]{:S(2)}) %all-to-all-start.1) | async-done | bytes 589856 | tf_op jit(solution)/shard_map/all_to_all | solution.py:449
  189.2 49.0 %all-gather.10.cloned.1.call-done = f32[24,256,256]{2,1,0:T(8,128)} async-done(((f32[3,256,256]{2,1,0:T(8,128)}), f32[24,256,256]{2,1,0:T(8,128)}) %all-gather.10.cloned.1.call-update) | async-done | bytes 6291472 | tf_op jit(solution)/shard_map/all_gather | solution.py:463
  238.2 6.9 %shard_map.45 = (f32[2,32,256]{2,1,0:T(8,128)}, f32[8,256]{1,0:T(8,128)}) custom-call(s32[1]{0:T(128)} %bitcast.position, f32[8,3,256,256]{3,2,1,0:T(8,128)} %bitcast.13, f32[8,72,256]{2,1,0:T(8,128)} %copy-done.1, f32[3,256,256]{2,1,0:T(8,128)} %get-tuple-element.34.own.refs_0_, f32[2,32,256]{2,1,0:T(8,128)} %get-tuple-element.35.inner), custom_call_target="tpu_custom_call" | custom-call | flops 301989888 | bytes 7806976 | tf_op jit(solution)/shard_map/pallas_call | solution.py:49
  245.2 9.2 %shard_map.47 = (f32[16,32,256]{2,1,0:T(8,128)}, f32[72,256]{1,0:T(8,128)}) custom-call(bf16[16,256,256]{2,1,0:T(8,128)(2,1)} %get-tuple-element.24.high.refs_1_, bf16[16,256,256]{2,1,0:T(8,128)(2,1)} %get-tuple-element.25.low.refs_2_, f32[16,32,256]{2,1,0:T(8,128)} %source.3, f32[2,32,256]{2,1,0:T(8,128)} %get-tuple-element.36.entering, ...), custom_call_target="tpu_custom_call" | custom-call | flops 402653184 | bytes 6496256 | tf_op jit(solution)/shard_map/pallas_call | solution.py:49
  254.3 0.9 broadcast_in_dim.20
  255.3 15.2 %all_to_all.30.ends = f32[8,72,256]{2,1,0:T(8,128)} all-to-all(f32[8,72,256]{2,1,0:T(8,128)S(1)} %broadcast_in_dim.20), channel_id=1, replica_groups=mesh['outer'=8,'inner'=8,'cols'=8] {'inner'}, dimensions={0} | all-to-all | bytes 1179648 | tf_op jit(solution)/shard_map/all_to_all | solution.py:449
  270.5 6.8 %shard_map.48 = (f32[2,32,256]{2,1,0:T(8,128)}, f32[72,256]{1,0:T(8,128)}) custom-call(s32[1]{0:T(128)} %bitcast.1.refs_2_.position, f32[8,3,256,256]{3,2,1,0:T(8,128)} %bitcast.12, f32[8,72,256]{2,1,0:T(8,128)} %all_to_all.30.ends), custom_call_target="tpu_custom_call" | custom-call | flops 301989888 | bytes 7020544 | tf_op jit(solution)/shard_map/pallas_call | solution.py:49
  277.3 0.9 broadcast_in_dim.21
  278.2 21.4 %all_to_all.31.ends = f32[8,72,256]{2,1,0:T(8,128)} all-to-all(f32[8,72,256]{2,1,0:T(8,128)S(1)} %broadcast_in_dim.21), channel_id=1, replica_groups=mesh['outer'=8,'inner'=8,'cols'=8] {'outer'}, dimensions={0} | all-to-all | bytes 1179648 | tf_op jit(solution)/shard_map/all_to_all | solution.py:449
  299.6 6.9 %shard_map.49 = (f32[2,32,256]{2,1,0:T(8,128)}, f32[8,256]{1,0:T(8,128)}) custom-call(s32[1]{0:T(128)} %bitcast.position, f32[8,3,256,256]{3,2,1,0:T(8,128)} %bitcast.14, f32[8,72,256]{2,1,0:T(8,128)} %all_to_all.31.ends, f32[3,256,256]{2,1,0:T(8,128)} %get-tuple-element.34.own.refs_0_, f32[2,32,256]{2,1,0:T(8,128)} %get-tuple-element.41.inner), custom_call_target="tpu_custom_call" | custom-call | flops 301989888 | bytes 7806976 | tf_op jit(solution)/shard_map/pallas_call | solution.py:49
  306.5 0.7 sqrt_bitcast_fusion.1
  307.2 0.7 copy.8.scale
  307.9 8.7 %shard_map.50 = (f32[16,32,256]{2,1,0:T(8,128)}, f32[8,128]{1,0:T(8,128)}) custom-call(bf16[16,256,256]{2,1,0:T(8,128)(2,1)} %get-tuple-element.24.high.refs_1_, bf16[16,256,256]{2,1,0:T(8,128)(2,1)} %get-tuple-element.25.low.refs_2_, f32[16,32,256]{2,1,0:T(8,128)} %get-tuple-element.38.source, f32[2,32,256]{2,1,0:T(8,128)} %get-tuple-element.42.entering, ...), custom_call_target="tpu_custom_call" | custom-call | flops 402653184 | bytes 5312640 | tf_op jit(solution)/shard_map/pallas_call | solution.py:49
  316.6 0.7 broadcast_in_dim.22
  317.3 9.6 %all_to_all.32 = f32[8,8,128]{2,1,0:T(8,128)S(1)} all-to-all(f32[8,8,128]{2,1,0:T(8,128)S(1)} %broadcast_in_dim.22), channel_id=1, replica_groups=mesh['outer'=8,'inner'=8,'cols'=8] {'inner'}, dimensions={0} | all-to-all | bytes 65536 | tf_op jit(solution)/shard_map/all_to_all | solution.py:449
  326.9 9.2 %all_to_all.33 = f32[8,8,128]{2,1,0:T(8,128)S(1)} all-to-all(f32[8,8,128]{2,1,0:T(8,128)S(1)} %broadcast_in_dim.23), channel_id=1, replica_groups=mesh['outer'=8,'inner'=8,'cols'=8] {'outer'}, dimensions={0} | all-to-all | bytes 65536 | tf_op jit(solution)/shard_map/all_to_all | solution.py:449
  336.2 0.5 multiply_bitcast_fusion
  336.7 0.7 copy.9.scale
  337.4 1.9 shard_map.51
  (12 shorter events, 0.1 us)
Async XLA Ops:
  7.2 66.7 %all-gather.6.cloned.1.call-start = ((), (), s32[]{:S(2)}) async-start(), calls=%async_computation.6 | async-start | bytes 4718592 | tf_op jit(solution)/shard_map/all_gather | solution.py:455
  7.9 131.0 %all-gather.8.cloned.1.call-start = ((), (), s32[]{:S(2)}) async-start(), calls=%async_computation.7 | async-start | bytes 7077888 | tf_op jit(solution)/shard_map/all_gather | solution.py:459
  95.8 19.6 %all-to-all-start = ((f32[8,72,256]{2,1,0:T(8,128)}), f32[8,72,256]{2,1,0:T(8,128)S(1)}, u32[]{:S(2)}, u32[]{:S(2)}) async-start(f32[8,72,256]{2,1,0:T(8,128)} %broadcast_in_dim.17), calls=%async_computation | async-start | bytes 1179648 | tf_op jit(solution)/shard_map/all_to_all | solution.py:449
  100.7 137.5 %all-gather.10.cloned.1.call-start = ((), (), s32[]{:S(2)}) async-start(), calls=%async_computation.8 | async-start | bytes 7077888 | tf_op jit(solution)/shard_map/all_gather | solution.py:463
  115.4 23.5 %copy-start = (f32[8,72,256]{2,1,0:T(8,128)}, f32[8,72,256]{2,1,0:T(8,128)S(1)}, u32[]{:S(2)}) copy-start(f32[8,72,256]{2,1,0:T(8,128)S(1)} %all-to-all-done.refs_1_.ends) | copy-start | bytes 1769476
  157.5 31.7 %all-to-all-start.1 = ((f32[8,72,256]{2,1,0:T(8,128)}), f32[8,72,256]{2,1,0:T(8,128)S(1)}, u32[]{:S(2)}, u32[]{:S(2)}) async-start(f32[8,72,256]{2,1,0:T(8,128)} %broadcast_in_dim.19), calls=%async_computation.1 | async-start | bytes 1179648 | tf_op jit(solution)/shard_map/all_to_all | solution.py:449
  189.2 49.0 %copy-start.1 = (f32[8,72,256]{2,1,0:T(8,128)}, f32[8,72,256]{2,1,0:T(8,128)S(1)}, u32[]{:S(2)}) copy-start(f32[8,72,256]{2,1,0:T(8,128)S(1)} %all-to-all-done.1.ends) | copy-start | bytes 1769476
Sparse Core Ops, SparseCore 0:
  10.1 63.7 all-gather.5
  94.2 44.7 all-gather.7
  149.0 89.1 all-gather.9

commit v4 on v3

--- a/solution.py
+++ b/solution.py
@@ -9,7 +9,8 @@
 
 eps_value = 1e-06
 VMEM_BYTES = 56 * 1024 * 1024
-CHAIN = ("outer", "inner")
+INNER = ("mid", "core")
+CHAIN = ("outer", *INNER)
 
 
 def split(value):
@@ -57,6 +58,17 @@
     )(*operands)
 
 
+def gate(value, after):
+    anywhere = pl.BlockSpec(memory_space=pl.ANY)
+    return pl.pallas_call(
+        lambda *refs: None,
+        out_shape=shape(*value.shape, dtype=value.dtype),
+        in_specs=[anywhere] * (1 + len(after)),
+        out_specs=anywhere,
+        input_output_aliases={0: 0},
+    )(value, *after)
+
+
 def shape(*dims, dtype=jnp.float32):
     return jax.ShapeDtypeStruct(dims, dtype)
 
@@ -91,7 +103,6 @@
     lax.fori_loop(0, rows, step, 0)
     operators[0] = ahead[count:]
     operators[1] = behind[...]
-    ends[:count] = ahead[:count]
     ahead[...] = jnp.zeros_like(ahead)
 
     def back(i, _):
@@ -105,11 +116,13 @@
 
     lax.fori_loop(0, rows, back, 0)
     operators[2] = ahead[count:]
-    ends[count : 2 * count] = ahead[:count]
-    ends[2 * count :] = jnp.zeros((8, width), jnp.float32)
-
-
-def prepare(factors, source):
+    for member in range(ends.shape[0]):
+        ends[member, :count] = forward[rows - 1]
+        ends[member, count : 2 * count] = ahead[:count]
+        ends[member, 2 * count :] = jnp.zeros((8, width), jnp.float32)
+
+
+def prepare(factors, source, copies):
     rows, width, _ = factors.shape
     count = source.shape[1]
     square = (rows, width, width)
@@ -122,7 +135,7 @@
             shape(*square),
             shape(*source.shape),
             shape(3, width, width),
-            shape(2 * count + 8, width),
+            shape(copies, 2 * count + 8, width),
         ],
         [
             pltpu.VMEM(square, jnp.float32),
@@ -199,12 +212,31 @@
     ).astype(jnp.float32)
 
 
-def join_body(position, spans, own, whole, reach, crossing):
-    members, _, width, _ = spans.shape
-    eye = identity(width)
-    reach[0] = eye
-    reach[1] = eye
-    mine = position[0]
+def row_span(place, own, other, e, part):
+    return jnp.where(e % 2 == place[1], own[e // 2, part], other[e // 2, part])
+
+
+def far_span(place, own, other, e, part):
+    first = place[1] == 0
+    return jnp.concatenate(
+        [
+            jnp.where(first, own[e, part], other[e, part]),
+            jnp.where(first, other[e, part], own[e, part]),
+        ],
+        axis=0,
+    )
+
+
+def join_body(place, spans, others, own, half, reach, crossing):
+    members = 2 * spans.shape[0]
+    width = spans.shape[2]
+    reach[0] = identity(width)
+    reach[1] = identity(width)
+    mine = place[0]
+    kept = pl.ds(pl.multiple_of(place[1] * (width // 2), width // 2), width // 2)
+
+    def span(e, part):
+        return split(row_span(place, spans, others, e, part))
 
     def outward(e, _):
         @pl.when(e == mine)
@@ -218,14 +250,14 @@
             own[1] = reach[1]
 
         ahead = reach[0]
-        crossing[e] = apply_split(ahead, *split(spans[e, 2]))
-        reach[1] = apply_split(reach[1], *split(spans[back, 1]))
-        reach[0] = apply_split(ahead, *split(spans[e, 0]))
+        crossing[e] = apply_split(ahead, *span(e, 2))
+        reach[1] = apply_split(reach[1], *span(back, 1))
+        reach[0] = apply_split(ahead, *span(e, 0))
         return 0
 
     lax.fori_loop(0, members, outward, 0)
-    whole[0] = reach[0]
-    whole[1] = reach[1]
+    half[0] = reach[0, kept]
+    half[1] = reach[1, kept]
     reach[0] = jnp.zeros((width, width), jnp.float32)
 
     def inward(i, _):
@@ -235,52 +267,47 @@
         def _():
             own[2] = reach[0]
 
-        reach[0] = apply_split(reach[0], *split(spans[e, 1])) + crossing[e]
+        reach[0] = apply_split(reach[0], *span(e, 1)) + crossing[e]
         return 0
 
     lax.fori_loop(0, members, inward, 0)
-    whole[2] = reach[0]
-
-
-def join(position, spans, after):
-    members, parts, width, _ = spans.shape
+    half[2] = reach[0, kept]
+
+
+def join(place, spans, others):
+    chips, parts, width, _ = spans.shape
     return call(
         join_body,
-        [shape(parts, width, width), shape(parts, width, width)],
-        [pltpu.VMEM((2, width, width), jnp.float32), pltpu.VMEM((members, width, width), jnp.float32)],
-        members * 6 * 4 * width**3,
+        [shape(parts, width, width), shape(parts, width // 2, width)],
+        [
+            pltpu.VMEM((2, width, width), jnp.float32),
+            pltpu.VMEM((2 * chips, width, width), jnp.float32),
+        ],
+        2 * chips * 6 * 4 * width**3,
         spans,
-        after=after,
-        position=position,
-    )
-
-
-def relay(mine, spans, ends, entered):
-    members, _, width, _ = spans.shape
-    count = (ends.shape[1] - 8) // 2
+        others,
+        position=place,
+    )
+
+
+def relay(span, ends, states):
+    members, length, width = ends.shape
+    count = (length - 8) // 2
     state = jnp.zeros((count, width), jnp.float32)
-    states = []
+    entered = []
     for e in range(members):
-        states.append(state)
-
-        @pl.when(mine == e)
-        def _(state=state):
-            entered[0] = state
-
+        entered.append(state)
+        states[0, e] = state
         end = ends[e, :count]
-        state = end if e == 0 else apply_split(state, *split(spans[e, 0])) + end
+        state = end if e == 0 else apply_split(state, *split(span(e, 0))) + end
     ahead = state
     state = jnp.zeros((count, width), jnp.float32)
     for e in reversed(range(members)):
-
-        @pl.when(mine == e)
-        def _(state=state):
-            entered[1] = state
-
+        states[1, e] = state
         end = ends[e, count : 2 * count]
         if e > 0:
-            end = end + apply_split(states[e], *split(spans[e, 2]))
-        state = end if e == members - 1 else apply_split(state, *split(spans[e, 1])) + end
+            end = end + apply_split(entered[e], *split(span(e, 2)))
+        state = end if e == members - 1 else apply_split(state, *split(span(e, 1))) + end
     return ahead, state
 
 
@@ -292,31 +319,34 @@
     return total
 
 
-def near_body(position, spans, ends, entered, whole):
+def near_body(place, spans, others, ends, entered, messages, states):
     count = entered.shape[1]
-    ahead, behind = relay(position[0], spans, ends, entered)
-    whole[:count] = ahead
-    whole[count : 2 * count] = behind
-    whole[2 * count :] = total_of(ends)
-
-
-def near(position, spans, ends):
+    ahead, behind = relay(functools.partial(row_span, place, spans, others), ends, states)
+    message = jnp.concatenate([ahead, behind, total_of(ends)], axis=0)
+    for member in range(messages.shape[0]):
+        messages[member] = message
+    entered[0] = states[0, place[0]]
+    entered[1] = states[1, place[0]]
+
+
+def near(place, spans, others, ends, copies):
     members, length, width = ends.shape
     count = (length - 8) // 2
     return call(
         near_body,
-        [shape(2, count, width), shape(length, width)],
-        [],
+        [shape(2, count, width), shape(copies, length, width)],
+        [pltpu.VMEM((2, members, count, width), jnp.float32)],
         members * 6 * 3 * count * width * width,
         spans,
+        others,
         ends,
-        position=position,
-    )
-
-
-def far_body(position, spans, ends, own, inner, entering, squares, entered):
-    relay(position[0], spans, ends, entered)
-    ahead, behind = entered[0], entered[1]
+        position=place,
+    )
+
+
+def far_body(place, spans, others, ends, own, inner, entering, squares, states):
+    relay(functools.partial(far_span, place, spans, others), ends, states)
+    ahead, behind = states[0, place[0]], states[1, place[0]]
     entering[0] = apply_split(ahead, *split(own[0])) + inner[0]
     entering[1] = (
         apply_split(behind, *split(own[1])) + apply_split(ahead, *split(own[2])) + inner[1]
@@ -324,19 +354,20 @@
     squares[...] = total_of(ends)
 
 
-def far(position, spans, ends, own, inner):
+def far(place, spans, others, ends, own, inner):
     members, length, width = ends.shape
     count = (length - 8) // 2
     return call(
         far_body,
         [shape(2, count, width), shape(8, width)],
-        [pltpu.VMEM((2, count, width), jnp.float32)],
+        [pltpu.VMEM((2, members, count, width), jnp.float32)],
         members * 6 * 3 * count * width * width,
         spans,
+        others,
         ends,
         own,
         inner,
-        position=position,
+        position=place,
     )
 
 
@@ -351,7 +382,7 @@
     )
 
 
-def first_body(high, low, source, entering, ahead_ends, behind_ends, solved, message, forward):
+def first_body(high, low, source, entering, ahead_ends, behind_ends, solved, messages, forward):
     rows, count, width = source.shape
 
     def ahead(i, state):
@@ -370,21 +401,25 @@
 
     zero = jnp.zeros((count, width), jnp.float32)
     _, total = lax.fori_loop(0, rows, behind, (entering[1], zero), unroll=2)
-    for place, ends in enumerate((ahead_ends, behind_ends)):
-        message[place * count : (place + 1) * count] = (
-            ends[2 * width :]
-            + apply_split(entering[0], *split(ends[:width]))
-            + apply_split(entering[1], *split(ends[width : 2 * width]))
-        )
-    message[2 * count :] = jnp.zeros((8, width), jnp.float32)
-    message[2 * count :, :count] = row_sums(total)
-
-
-def first_rows(high, low, source, entering, ahead_ends, behind_ends):
+    parts = [
+        ends[2 * width :]
+        + apply_split(entering[0], *split(ends[:width]))
+        + apply_split(entering[1], *split(ends[width : 2 * width]))
+        for ends in (ahead_ends, behind_ends)
+    ]
+    sums = row_sums(total)
+    for member in range(messages.shape[0]):
+        messages[member, :count] = parts[0]
+        messages[member, count : 2 * count] = parts[1]
+        messages[member, 2 * count :] = jnp.zeros((8, width), jnp.float32)
+        messages[member, 2 * count :, :count] = sums
+
+
+def first_rows(high, low, source, entering, ahead_ends, behind_ends, copies):
     rows, count, width = source.shape
     return call(
         first_body,
-        [shape(*source.shape), shape(2 * count + 8, width)],
+        [shape(*source.shape), shape(copies, 2 * count + 8, width)],
         [pltpu.VMEM(source.shape, jnp.float32)],
         2 * rows * 6 * count * width * width,
         high,
@@ -418,14 +453,16 @@
     zero = jnp.zeros((count, width), jnp.float32)
     _, total = lax.fori_loop(0, rows, behind, (entering[1], zero), unroll=2)
     squares[...] = jnp.zeros(squares.shape, jnp.float32)
-    squares[:, :count] = row_sums(total)
-
-
-def second_rows(high, low, source, entering, scale):
+    sums = row_sums(total)
+    for member in range(squares.shape[0]):
+        squares[member, :, :count] = sums
+
+
+def second_rows(high, low, source, entering, scale, copies):
     rows, count, width = source.shape
     return call(
         second_body,
-        [shape(*source.shape), shape(8, 128)],
+        [shape(*source.shape), shape(copies, 8, 128)],
         [pltpu.VMEM(source.shape, jnp.float32)],
         2 * rows * 6 * count * width * width,
         high,
@@ -444,44 +481,55 @@
     return call(scale_body, [shape(*vectors.shape)], [], vectors.size, vectors, scale)[0]
 
 
-def to_all(value, axis):
-    copies = jnp.broadcast_to(value[None], (lax.axis_size(axis), *value.shape))
-    return lax.all_to_all(copies, axis, 0, 0, tiled=True)
+def swap(value, axis):
+    return lax.all_to_all(value, axis, 0, 0, tiled=True)
 
 
 def shards(start_vectors, factors):
     rows, count, width = start_vectors.shape
     cell_count = rows * lax.axis_size(CHAIN) * width
+    members, groups = lax.axis_size(INNER), lax.axis_size("outer")
+    core = lax.axis_index("core")
+    near_place = jnp.stack([lax.axis_index(INNER), core]).astype(jnp.int32)
+    far_place = jnp.stack([lax.axis_index("outer"), core]).astype(jnp.int32)
+    cross_core = functools.partial(lax.ppermute, axis_name="core", perm=[(0, 1), (1, 0)])
+
     whole = lax.all_gather(factors, "cols", axis=1, tiled=True)
-    high, low, suffix, cross, solved, operators, ends = prepare(whole, start_vectors)
-    near_position = lax.axis_index("inner").astype(jnp.int32)[None]
-    far_position = lax.axis_index("outer").astype(jnp.int32)[None]
-    near_spans = lax.all_gather(operators, "inner")
-    near_ends = to_all(ends, "inner")
+    high, low, suffix, cross, solved, operators, ends = prepare(whole, start_vectors, members)
+    own_spans = lax.all_gather(operators, "mid")
+    near_ends = swap(ends, INNER)
     ahead_rows, ahead_ends = respond_ahead(high, low, cross, suffix, solved)
-    own, composed = join(near_position, near_spans, (ahead_ends, near_ends))
-    far_spans = lax.all_gather(composed, "outer")
+    own_spans = gate(own_spans, (near_ends, ahead_ends))
+    near_spans = (own_spans, cross_core(own_spans))
+    own, half = join(near_place, *near_spans)
+    own_halves = lax.all_gather(half, "outer")
     behind_ends = respond_behind(high, low, ahead_rows, (own,))
-
-    inner, message = near(near_position, near_spans, near_ends)
-    entering, _ = far(far_position, far_spans, to_all(message, "outer"), own, inner)
+    inner, message = near(near_place, *near_spans, near_ends, groups)
+    far_ends = swap(message, "outer")
+    own_halves = gate(own_halves, (far_ends, behind_ends))
+    far_spans = (own_halves, cross_core(own_halves))
+    entering, _ = far(far_place, *far_spans, far_ends, own, inner)
+
     first_solve, message = first_rows(
-        high, low, start_vectors, entering, ahead_ends, behind_ends
-    )
-    inner, message = near(near_position, near_spans, to_all(message, "inner"))
-    entering, squares = far(far_position, far_spans, to_all(message, "outer"), own, inner)
+        high, low, start_vectors, entering, ahead_ends, behind_ends, members
+    )
+    inner, message = near(near_place, *near_spans, swap(message, INNER), groups)
+    entering, squares = far(far_place, *far_spans, swap(message, "outer"), own, inner)
     scale_one = jnp.sqrt(squares[0, :count] / cell_count + eps_value)
-    second, squares = second_rows(high, low, first_solve, entering, scale_one[:, None])
-    squares = jnp.sum(to_all(squares, "inner"), axis=0)
-    squares = jnp.sum(to_all(squares, "outer"), axis=0)
+    second, squares = second_rows(
+        high, low, first_solve, entering, scale_one[:, None], members
+    )
+    squares = jnp.sum(swap(squares, INNER), axis=0)
+    squares = jnp.broadcast_to(squares[None], (groups, *squares.shape))
+    squares = jnp.sum(swap(squares, "outer"), axis=0)
     scale_two = jnp.sqrt(squares[0, :count] / cell_count + eps_value)
     return rescale(second, scale_two[:, None]), jnp.log(scale_two)
 
 
 def solution(mesh):
     size = mesh.shape["chain"]
-    inner = 1 << ((size - 1).bit_length() // 2)
-    devices = mesh.devices.reshape(size // inner, inner, mesh.shape["cols"])
+    outer = 1 << ((size - 1).bit_length() // 2)
+    devices = mesh.devices.reshape(outer, size // outer // 2, 2, mesh.shape["cols"])
     placed = P(CHAIN, "cols", None)
     return jax.shard_map(
         shards,

time: 347 us -> 330 us (0.951)
  waiting for transfers between devices: 153 us -> 134 us
  starting transfers between devices: 11.5 us -> 16.9 us
    all_gather x2, waiting for transfers between devices: 72.5 us -> 44.5 us  [the longest x1 23.5 us: shards(): own_spans = lax.all_gather(operators, 'mid')]
    ppermute x0 -> x2, waiting for transfers between devices: none -> 9.62 us  [the longest x1 4.82 us: shards(): far_spans = (own_halves, cross_core(own_halves))]
    broadcast_in_dim x6 -> x1, local copies, waits for them, and re-layouts: 6.01 us -> 0.01 us  [shards(): squares = jnp.broadcast_to(squares[None], (groups, *squares.shape))]
    ppermute x0 -> x2, starting transfers between devices: none -> 5.44 us  [the longest x1 2.87 us: shards(): far_spans = (own_halves, cross_core(own_halves))]
  transfers between devices with their start and end apart: 5 -> 7, of which waited for: 4 -> 6; matrix products, arithmetic and copies ran while one was open for 1% -> 0% of each run, Pallas kernels for 10% -> 10%
where the time goes in v4:
time: 330 us
  waiting for transfers between devices  134 us (41%)
  Pallas kernels  101 us (31%)
  blocking collectives  56.3 us (17%)
  starting transfers between devices  16.9 us (5%)
  between operations  13.8 us (4%)
  local copies, waits for them, and re-layouts  4.65 us (1%)
    pallas_call x11, Pallas kernels, call(): pl.pallas_call(kernel, out_shape=tuple(out_shapes), in_specs=specs, out_s...  101 us
    all_gather x1, waiting for transfers between devices, shards(): whole = lax.all_gather(factors, 'cols', axis=1, tiled=True)  65.9 us
    all_to_all x4, blocking collectives, swap(): return lax.all_to_all(value, axis, 0, 0, tiled=True)  56.3 us
    all_gather x1, waiting for transfers between devices, shards(): own_spans = lax.all_gather(operators, 'mid')  23.5 us
    all_gather x1, waiting for transfers between devices, shards(): own_halves = lax.all_gather(half, 'outer')  20.9 us
    all_to_all x2, waiting for transfers between devices, swap(): return lax.all_to_all(value, axis, 0, 0, tiled=True)  13.2 us
    all_to_all x2, starting transfers between devices, swap(): return lax.all_to_all(value, axis, 0, 0, tiled=True)  11.4 us
  transfers between devices with their start and end apart: 7, of which 6 were waited for; matrix products, arithmetic and copies ran while one was open for 0% of the time, Pallas kernels for 10%

profile of v4, /device:TPU:1, one launch (start us, length us, event | category | flops | bytes accessed | tf_op | source)
XLA Modules:
  0.0 329.5 jit_solution(15169614659061094908)
XLA Ops:
  7.2 0.7 all-gather.6.cloned.1.call-update
  7.9 65.9 %all-gather.6.cloned.1.call-done.factors = f32[16,256,256]{2,1,0:T(8,128)} async-done(((f32[16,32,256]{2,1,0:T(8,128)}), f32[16,256,256]{2,1,0:T(8,128)}) %all-gather.6.cloned.1.call-update) | async-done | bytes 4194320 | tf_op jit(solution)/shard_map/all_gather | solution.py:497
  73.9 20.4 %shard_map.41 = (bf16[16,256,256]{2,1,0:T(8,128)(2,1)}, bf16[16,256,256]{2,1,0:T(8,128)(2,1)}, f32[16,256,256]{2,1,0:T(8,128)}, f32[16,256,256]{2,1,0:T(8,128)},...) custom-call(f32[16,256,256]{2,1,0:T(8,128)} %all-gather.6.cloned.1.call-done.factors, ...), custom_call_target="tpu_custom_call" | custom-call | flops 5234491392 | bytes 19202048 | tf_op jit(solution)/shard_map/pallas_call | solution.py:50
  94.3 4.9 %all-to-all-start = ((f32[8,72,256]{2,1,0:T(8,128)}), f32[8,72,256]{2,1,0:T(8,128)S(1)}, u32[]{:S(2)}, u32[]{:S(2)}) async-start(f32[8,72,256]{2,1,0:T(8,128)} %get-tuple-element.27), calls=%async_computation | async-start | bytes 1179648 | tf_op jit(solution)/shard_map/all_to_all | solution.py:485
  99.2 14.6 %shard_map.42 = (f32[16,544,256]{2,1,0:T(8,128)}, f32[544,256]{1,0:T(8,128)}) custom-call(bf16[16,256,256]{2,1,0:T(8,128)(2,1)} %get-tuple-element.24.high.refs_1_, bf16[16,256,256]{2,1,0:T(8,128)(2,1)} %get-tuple-element.25.low.refs_2_, f32[16,256,256]{2,1,0:T(8,128)} %get-tuple-element.28.cross, f32[16,256,256]{2,1,0:T(8,128)} %get-tuple-element.29.suffix, ...), custom_call_target="tpu_custom_call" | custom-call | flops 3422552064 | bytes 22577152 | tf_op jit(solution)/shard_map/pallas_call | solution.py:50
  113.8 23.5 %all-gather.8.cloned.1.call-done = f32[12,256,256]{2,1,0:T(8,128)} async-done(((f32[3,256,256]{2,1,0:T(8,128)}), f32[12,256,256]{2,1,0:T(8,128)}) %all-gather.8.cloned.1.call-update) | async-done | bytes 3145744 | tf_op jit(solution)/shard_map/all_gather | solution.py:499
  137.4 2.6 collective-permute-start
  140.0 0.7 pad_add_fusion.1.place
  140.6 4.8 %collective-permute-done.others = f32[4,3,256,256]{3,2,1,0:T(8,128)S(1)} collective-permute-done((f32[4,3,256,256]{3,2,1,0:T(8,128)}, f32[4,3,256,256]{3,2,1,0:T(8,128)S(1)}, u32[]{:S(2)}, u32[]{:S(2)}) %collective-permute-start) | collective-permute-done | bytes 3145760 | tf_op jit(solution)/shard_map/ppermute | solution.py:503
  145.4 1.6 copy-done
  147.0 9.9 %shard_map.44 = (f32[3,256,256]{2,1,0:T(8,128)}, f32[3,128,256]{2,1,0:T(8,128)}) custom-call(s32[2]{0:T(128)} %pad_add_fusion.1.place, f32[4,3,256,256]{3,2,1,0:T(8,128)} %shard_map.43.spans, f32[4,3,256,256]{3,2,1,0:T(8,128)} %copy-done), custom_call_target="tpu_custom_call" | custom-call | flops 3221225472 | bytes 7471104 | tf_op jit(solution)/shard_map/pallas_call | solution.py:50
  157.0 6.0 %shard_map.45 = (f32[2,32,256]{2,1,0:T(8,128)}, f32[8,72,256]{2,1,0:T(8,128)}) custom-call(s32[2]{0:T(128)} %pad_add_fusion.1.place, f32[4,3,256,256]{3,2,1,0:T(8,128)} %shard_map.43.spans, f32[4,3,256,256]{3,2,1,0:T(8,128)} %copy-done, f32[8,72,256]{2,1,0:T(8,128)} %copy-done.2), custom_call_target="tpu_custom_call" | custom-call | flops 301989888 | bytes 7536640 | tf_op jit(solution)/shard_map/pallas_call | solution.py:50
  163.0 6.5 %all-to-all-start.1 = ((f32[8,72,256]{2,1,0:T(8,128)}), f32[8,72,256]{2,1,0:T(8,128)S(1)}, u32[]{:S(2)}, u32[]{:S(2)}) async-start(f32[8,72,256]{2,1,0:T(8,128)} %get-tuple-element.33), calls=%async_computation.1 | async-start | bytes 1179648 | tf_op jit(solution)/shard_map/all_to_all | solution.py:485
  169.5 12.2 %shard_map.46.refs_2_.behind_ends = f32[544,256]{1,0:T(8,128)} custom-call(f32[3,256,256]{2,1,0:T(8,128)} %get-tuple-element.34.refs_0_.own, bf16[16,256,256]{2,1,0:T(8,128)(2,1)} %get-tuple-element.24.high.refs_1_, bf16[16,256,256]{2,1,0:T(8,128)(2,1)} %get-tuple-element.25.low.refs_2_, f32[16,544,256]{2,1,0:T(8,128)} %get-tuple-element.35.refs_3_), custom_call_target="tpu_custom_call" | custom-call | flops 3422552064 | bytes 13664256 | tf_op jit(solution)/shard_map/pallas_call | solution.py:50
  181.7 13.2 %all-to-all-done.1.refs_1_.ends = f32[8,72,256]{2,1,0:T(8,128)S(1)} async-done(((f32[8,72,256]{2,1,0:T(8,128)}), f32[8,72,256]{2,1,0:T(8,128)S(1)}, u32[]{:S(2)}, u32[]{:S(2)}) %all-to-all-start.1) | async-done | bytes 589856 | tf_op jit(solution)/shard_map/all_to_all | solution.py:485
  194.9 20.9 %all-gather.10.cloned.1.call-done = f32[24,128,256]{2,1,0:T(8,128)} async-done(((f32[3,128,256]{2,1,0:T(8,128)}), f32[24,128,256]{2,1,0:T(8,128)}) %all-gather.10.cloned.1.call-update) | async-done | bytes 3145744 | tf_op jit(solution)/shard_map/all_gather | solution.py:505
  215.8 2.9 collective-permute-start.1
  219.3 4.8 %collective-permute-done.1.others = f32[8,3,128,256]{3,2,1,0:T(8,128)S(1)} collective-permute-done((f32[8,3,128,256]{3,2,1,0:T(8,128)}, f32[8,3,128,256]{3,2,1,0:T(8,128)S(1)}, u32[]{:S(2)}, u32[]{:S(2)}) %collective-permute-start.1) | collective-permute-done | bytes 3145760 | tf_op jit(solution)/shard_map/ppermute | solution.py:510
  224.2 1.6 copy-done.1
  225.8 6.1 %shard_map.48 = (f32[2,32,256]{2,1,0:T(8,128)}, f32[8,256]{1,0:T(8,128)}) custom-call(s32[2]{0:T(128)} %pad_add_fusion.place, f32[8,3,128,256]{3,2,1,0:T(8,128)} %shard_map.47.spans, f32[8,3,128,256]{3,2,1,0:T(8,128)} %copy-done.1, f32[8,72,256]{2,1,0:T(8,128)} %copy-done.3, f32[3,256,256]{2,1,0:T(8,128)} %get-tuple-element.34.refs_0_.own, ...), custom_call_target="tpu_custom_call" | custom-call | flops 301989888 | bytes 7806976 | tf_op jit(solution)/shard_map/pallas_call | solution.py:50
  231.9 9.4 %shard_map.49 = (f32[16,32,256]{2,1,0:T(8,128)}, f32[8,72,256]{2,1,0:T(8,128)}) custom-call(bf16[16,256,256]{2,1,0:T(8,128)(2,1)} %get-tuple-element.24.high.refs_1_, bf16[16,256,256]{2,1,0:T(8,128)(2,1)} %get-tuple-element.25.low.refs_2_, f32[16,32,256]{2,1,0:T(8,128)} %source.3, f32[2,32,256]{2,1,0:T(8,128)} %get-tuple-element.37.entering, ...), custom_call_target="tpu_custom_call" | custom-call | flops 402653184 | bytes 7012352 | tf_op jit(solution)/shard_map/pallas_call | solution.py:50
  241.3 14.9 %all_to_all.30.ends = f32[8,72,256]{2,1,0:T(8,128)} all-to-all(f32[8,72,256]{2,1,0:T(8,128)} %get-tuple-element.39), channel_id=1, replica_groups=mesh['outer'=8,'mid'=4,'core'=2,'cols'=8] {'mid','core'}, dimensions={0} | all-to-all | bytes 1179648 | tf_op jit(solution)/shard_map/all_to_all | solution.py:485
  256.2 6.0 %shard_map.50 = (f32[2,32,256]{2,1,0:T(8,128)}, f32[8,72,256]{2,1,0:T(8,128)}) custom-call(s32[2]{0:T(128)} %pad_add_fusion.1.place, f32[4,3,256,256]{3,2,1,0:T(8,128)} %shard_map.43.spans, f32[4,3,256,256]{3,2,1,0:T(8,128)} %copy-done, f32[8,72,256]{2,1,0:T(8,128)} %all_to_all.30.ends), custom_call_target="tpu_custom_call" | custom-call | flops 301989888 | bytes 7536640 | tf_op jit(solution)/shard_map/pallas_call | solution.py:50
  262.2 21.6 %all_to_all.31.ends = f32[8,72,256]{2,1,0:T(8,128)} all-to-all(f32[8,72,256]{2,1,0:T(8,128)} %get-tuple-element.40), channel_id=1, replica_groups=mesh['outer'=8,'mid'=4,'core'=2,'cols'=8] {'outer'}, dimensions={0} | all-to-all | bytes 1179648 | tf_op jit(solution)/shard_map/all_to_all | solution.py:485
  283.9 6.1 %shard_map.51 = (f32[2,32,256]{2,1,0:T(8,128)}, f32[8,256]{1,0:T(8,128)}) custom-call(s32[2]{0:T(128)} %pad_add_fusion.place, f32[8,3,128,256]{3,2,1,0:T(8,128)} %shard_map.47.spans, f32[8,3,128,256]{3,2,1,0:T(8,128)} %copy-done.1, f32[8,72,256]{2,1,0:T(8,128)} %all_to_all.31.ends, f32[3,256,256]{2,1,0:T(8,128)} %get-tuple-element.34.refs_0_.own, ...), custom_call_target="tpu_custom_call" | custom-call | flops 301989888 | bytes 7806976 | tf_op jit(solution)/shard_map/pallas_call | solution.py:50
  290.0 0.7 sqrt_bitcast_fusion.1
  290.6 0.7 copy.10.scale
  291.3 8.7 %shard_map.52 = (f32[16,32,256]{2,1,0:T(8,128)}, f32[8,8,128]{2,1,0:T(8,128)}) custom-call(bf16[16,256,256]{2,1,0:T(8,128)(2,1)} %get-tuple-element.24.high.refs_1_, bf16[16,256,256]{2,1,0:T(8,128)(2,1)} %get-tuple-element.25.low.refs_2_, f32[16,32,256]{2,1,0:T(8,128)} %get-tuple-element.38.source, f32[2,32,256]{2,1,0:T(8,128)} %get-tuple-element.42.entering, ...), custom_call_target="tpu_custom_call" | custom-call | flops 402653184 | bytes 5341312 | tf_op jit(solution)/shard_map/pallas_call | solution.py:50
  300.1 10.5 %all_to_all.32 = f32[8,8,128]{2,1,0:T(8,128)S(1)} all-to-all(f32[8,8,128]{2,1,0:T(8,128)} %get-tuple-element.45), channel_id=1, replica_groups=mesh['outer'=8,'mid'=4,'core'=2,'cols'=8] {'mid','core'}, dimensions={0} | all-to-all | bytes 65536 | tf_op jit(solution)/shard_map/all_to_all | solution.py:485
  310.6 9.2 %all_to_all.33 = f32[8,8,128]{2,1,0:T(8,128)S(1)} all-to-all(f32[8,8,128]{2,1,0:T(8,128)S(1)} %broadcast_in_dim.2), channel_id=1, replica_groups=mesh['outer'=8,'mid'=4,'core'=2,'cols'=8] {'outer'}, dimensions={0} | all-to-all | bytes 65536 | tf_op jit(solution)/shard_map/all_to_all | solution.py:485
  320.4 0.7 copy.11.scale
  321.1 1.9 shard_map.53
  (19 shorter events, 1.3 us)
Async XLA Ops:
  7.2 66.7 %all-gather.6.cloned.1.call-start = ((), (), s32[]{:S(2)}) async-start(), calls=%async_computation.6 | async-start | bytes 4718592 | tf_op jit(solution)/shard_map/all_gather | solution.py:497
  7.9 129.5 %all-gather.8.cloned.1.call-start = ((), (), s32[]{:S(2)}) async-start(), calls=%async_computation.7 | async-start | bytes 3932160 | tf_op jit(solution)/shard_map/all_gather | solution.py:499
  94.3 19.6 %all-to-all-start = ((f32[8,72,256]{2,1,0:T(8,128)}), f32[8,72,256]{2,1,0:T(8,128)S(1)}, u32[]{:S(2)}, u32[]{:S(2)}) async-start(f32[8,72,256]{2,1,0:T(8,128)} %get-tuple-element.27), calls=%async_computation | async-start | bytes 1179648 | tf_op jit(solution)/shard_map/all_to_all | solution.py:485
  99.2 116.6 %all-gather.10.cloned.1.call-start = ((), (), s32[]{:S(2)}) async-start(), calls=%async_computation.8 | async-start | bytes 3538944 | tf_op jit(solution)/shard_map/all_gather | solution.py:505
  113.8 23.5 %copy-start.2 = (f32[8,72,256]{2,1,0:T(8,128)}, f32[8,72,256]{2,1,0:T(8,128)S(1)}, u32[]{:S(2)}) copy-start(f32[8,72,256]{2,1,0:T(8,128)S(1)} %all-to-all-done.refs_1_.ends) | copy-start | bytes 1769476
  137.4 8.1 %collective-permute-start = (f32[4,3,256,256]{3,2,1,0:T(8,128)}, f32[4,3,256,256]{3,2,1,0:T(8,128)S(1)}, u32[]{:S(2)}, u32[]{:S(2)}) collective-permute-start(f32[4,3,256,256]{3,2,1,0:T(8,128)} %shard_map.43.spans), channel_id=1, source_target_pairs={{0,8},{8,0},{1,9},{9,1},{2,10},{10,2},{3,11},{11,3},{4,12},{12,4},... | collective-permute-start | bytes 9437192 | tf_op jit(solution)/shard_map/ppermute | solution.py:503
  145.4 1.6 copy-start
  163.0 31.8 %all-to-all-start.1 = ((f32[8,72,256]{2,1,0:T(8,128)}), f32[8,72,256]{2,1,0:T(8,128)S(1)}, u32[]{:S(2)}, u32[]{:S(2)}) async-start(f32[8,72,256]{2,1,0:T(8,128)} %get-tuple-element.33), calls=%async_computation.1 | async-start | bytes 1179648 | tf_op jit(solution)/shard_map/all_to_all | solution.py:485
  194.9 21.0 %copy-start.3 = (f32[8,72,256]{2,1,0:T(8,128)}, f32[8,72,256]{2,1,0:T(8,128)S(1)}, u32[]{:S(2)}) copy-start(f32[8,72,256]{2,1,0:T(8,128)S(1)} %all-to-all-done.1.refs_1_.ends) | copy-start | bytes 1769476
  215.8 8.4 %collective-permute-start.1 = (f32[8,3,128,256]{3,2,1,0:T(8,128)}, f32[8,3,128,256]{3,2,1,0:T(8,128)S(1)}, u32[]{:S(2)}, u32[]{:S(2)}) collective-permute-start(f32[8,3,128,256]{3,2,1,0:T(8,128)} %shard_map.47.spans), channel_id=1, source_target_pairs={{0,8},{8,0},{1,9},{9,1},{2,10},{10,2},{3,11},{11,3},{4,12},{12,4},... | collective-permute-start | bytes 9437192 | tf_op jit(solution)/shard_map/ppermute | solution.py:510
  224.2 1.6 copy-start.1
Sparse Core Ops, SparseCore 0:
  10.1 63.7 all-gather.5
  94.4 42.9 all-gather.7
  157.1 58.6 all-gather.9

commit v5 on v4

--- a/solution.py
+++ b/solution.py
@@ -116,10 +116,7 @@
 
     lax.fori_loop(0, rows, back, 0)
     operators[2] = ahead[count:]
-    for member in range(ends.shape[0]):
-        ends[member, :count] = forward[rows - 1]
-        ends[member, count : 2 * count] = ahead[:count]
-        ends[member, 2 * count :] = jnp.zeros((8, width), jnp.float32)
+    put_messages(ends, forward[rows - 1], ahead[:count], None)
 
 
 def prepare(factors, source, copies):
@@ -135,7 +132,7 @@
             shape(*square),
             shape(*source.shape),
             shape(3, width, width),
-            shape(copies, 2 * count + 8, width),
+            shape(copies, count + 8, width),
         ],
         [
             pltpu.VMEM(square, jnp.float32),
@@ -212,8 +209,8 @@
     ).astype(jnp.float32)
 
 
-def row_span(place, own, other, e, part):
-    return jnp.where(e % 2 == place[1], own[e // 2, part], other[e // 2, part])
+def row_span(spans, e, part):
+    return spans[e, part]
 
 
 def far_span(place, own, other, e, part):
@@ -227,32 +224,28 @@
     )
 
 
-def join_body(place, spans, others, own, half, reach, crossing):
-    members = 2 * spans.shape[0]
-    width = spans.shape[2]
+def join_body(place, spans, own, half, reach, crossing):
+    members, _, width, _ = spans.shape
     reach[0] = identity(width)
     reach[1] = identity(width)
-    mine = place[0]
+    chip = place[0]
     kept = pl.ds(pl.multiple_of(place[1] * (width // 2), width // 2), width // 2)
 
-    def span(e, part):
-        return split(row_span(place, spans, others, e, part))
-
     def outward(e, _):
-        @pl.when(e == mine)
+        @pl.when(e // 2 == chip)
         def _():
-            own[0] = reach[0]
+            own[e % 2, 0] = reach[0]
 
         back = members - 1 - e
 
-        @pl.when(back == mine)
+        @pl.when(back // 2 == chip)
         def _():
-            own[1] = reach[1]
+            own[back % 2, 1] = reach[1]
 
         ahead = reach[0]
-        crossing[e] = apply_split(ahead, *span(e, 2))
-        reach[1] = apply_split(reach[1], *span(back, 1))
-        reach[0] = apply_split(ahead, *span(e, 0))
+        crossing[e] = apply_split(ahead, *split(spans[e, 2]))
+        reach[1] = apply_split(reach[1], *split(spans[back, 1]))
+        reach[0] = apply_split(ahead, *split(spans[e, 0]))
         return 0
 
     lax.fori_loop(0, members, outward, 0)
@@ -263,29 +256,29 @@
     def inward(i, _):
         e = members - 1 - i
 
-        @pl.when(e == mine)
+        @pl.when(e // 2 == chip)
         def _():
-            own[2] = reach[0]
-
-        reach[0] = apply_split(reach[0], *span(e, 1)) + crossing[e]
+            own[e % 2, 2] = reach[0]
+
+        reach[0] = apply_split(reach[0], *split(spans[e, 1])) + crossing[e]
         return 0
 
     lax.fori_loop(0, members, inward, 0)
     half[2] = reach[0, kept]
 
 
-def join(place, spans, others):
-    chips, parts, width, _ = spans.shape
+def join(place, spans, after):
+    members, parts, width, _ = spans.shape
     return call(
         join_body,
-        [shape(parts, width, width), shape(parts, width // 2, width)],
+        [shape(2, parts, width, width), shape(parts, width // 2, width)],
         [
             pltpu.VMEM((2, width, width), jnp.float32),
-            pltpu.VMEM((2 * chips, width, width), jnp.float32),
+            pltpu.VMEM((members, width, width), jnp.float32),
         ],
-        2 * chips * 6 * 4 * width**3,
+        members * 6 * 4 * width**3,
         spans,
-        others,
+        after=after,
         position=place,
     )
 
@@ -319,38 +312,43 @@
     return total
 
 
-def near_body(place, spans, others, ends, entered, messages, states):
-    count = entered.shape[1]
-    ahead, behind = relay(functools.partial(row_span, place, spans, others), ends, states)
+def near_body(place, spans, ends, entered, messages, states):
+    count = entered.shape[2]
+    ahead, behind = relay(functools.partial(row_span, spans), ends, states)
     message = jnp.concatenate([ahead, behind, total_of(ends)], axis=0)
     for member in range(messages.shape[0]):
         messages[member] = message
-    entered[0] = states[0, place[0]]
-    entered[1] = states[1, place[0]]
-
-
-def near(place, spans, others, ends, copies):
+    for core in range(2):
+        for way in range(2):
+            entered[core, way] = states[way, 2 * place[0] + core]
+
+
+def near(place, spans, ends, copies):
     members, length, width = ends.shape
     count = (length - 8) // 2
     return call(
         near_body,
-        [shape(2, count, width), shape(copies, length, width)],
+        [shape(2, 2, count, width), shape(copies, length, width)],
         [pltpu.VMEM((2, members, count, width), jnp.float32)],
         members * 6 * 3 * count * width * width,
         spans,
-        others,
         ends,
         position=place,
     )
 
 
-def far_body(place, spans, others, ends, own, inner, entering, squares, states):
+def far_body(place, spans, others, ends, own, inner, mine, theirs, squares, states, entering):
     relay(functools.partial(far_span, place, spans, others), ends, states)
     ahead, behind = states[0, place[0]], states[1, place[0]]
-    entering[0] = apply_split(ahead, *split(own[0])) + inner[0]
-    entering[1] = (
-        apply_split(behind, *split(own[1])) + apply_split(ahead, *split(own[2])) + inner[1]
-    )
+    for core in range(2):
+        entering[core, 0] = apply_split(ahead, *split(own[core, 0])) + inner[core, 0]
+        entering[core, 1] = (
+            apply_split(behind, *split(own[core, 1]))
+            + apply_split(ahead, *split(own[core, 2]))
+            + inner[core, 1]
+        )
+    mine[...] = entering[place[1]]
+    theirs[...] = entering[1 - place[1]]
     squares[...] = total_of(ends)
 
 
@@ -359,8 +357,11 @@
     count = (length - 8) // 2
     return call(
         far_body,
-        [shape(2, count, width), shape(8, width)],
-        [pltpu.VMEM((2, members, count, width), jnp.float32)],
+        [shape(2, count, width), shape(2, count, width), shape(8, width)],
+        [
+            pltpu.VMEM((2, members, count, width), jnp.float32),
+            pltpu.VMEM((2, 2, count, width), jnp.float32),
+        ],
         members * 6 * 3 * count * width * width,
         spans,
         others,
@@ -369,6 +370,28 @@
         inner,
         position=place,
     )
+
+
+def both_halves(place, mine, theirs, way):
+    first = place[1] == 0
+    return jnp.concatenate(
+        [
+            jnp.where(first, mine[way], theirs[way]),
+            jnp.where(first, theirs[way], mine[way]),
+        ],
+        axis=0,
+    )
+
+
+def put_messages(messages, ahead, behind, sums):
+    count = ahead.shape[0] // 2
+    for member in range(messages.shape[0]):
+        chosen = slice((member % 2) * count, (member % 2 + 1) * count)
+        messages[member, :count] = ahead[chosen]
+        messages[member, count : 2 * count] = behind[chosen]
+        messages[member, 2 * count :] = jnp.zeros((8, messages.shape[2]), jnp.float32)
+        if sums is not None:
+            messages[member, 2 * count :, : 2 * count] = sums
 
 
 def row_sums(total):
@@ -382,8 +405,9 @@
     )
 
 
-def first_body(high, low, source, entering, ahead_ends, behind_ends, solved, messages, forward):
+def first_body(place, high, low, source, mine, theirs, ahead_ends, behind_ends, solved, messages, forward):
     rows, count, width = source.shape
+    entering = [both_halves(place, mine, theirs, way) for way in range(2)]
 
     def ahead(i, state):
         state = apply_split(state, high[i], low[i]) + source[i]
@@ -407,33 +431,31 @@
         + apply_split(entering[1], *split(ends[width : 2 * width]))
         for ends in (ahead_ends, behind_ends)
     ]
-    sums = row_sums(total)
-    for member in range(messages.shape[0]):
-        messages[member, :count] = parts[0]
-        messages[member, count : 2 * count] = parts[1]
-        messages[member, 2 * count :] = jnp.zeros((8, width), jnp.float32)
-        messages[member, 2 * count :, :count] = sums
-
-
-def first_rows(high, low, source, entering, ahead_ends, behind_ends, copies):
+    put_messages(messages, *parts, row_sums(total))
+
+
+def first_rows(place, high, low, source, mine, theirs, ahead_ends, behind_ends, copies):
     rows, count, width = source.shape
     return call(
         first_body,
-        [shape(*source.shape), shape(copies, 2 * count + 8, width)],
+        [shape(*source.shape), shape(copies, count + 8, width)],
         [pltpu.VMEM(source.shape, jnp.float32)],
         2 * rows * 6 * count * width * width,
         high,
         low,
         source,
-        entering,
+        mine,
+        theirs,
         ahead_ends,
         behind_ends,
-    )
-
-
-def second_body(high, low, source, entering, scale, result, squares, forward):
+        position=place,
+    )
+
+
+def second_body(place, high, low, source, mine, theirs, scale, result, squares, forward):
     rows, count, width = source.shape
     inverse = 1.0 / scale[...]
+    entering = [both_halves(place, mine, theirs, way) for way in range(2)]
 
     def ahead(i, state):
         state = apply_split(state, high[i], low[i]) + source[i]
@@ -458,7 +480,7 @@
         squares[member, :, :count] = sums
 
 
-def second_rows(high, low, source, entering, scale, copies):
+def second_rows(place, high, low, source, mine, theirs, scale, copies):
     rows, count, width = source.shape
     return call(
         second_body,
@@ -468,8 +490,10 @@
         high,
         low,
         source,
-        entering,
+        mine,
+        theirs,
         scale,
+        position=place,
     )
 
 
@@ -490,34 +514,40 @@
     cell_count = rows * lax.axis_size(CHAIN) * width
     members, groups = lax.axis_size(INNER), lax.axis_size("outer")
     core = lax.axis_index("core")
-    near_place = jnp.stack([lax.axis_index(INNER), core]).astype(jnp.int32)
+    near_place = jnp.stack([lax.axis_index("mid"), core]).astype(jnp.int32)
     far_place = jnp.stack([lax.axis_index("outer"), core]).astype(jnp.int32)
     cross_core = functools.partial(lax.ppermute, axis_name="core", perm=[(0, 1), (1, 0)])
 
     whole = lax.all_gather(factors, "cols", axis=1, tiled=True)
     high, low, suffix, cross, solved, operators, ends = prepare(whole, start_vectors, members)
-    own_spans = lax.all_gather(operators, "mid")
+    near_spans = lax.all_gather(operators, INNER)
     near_ends = swap(ends, INNER)
     ahead_rows, ahead_ends = respond_ahead(high, low, cross, suffix, solved)
-    own_spans = gate(own_spans, (near_ends, ahead_ends))
-    near_spans = (own_spans, cross_core(own_spans))
-    own, half = join(near_place, *near_spans)
+    own, half = join(near_place, near_spans, (ahead_ends, near_ends))
     own_halves = lax.all_gather(half, "outer")
     behind_ends = respond_behind(high, low, ahead_rows, (own,))
-    inner, message = near(near_place, *near_spans, near_ends, groups)
+    inner, message = near(near_place, near_spans, near_ends, groups)
     far_ends = swap(message, "outer")
     own_halves = gate(own_halves, (far_ends, behind_ends))
     far_spans = (own_halves, cross_core(own_halves))
-    entering, _ = far(far_place, *far_spans, far_ends, own, inner)
+    mine, theirs, _ = far(far_place, *far_spans, far_ends, own, inner)
 
     first_solve, message = first_rows(
-        high, low, start_vectors, entering, ahead_ends, behind_ends, members
-    )
-    inner, message = near(near_place, *near_spans, swap(message, INNER), groups)
-    entering, squares = far(far_place, *far_spans, swap(message, "outer"), own, inner)
+        near_place,
+        high,
+        low,
+        start_vectors,
+        mine,
+        cross_core(theirs),
+        ahead_ends,
+        behind_ends,
+        members,
+    )
+    inner, message = near(near_place, near_spans, swap(message, INNER), groups)
+    mine, theirs, squares = far(far_place, *far_spans, swap(message, "outer"), own, inner)
     scale_one = jnp.sqrt(squares[0, :count] / cell_count + eps_value)
     second, squares = second_rows(
-        high, low, first_solve, entering, scale_one[:, None], members
+        near_place, high, low, first_solve, mine, cross_core(theirs), scale_one[:, None], members
     )
     squares = jnp.sum(swap(squares, INNER), axis=0)
     squares = jnp.broadcast_to(squares[None], (groups, *squares.shape))

time: 330 us -> 315 us (0.955)
  blocking collectives: 56.3 us -> 44.8 us
  waiting for transfers between devices: 134 us -> 126 us
  starting transfers between devices: 16.9 us -> 21.4 us
    all_to_all x4, blocking collectives: 56.3 us -> 44.8 us  [swap(): return lax.all_to_all(value, axis, 0, 0, tiled=True)]
    all_to_all x2, waiting for transfers between devices: 13.2 us -> 4.71 us  [swap(): return lax.all_to_all(value, axis, 0, 0, tiled=True)]
    ppermute x1 -> x2, starting transfers between devices: 2.57 us -> 7.06 us  [shards(): cross_core(theirs)]
    ppermute x1 -> x2, waiting for transfers between devices: 4.8 us -> 1.05 us  [shards(): cross_core(theirs)]
  transfers between devices with their start and end apart: 7 -> 8, of which waited for: 6 -> 6; matrix products, arithmetic and copies ran while one was open for 0% -> 1% of each run, Pallas kernels for 10% -> 10%
where the time goes in v5:
time: 315 us; the launch traced here: 314 us
  waiting for transfers between devices  126 us (40%)
  Pallas kernels  101 us (32%)
  blocking collectives  44.8 us (14%)
  starting transfers between devices  21.4 us (7%)
  between operations  13.8 us (4%)
  local copies, waits for them, and re-layouts  4.21 us (1%)
    pallas_call x11, Pallas kernels, call(): pl.pallas_call(kernel, out_shape=tuple(out_shapes), in_specs=specs, out_s...  101 us
    all_gather x1, waiting for transfers between devices, shards(): whole = lax.all_gather(factors, 'cols', axis=1, tiled=True)  65.9 us
    all_to_all x4, blocking collectives, swap(): return lax.all_to_all(value, axis, 0, 0, tiled=True)  44.8 us
    all_gather x1, waiting for transfers between devices, shards(): near_spans = lax.all_gather(operators, INNER)  24.7 us
    all_gather x1, waiting for transfers between devices, shards(): own_halves = lax.all_gather(half, 'outer')  23.9 us
    all_to_all x2, starting transfers between devices, swap(): return lax.all_to_all(value, axis, 0, 0, tiled=True)  11.4 us
    ppermute x2, starting transfers between devices, shards(): cross_core(theirs)  7.06 us
  transfers between devices with their start and end apart: 8, of which 6 were waited for; matrix products, arithmetic and copies ran while one was open for 1% of the time, Pallas kernels for 10%

profile of v5, /device:TPU:1, one launch (start us, length us, event | category | flops | bytes accessed | tf_op | source)
XLA Modules:
  0.0 313.8 jit_solution(295211421324832082)
XLA Ops:
  7.2 0.7 all-gather.6.cloned.1.call-update
  7.9 65.9 %all-gather.6.cloned.1.call-done.factors = f32[16,256,256]{2,1,0:T(8,128)} async-done(((f32[16,32,256]{2,1,0:T(8,128)}), f32[16,256,256]{2,1,0:T(8,128)}) %all-gather.6.cloned.1.call-update) | async-done | bytes 4194320 | tf_op jit(solution)/shard_map/all_gather | solution.py:521
  73.9 20.3 %shard_map.41 = (bf16[16,256,256]{2,1,0:T(8,128)(2,1)}, bf16[16,256,256]{2,1,0:T(8,128)(2,1)}, f32[16,256,256]{2,1,0:T(8,128)}, f32[16,256,256]{2,1,0:T(8,128)},...) custom-call(f32[16,256,256]{2,1,0:T(8,128)} %all-gather.6.cloned.1.call-done.factors, ...), custom_call_target="tpu_custom_call" | custom-call | flops 5234491392 | bytes 18939904 | tf_op jit(solution)/shard_map/pallas_call | solution.py:50
  94.7 4.9 %all-to-all-start = ((f32[8,40,256]{2,1,0:T(8,128)}), f32[8,40,256]{2,1,0:T(8,128)S(1)}, u32[]{:S(2)}, u32[]{:S(2)}) async-start(f32[8,40,256]{2,1,0:T(8,128)} %get-tuple-element.32), calls=%async_computation | async-start | bytes 655360 | tf_op jit(solution)/shard_map/all_to_all | solution.py:509
  99.7 14.6 %shard_map.42 = (f32[16,544,256]{2,1,0:T(8,128)}, f32[544,256]{1,0:T(8,128)}) custom-call(bf16[16,256,256]{2,1,0:T(8,128)(2,1)} %get-tuple-element.26.high.refs_1_, bf16[16,256,256]{2,1,0:T(8,128)(2,1)} %get-tuple-element.27.low.refs_2_, f32[16,256,256]{2,1,0:T(8,128)} %get-tuple-element.28.cross, f32[16,256,256]{2,1,0:T(8,128)} %get-tuple-element.29.suffix, ...), custom_call_target="tpu_custom_call" | custom-call | flops 3422552064 | bytes 22577152 | tf_op jit(solution)/shard_map/pallas_call | solution.py:50
  114.3 24.7 %all-gather.8.cloned.1.call-done = f32[24,256,256]{2,1,0:T(8,128)} async-done(((f32[3,256,256]{2,1,0:T(8,128)}), f32[24,256,256]{2,1,0:T(8,128)}) %all-gather.8.cloned.1.call-update) | async-done | bytes 6291472 | tf_op jit(solution)/shard_map/all_gather | solution.py:523
  139.0 10.3 %shard_map.43 = (f32[2,3,256,256]{3,2,1,0:T(8,128)}, f32[3,128,256]{2,1,0:T(8,128)}) custom-call(f32[544,256]{1,0:T(8,128)} %get-tuple-element.31.refs_0_.ahead_ends, f32[8,40,256]{2,1,0:T(8,128)} %copy-done.2, s32[2]{0:T(128)} %pad_add_fusion.refs_2_.place, f32[8,3,256,256]{3,2,1,0:T(8,128)} %bitcast.12), custom_call_target="tpu_custom_call" | custom-call | flops 3221225472 | bytes 8257536 | tf_op jit(solution)/shard_map/pallas_call | solution.py:50
  149.3 5.7 %shard_map.44 = (f32[2,2,16,256]{3,2,1,0:T(8,128)}, f32[8,40,256]{2,1,0:T(8,128)}) custom-call(s32[2]{0:T(128)} %pad_add_fusion.refs_2_.place, f32[8,3,256,256]{3,2,1,0:T(8,128)} %bitcast.13, f32[8,40,256]{2,1,0:T(8,128)} %copy-done.2), custom_call_target="tpu_custom_call" | custom-call | flops 150994944 | bytes 7012352 | tf_op jit(solution)/shard_map/pallas_call | solution.py:50
  155.0 6.5 %all-to-all-start.1 = ((f32[8,40,256]{2,1,0:T(8,128)}), f32[8,40,256]{2,1,0:T(8,128)S(1)}, u32[]{:S(2)}, u32[]{:S(2)}) async-start(f32[8,40,256]{2,1,0:T(8,128)} %get-tuple-element.35), calls=%async_computation.1 | async-start | bytes 655360 | tf_op jit(solution)/shard_map/all_to_all | solution.py:509
  161.5 12.1 %shard_map.45.refs_2_.behind_ends = f32[544,256]{1,0:T(8,128)} custom-call(f32[2,3,256,256]{3,2,1,0:T(8,128)} %get-tuple-element.36.refs_0_.own, bf16[16,256,256]{2,1,0:T(8,128)(2,1)} %get-tuple-element.26.high.refs_1_, bf16[16,256,256]{2,1,0:T(8,128)(2,1)} %get-tuple-element.27.low.refs_2_, f32[16,544,256]{2,1,0:T(8,128)} %get-tuple-element.37.refs_3_), custom_call_target="tpu_custom_call" | custom-call | flops 3422552064 | bytes 13664256 | tf_op jit(solution)/shard_map/pallas_call | solution.py:50
  173.5 4.7 %all-to-all-done.1.refs_1_.ends = f32[8,40,256]{2,1,0:T(8,128)S(1)} async-done(((f32[8,40,256]{2,1,0:T(8,128)}), f32[8,40,256]{2,1,0:T(8,128)S(1)}, u32[]{:S(2)}, u32[]{:S(2)}) %all-to-all-start.1) | async-done | bytes 327712 | tf_op jit(solution)/shard_map/all_to_all | solution.py:509
  178.2 23.9 %all-gather.10.cloned.1.call-done = f32[24,128,256]{2,1,0:T(8,128)} async-done(((f32[3,128,256]{2,1,0:T(8,128)}), f32[24,128,256]{2,1,0:T(8,128)}) %all-gather.10.cloned.1.call-update) | async-done | bytes 3145744 | tf_op jit(solution)/shard_map/all_gather | solution.py:527
  202.2 2.9 collective-permute-start
  205.0 0.7 pad_add_fusion.1.place
  205.7 4.8 %collective-permute-done.others = f32[8,3,128,256]{3,2,1,0:T(8,128)S(1)} collective-permute-done((f32[8,3,128,256]{3,2,1,0:T(8,128)}, f32[8,3,128,256]{3,2,1,0:T(8,128)S(1)}, u32[]{:S(2)}, u32[]{:S(2)}) %collective-permute-start) | collective-permute-done | bytes 3145760 | tf_op jit(solution)/shard_map/ppermute | solution.py:532
  210.5 1.6 copy-done
  212.1 6.3 %shard_map.47 = (f32[2,16,256]{2,1,0:T(8,128)}, f32[2,16,256]{2,1,0:T(8,128)}, f32[8,256]{1,0:T(8,128)}) custom-call(s32[2]{0:T(128)} %pad_add_fusion.1.place, f32[8,3,128,256]{3,2,1,0:T(8,128)} %shard_map.46.spans, f32[8,3,128,256]{3,2,1,0:T(8,128)} %copy-done, f32[8,40,256]{2,1,0:T(8,128)} %copy-done.1, f32[2,3,256,256]{3,2,1,0:T(8,128)} %get-tuple-element.36.refs_0_.own, ...), custom_call_target="tpu_custom_call" | custom-call | flops 150994944 | bytes 8331264 | tf_op jit(solution)/shard_map/pallas_call | solution.py:50
  218.5 2.3 collective-permute-start.1
  220.8 1.0 collective-permute-done.1.theirs
  222.4 9.3 %shard_map.48 = (f32[16,32,256]{2,1,0:T(8,128)}, f32[8,40,256]{2,1,0:T(8,128)}) custom-call(s32[2]{0:T(128)} %pad_add_fusion.refs_2_.place, bf16[16,256,256]{2,1,0:T(8,128)(2,1)} %get-tuple-element.26.high.refs_1_, bf16[16,256,256]{2,1,0:T(8,128)(2,1)} %get-tuple-element.27.low.refs_2_, f32[16,32,256]{2,1,0:T(8,128)} %source.3, ...), custom_call_target="tpu_custom_call" | custom-call | flops 402653184 | bytes 6750208 | tf_op jit(solution)/shard_map/pallas_call | solution.py:50
  231.7 11.9 %all_to_all.30.ends = f32[8,40,256]{2,1,0:T(8,128)} all-to-all(f32[8,40,256]{2,1,0:T(8,128)} %get-tuple-element.42), channel_id=1, replica_groups=mesh['outer'=8,'mid'=4,'core'=2,'cols'=8] {'mid','core'}, dimensions={0} | all-to-all | bytes 655360 | tf_op jit(solution)/shard_map/all_to_all | solution.py:509
  243.6 5.7 %shard_map.49 = (f32[2,2,16,256]{3,2,1,0:T(8,128)}, f32[8,40,256]{2,1,0:T(8,128)}) custom-call(s32[2]{0:T(128)} %pad_add_fusion.refs_2_.place, f32[8,3,256,256]{3,2,1,0:T(8,128)} %bitcast.14, f32[8,40,256]{2,1,0:T(8,128)} %all_to_all.30.ends), custom_call_target="tpu_custom_call" | custom-call | flops 150994944 | bytes 7012352 | tf_op jit(solution)/shard_map/pallas_call | solution.py:50
  249.3 15.7 %all_to_all.31.ends = f32[8,40,256]{2,1,0:T(8,128)} all-to-all(f32[8,40,256]{2,1,0:T(8,128)} %get-tuple-element.43), channel_id=1, replica_groups=mesh['outer'=8,'mid'=4,'core'=2,'cols'=8] {'outer'}, dimensions={0} | all-to-all | bytes 655360 | tf_op jit(solution)/shard_map/all_to_all | solution.py:509
  265.0 6.3 %shard_map.50 = (f32[2,16,256]{2,1,0:T(8,128)}, f32[2,16,256]{2,1,0:T(8,128)}, f32[8,256]{1,0:T(8,128)}) custom-call(s32[2]{0:T(128)} %pad_add_fusion.1.place, f32[8,3,128,256]{3,2,1,0:T(8,128)} %shard_map.46.spans, f32[8,3,128,256]{3,2,1,0:T(8,128)} %copy-done, f32[8,40,256]{2,1,0:T(8,128)} %all_to_all.31.ends, ...), custom_call_target="tpu_custom_call" | custom-call | flops 150994944 | bytes 8331264 | tf_op jit(solution)/shard_map/pallas_call | solution.py:50
  271.3 4.8 %collective-permute-start.2 = (f32[2,16,256]{2,1,0:T(8,128)}, f32[2,16,256]{2,1,0:T(8,128)S(1)}, u32[]{:S(2)}, u32[]{:S(2)}) collective-permute-start(f32[2,16,256]{2,1,0:T(8,128)} %get-tuple-element.46), channel_id=1, source_target_pairs={{0,8},{8,0},{1,9},{9,1},{2,10},{10,2},{3,11},{11,3},{4,12},{12,4},... | collective-permute-start | bytes 98312 | tf_op jit(solution)/shard_map/ppermute | solution.py:550
  276.1 0.7 sqrt_bitcast_fusion.1
  276.8 0.7 copy.9.scale
  278.1 8.7 %shard_map.51 = (f32[16,32,256]{2,1,0:T(8,128)}, f32[8,8,128]{2,1,0:T(8,128)}) custom-call(s32[2]{0:T(128)} %pad_add_fusion.refs_2_.place, bf16[16,256,256]{2,1,0:T(8,128)(2,1)} %get-tuple-element.26.high.refs_1_, bf16[16,256,256]{2,1,0:T(8,128)(2,1)} %get-tuple-element.27.low.refs_2_, f32[16,32,256]{2,1,0:T(8,128)} %get-tuple-element.41.source, ...), custom_call_target="tpu_custom_call" | custom-call | flops 402653184 | bytes 5341312 | tf_op jit(solution)/shard_map/pallas_call | solution.py:50
  286.9 8.0 %all_to_all.32 = f32[8,8,128]{2,1,0:T(8,128)S(1)} all-to-all(f32[8,8,128]{2,1,0:T(8,128)} %get-tuple-element.49), channel_id=1, replica_groups=mesh['outer'=8,'mid'=4,'core'=2,'cols'=8] {'mid','core'}, dimensions={0} | all-to-all | bytes 65536 | tf_op jit(solution)/shard_map/all_to_all | solution.py:509
  294.8 9.2 %all_to_all.33 = f32[8,8,128]{2,1,0:T(8,128)S(1)} all-to-all(f32[8,8,128]{2,1,0:T(8,128)S(1)} %broadcast_in_dim.2), channel_id=1, replica_groups=mesh['outer'=8,'mid'=4,'core'=2,'cols'=8] {'outer'}, dimensions={0} | all-to-all | bytes 65536 | tf_op jit(solution)/shard_map/all_to_all | solution.py:509
  304.6 0.7 copy.10.scale
  305.3 1.9 shard_map.52
  (22 shorter events, 2.5 us)
Async XLA Ops:
  7.2 66.7 %all-gather.6.cloned.1.call-start = ((), (), s32[]{:S(2)}) async-start(), calls=%async_computation.6 | async-start | bytes 4718592 | tf_op jit(solution)/shard_map/all_gather | solution.py:521
  7.9 131.1 %all-gather.8.cloned.1.call-start = ((), (), s32[]{:S(2)}) async-start(), calls=%async_computation.7 | async-start | bytes 7077888 | tf_op jit(solution)/shard_map/all_gather | solution.py:523
  94.7 19.6 %all-to-all-start = ((f32[8,40,256]{2,1,0:T(8,128)}), f32[8,40,256]{2,1,0:T(8,128)S(1)}, u32[]{:S(2)}, u32[]{:S(2)}) async-start(f32[8,40,256]{2,1,0:T(8,128)} %get-tuple-element.32), calls=%async_computation | async-start | bytes 655360 | tf_op jit(solution)/shard_map/all_to_all | solution.py:509
  99.7 102.5 %all-gather.10.cloned.1.call-start = ((), (), s32[]{:S(2)}) async-start(), calls=%async_computation.8 | async-start | bytes 3538944 | tf_op jit(solution)/shard_map/all_gather | solution.py:527
  114.3 24.7 %copy-start.2 = (f32[8,40,256]{2,1,0:T(8,128)}, f32[8,40,256]{2,1,0:T(8,128)S(1)}, u32[]{:S(2)}) copy-start(f32[8,40,256]{2,1,0:T(8,128)S(1)} %all-to-all-done.refs_1_.ends) | copy-start | bytes 983044
  155.0 23.3 %all-to-all-start.1 = ((f32[8,40,256]{2,1,0:T(8,128)}), f32[8,40,256]{2,1,0:T(8,128)S(1)}, u32[]{:S(2)}, u32[]{:S(2)}) async-start(f32[8,40,256]{2,1,0:T(8,128)} %get-tuple-element.35), calls=%async_computation.1 | async-start | bytes 655360 | tf_op jit(solution)/shard_map/all_to_all | solution.py:509
  178.2 23.9 %copy-start.1 = (f32[8,40,256]{2,1,0:T(8,128)}, f32[8,40,256]{2,1,0:T(8,128)S(1)}, u32[]{:S(2)}) copy-start(f32[8,40,256]{2,1,0:T(8,128)S(1)} %all-to-all-done.1.refs_1_.ends) | copy-start | bytes 983044
  202.2 8.4 %collective-permute-start = (f32[8,3,128,256]{3,2,1,0:T(8,128)}, f32[8,3,128,256]{3,2,1,0:T(8,128)S(1)}, u32[]{:S(2)}, u32[]{:S(2)}) collective-permute-start(f32[8,3,128,256]{3,2,1,0:T(8,128)} %shard_map.46.spans), channel_id=1, source_target_pairs={{0,8},{8,0},{1,9},{9,1},{2,10},{10,2},{3,11},{11,3},{4,12},{12,4},... | collective-permute-start | bytes 9437192 | tf_op jit(solution)/shard_map/ppermute | solution.py:532
  210.5 1.6 copy-start
  218.5 3.3 %collective-permute-start.1 = (f32[2,16,256]{2,1,0:T(8,128)}, f32[2,16,256]{2,1,0:T(8,128)S(1)}, u32[]{:S(2)}, u32[]{:S(2)}) collective-permute-start(f32[2,16,256]{2,1,0:T(8,128)} %get-tuple-element.40), channel_id=1, source_target_pairs={{0,8},{8,0},{1,9},{9,1},{2,10},{10,2},{3,11},{11,3},{4,12},{12,4},... | collective-permute-start | bytes 98312 | tf_op jit(solution)/shard_map/ppermute | solution.py:541
  221.8 0.6 copy-start.4
  271.3 6.2 %collective-permute-start.2 = (f32[2,16,256]{2,1,0:T(8,128)}, f32[2,16,256]{2,1,0:T(8,128)S(1)}, u32[]{:S(2)}, u32[]{:S(2)}) collective-permute-start(f32[2,16,256]{2,1,0:T(8,128)} %get-tuple-element.46), channel_id=1, source_target_pairs={{0,8},{8,0},{1,9},{9,1},{2,10},{10,2},{3,11},{11,3},{4,12},{12,4},... | collective-permute-start | bytes 98312 | tf_op jit(solution)/shard_map/ppermute | solution.py:550
  277.5 0.6 copy-start.3
Sparse Core Ops, SparseCore 0:
  10.1 63.7 all-gather.5
  94.3 44.7 all-gather.7
  149.4 52.6 all-gather.9

commit v6 on v5

--- a/solution.py
+++ b/solution.py
@@ -56,17 +56,6 @@
         compiler_params=pltpu.CompilerParams(vmem_limit_bytes=VMEM_BYTES),
         cost_estimate=pl.CostEstimate(flops=flops, bytes_accessed=touched, transcendentals=0),
     )(*operands)
-
-
-def gate(value, after):
-    anywhere = pl.BlockSpec(memory_space=pl.ANY)
-    return pl.pallas_call(
-        lambda *refs: None,
-        out_shape=shape(*value.shape, dtype=value.dtype),
-        in_specs=[anywhere] * (1 + len(after)),
-        out_specs=anywhere,
-        input_output_aliases={0: 0},
-    )(value, *after)
 
 
 def shape(*dims, dtype=jnp.float32):
@@ -213,23 +202,48 @@
     return spans[e, part]
 
 
-def far_span(place, own, other, e, part):
-    first = place[1] == 0
-    return jnp.concatenate(
-        [
-            jnp.where(first, own[e, part], other[e, part]),
-            jnp.where(first, other[e, part], own[e, part]),
-        ],
-        axis=0,
-    )
-
-
-def join_body(place, spans, own, half, reach, crossing):
+def far_span(spans, e, part):
+    return jnp.concatenate([spans[2 * e, part], spans[2 * e + 1, part]], axis=0)
+
+
+def merge(before, behind):
+    width = before[0].shape[0]
+    ahead = apply_split(before[0], *split(behind[0]))
+    turned = apply_split(before[0], *split(behind[2]))
+    back = apply_split(jnp.concatenate([behind[1], turned], axis=0), *split(before[1]))
+    return ahead, back[:width], before[2] + back[width:]
+
+
+def compose_body(place, spans, half, whole):
+    parts = spans.shape[1]
+    width = spans.shape[2]
+    level = [tuple(spans[e, part] for part in range(parts)) for e in range(spans.shape[0])]
+    while len(level) > 1:
+        level = [merge(*level[i : i + 2]) for i in range(0, len(level), 2)]
+    kept = pl.ds(pl.multiple_of(place[1] * (width // 2), width // 2), width // 2)
+    for part in range(parts):
+        whole[...] = level[0][part]
+        half[part] = whole[kept]
+
+
+def compose(place, spans, after):
+    members, parts, width, _ = spans.shape
+    return call(
+        compose_body,
+        [shape(parts, width // 2, width)],
+        [pltpu.VMEM((width, width), jnp.float32)],
+        members * 6 * 4 * width**3,
+        spans,
+        after=after,
+        position=place,
+    )[0]
+
+
+def reach_body(place, spans, own, reach, crossing):
     members, _, width, _ = spans.shape
     reach[0] = identity(width)
     reach[1] = identity(width)
     chip = place[0]
-    kept = pl.ds(pl.multiple_of(place[1] * (width // 2), width // 2), width // 2)
 
     def outward(e, _):
         @pl.when(e // 2 == chip)
@@ -249,8 +263,6 @@
         return 0
 
     lax.fori_loop(0, members, outward, 0)
-    half[0] = reach[0, kept]
-    half[1] = reach[1, kept]
     reach[0] = jnp.zeros((width, width), jnp.float32)
 
     def inward(i, _):
@@ -264,14 +276,13 @@
         return 0
 
     lax.fori_loop(0, members, inward, 0)
-    half[2] = reach[0, kept]
-
-
-def join(place, spans, after):
+
+
+def reaching(place, spans, after):
     members, parts, width, _ = spans.shape
     return call(
-        join_body,
-        [shape(2, parts, width, width), shape(parts, width // 2, width)],
+        reach_body,
+        [shape(2, parts, width, width)],
         [
             pltpu.VMEM((2, width, width), jnp.float32),
             pltpu.VMEM((members, width, width), jnp.float32),
@@ -280,7 +291,7 @@
         spans,
         after=after,
         position=place,
-    )
+    )[0]
 
 
 def relay(span, ends, states):
@@ -337,8 +348,8 @@
     )
 
 
-def far_body(place, spans, others, ends, own, inner, mine, theirs, squares, states, entering):
-    relay(functools.partial(far_span, place, spans, others), ends, states)
+def far_body(place, spans, ends, own, inner, mine, theirs, squares, states, entering):
+    relay(functools.partial(far_span, spans), ends, states)
     ahead, behind = states[0, place[0]], states[1, place[0]]
     for core in range(2):
         entering[core, 0] = apply_split(ahead, *split(own[core, 0])) + inner[core, 0]
@@ -352,7 +363,7 @@
     squares[...] = total_of(ends)
 
 
-def far(place, spans, others, ends, own, inner):
+def far(place, spans, ends, own, inner, after=()):
     members, length, width = ends.shape
     count = (length - 8) // 2
     return call(
@@ -364,10 +375,10 @@
         ],
         members * 6 * 3 * count * width * width,
         spans,
-        others,
         ends,
         own,
         inner,
+        after=after,
         position=place,
     )
 
@@ -523,14 +534,13 @@
     near_spans = lax.all_gather(operators, INNER)
     near_ends = swap(ends, INNER)
     ahead_rows, ahead_ends = respond_ahead(high, low, cross, suffix, solved)
-    own, half = join(near_place, near_spans, (ahead_ends, near_ends))
-    own_halves = lax.all_gather(half, "outer")
-    behind_ends = respond_behind(high, low, ahead_rows, (own,))
+    half = compose(near_place, near_spans, (ahead_ends, near_ends))
+    far_spans = lax.all_gather(half, ("outer", "core"))
     inner, message = near(near_place, near_spans, near_ends, groups)
     far_ends = swap(message, "outer")
-    own_halves = gate(own_halves, (far_ends, behind_ends))
-    far_spans = (own_halves, cross_core(own_halves))
-    mine, theirs, _ = far(far_place, *far_spans, far_ends, own, inner)
+    behind_ends = respond_behind(high, low, ahead_rows, (half,))
+    own = reaching(near_place, near_spans, (half,))
+    mine, theirs, _ = far(far_place, far_spans, far_ends, own, inner, (behind_ends,))
 
     first_solve, message = first_rows(
         near_place,
@@ -544,7 +554,7 @@
         members,
     )
     inner, message = near(near_place, near_spans, swap(message, INNER), groups)
-    mine, theirs, squares = far(far_place, *far_spans, swap(message, "outer"), own, inner)
+    mine, theirs, squares = far(far_place, far_spans, swap(message, "outer"), own, inner)
     scale_one = jnp.sqrt(squares[0, :count] / cell_count + eps_value)
     second, squares = second_rows(
         near_place, high, low, first_solve, mine, cross_core(theirs), scale_one[:, None], members

time: 315 us -> 304 us (0.965)
  waiting for transfers between devices: 126 us -> 112 us
  Pallas kernels: 101 us -> 109 us
    pallas_call x11 -> x12, Pallas kernels: 101 us -> 109 us  [call(): pl.pallas_call(kernel, out_shape=tuple(out_shapes), in_specs=specs, out_s...]
    ppermute x1 -> x0, waiting for transfers between devices: 4.8 us -> none  [shards(): far_spans = (own_halves, cross_core(own_halves))]
    all_to_all x2, waiting for transfers between devices: 4.71 us -> 0.01 us  [swap(): return lax.all_to_all(value, axis, 0, 0, tiled=True)]
    all_gather x1, waiting for transfers between devices: 23.9 us -> 19.9 us  [shards(): far_spans = lax.all_gather(half, ('outer', 'core'))]
  transfers between devices with their start and end apart: 8 -> 7, of which waited for: 6 -> 4; matrix products, arithmetic and copies ran while one was open for 1% -> 1% of each run, Pallas kernels for 10% -> 14%
where the time goes in v6:
time: 304 us; the launch traced here: 303 us
  waiting for transfers between devices  112 us (37%)
  Pallas kernels  109 us (36%)
  blocking collectives  44.7 us (15%)
  starting transfers between devices  18.4 us (6%)
  between operations  13.8 us (5%)
    pallas_call x12, Pallas kernels, call(): pl.pallas_call(kernel, out_shape=tuple(out_shapes), in_specs=specs, out_s...  109 us
    all_gather x1, waiting for transfers between devices, shards(): whole = lax.all_gather(factors, 'cols', axis=1, tiled=True)  65.9 us
    all_to_all x4, blocking collectives, swap(): return lax.all_to_all(value, axis, 0, 0, tiled=True)  44.7 us
    all_gather x1, waiting for transfers between devices, shards(): near_spans = lax.all_gather(operators, INNER)  24.7 us
    all_gather x1, waiting for transfers between devices, shards(): far_spans = lax.all_gather(half, ('outer', 'core'))  19.9 us
    all_to_all x2, starting transfers between devices, swap(): return lax.all_to_all(value, axis, 0, 0, tiled=True)  11.4 us
    ppermute x2, starting transfers between devices, shards(): cross_core(theirs)  6.95 us
  transfers between devices with their start and end apart: 7, of which 4 were waited for; matrix products, arithmetic and copies ran while one was open for 1% of the time, Pallas kernels for 14%

profile of v6, /device:TPU:1, one launch (start us, length us, event | category | flops | bytes accessed | tf_op | source)
XLA Modules:
  0.0 303.2 jit_solution(13835117442299190278)
XLA Ops:
  7.2 0.7 all-gather.6.cloned.1.call-update
  7.9 65.9 %all-gather.6.cloned.1.call-done.factors = f32[16,256,256]{2,1,0:T(8,128)} async-done(((f32[16,32,256]{2,1,0:T(8,128)}), f32[16,256,256]{2,1,0:T(8,128)}) %all-gather.6.cloned.1.call-update) | async-done | bytes 4194320 | tf_op jit(solution)/shard_map/all_gather | solution.py:532
  73.9 20.2 %shard_map.41 = (bf16[16,256,256]{2,1,0:T(8,128)(2,1)}, bf16[16,256,256]{2,1,0:T(8,128)(2,1)}, f32[16,256,256]{2,1,0:T(8,128)}, f32[16,256,256]{2,1,0:T(8,128)},...) custom-call(f32[16,256,256]{2,1,0:T(8,128)} %all-gather.6.cloned.1.call-done.factors, ...), custom_call_target="tpu_custom_call" | custom-call | flops 5234491392 | bytes 18939904 | tf_op jit(solution)/shard_map/pallas_call | solution.py:50
  94.1 0.6 pad_add_fusion.refs_2_.place.refs_1_
  94.7 4.9 %all-to-all-start = ((f32[8,40,256]{2,1,0:T(8,128)}), f32[8,40,256]{2,1,0:T(8,128)S(1)}, u32[]{:S(2)}, u32[]{:S(2)}) async-start(f32[8,40,256]{2,1,0:T(8,128)} %get-tuple-element.30), calls=%async_computation | async-start | bytes 655360 | tf_op jit(solution)/shard_map/all_to_all | solution.py:520
  99.6 14.7 %shard_map.42 = (f32[16,544,256]{2,1,0:T(8,128)}, f32[544,256]{1,0:T(8,128)}) custom-call(bf16[16,256,256]{2,1,0:T(8,128)(2,1)} %get-tuple-element.24.high.refs_1_, bf16[16,256,256]{2,1,0:T(8,128)(2,1)} %get-tuple-element.25.low.refs_2_, f32[16,256,256]{2,1,0:T(8,128)} %get-tuple-element.26.cross, f32[16,256,256]{2,1,0:T(8,128)} %get-tuple-element.27.suffix, ...), custom_call_target="tpu_custom_call" | custom-call | flops 3422552064 | bytes 22577152 | tf_op jit(solution)/shard_map/pallas_call | solution.py:50
  114.3 24.7 %all-gather.8.cloned.1.call-done = f32[24,256,256]{2,1,0:T(8,128)} async-done(((f32[3,256,256]{2,1,0:T(8,128)}), f32[24,256,256]{2,1,0:T(8,128)}) %all-gather.8.cloned.1.call-update) | async-done | bytes 6291472 | tf_op jit(solution)/shard_map/all_gather | solution.py:534
  139.0 7.4 %shard_map.43.refs_0_ = f32[3,128,256]{2,1,0:T(8,128)} custom-call(f32[544,256]{1,0:T(8,128)} %get-tuple-element.29.refs_0_.ahead_ends, f32[8,40,256]{2,1,0:T(8,128)} %copy-done.1, s32[2]{0:T(128)} %pad_add_fusion.refs_2_.place.refs_1_, f32[8,3,256,256]{3,2,1,0:T(8,128)} %bitcast.13), custom_call_target="tpu_custom_call" | custom-call | flops 3221225472 | bytes 6684672 | tf_op jit(solution)/shard_map/pallas_call | solution.py:50
  146.4 0.7 pad_add_fusion.1.refs_1_.place
  147.0 5.7 %shard_map.45 = (f32[2,2,16,256]{3,2,1,0:T(8,128)}, f32[8,40,256]{2,1,0:T(8,128)}) custom-call(s32[2]{0:T(128)} %pad_add_fusion.refs_2_.place.refs_1_, f32[8,3,256,256]{3,2,1,0:T(8,128)} %bitcast.14, f32[8,40,256]{2,1,0:T(8,128)} %copy-done.1), custom_call_target="tpu_custom_call" | custom-call | flops 150994944 | bytes 7012352 | tf_op jit(solution)/shard_map/pallas_call | solution.py:50
  152.7 6.5 %all-to-all-start.1 = ((f32[8,40,256]{2,1,0:T(8,128)}), f32[8,40,256]{2,1,0:T(8,128)S(1)}, u32[]{:S(2)}, u32[]{:S(2)}) async-start(f32[8,40,256]{2,1,0:T(8,128)} %get-tuple-element.33), calls=%async_computation.1 | async-start | bytes 655360 | tf_op jit(solution)/shard_map/all_to_all | solution.py:520
  159.2 10.4 %shard_map.46.refs_4_.own = f32[2,3,256,256]{3,2,1,0:T(8,128)} custom-call(f32[3,128,256]{2,1,0:T(8,128)} %shard_map.43.refs_0_, s32[2]{0:T(128)} %pad_add_fusion.refs_2_.place.refs_1_, f32[8,3,256,256]{3,2,1,0:T(8,128)} %bitcast.15), custom_call_target="tpu_custom_call" | custom-call | flops 3221225472 | bytes 7864320 | tf_op jit(solution)/shard_map/pallas_call | solution.py:50
  169.6 12.1 %shard_map.44.refs_0_.behind_ends = f32[544,256]{1,0:T(8,128)} custom-call(f32[3,128,256]{2,1,0:T(8,128)} %shard_map.43.refs_0_, bf16[16,256,256]{2,1,0:T(8,128)(2,1)} %get-tuple-element.24.high.refs_1_, bf16[16,256,256]{2,1,0:T(8,128)(2,1)} %get-tuple-element.25.low.refs_2_, f32[16,544,256]{2,1,0:T(8,128)} %get-tuple-element.32.refs_3_), custom_call_target="tpu_custom_call" | custom-call | flops 3422552064 | bytes 13664256 | tf_op jit(solution)/shard_map/pallas_call | solution.py:50
  181.7 19.9 %all-gather.10.cloned.1.call-done = f32[48,128,256]{2,1,0:T(8,128)} async-done(((f32[3,128,256]{2,1,0:T(8,128)}), f32[48,128,256]{2,1,0:T(8,128)}) %all-gather.10.cloned.1.call-update) | async-done | bytes 6291472 | tf_op jit(solution)/shard_map/all_gather | solution.py:538
  201.7 6.3 %shard_map.47 = (f32[2,16,256]{2,1,0:T(8,128)}, f32[2,16,256]{2,1,0:T(8,128)}, f32[8,256]{1,0:T(8,128)}) custom-call(f32[544,256]{1,0:T(8,128)} %shard_map.44.refs_0_.behind_ends, s32[2]{0:T(128)} %pad_add_fusion.1.refs_1_.place, f32[16,3,128,256]{3,2,1,0:T(8,128)} %bitcast.11, f32[8,40,256]{2,1,0:T(8,128)} %copy-done, ...), custom_call_target="tpu_custom_call" | custom-call | flops 150994944 | bytes 8331264 | tf_op jit(solution)/shard_map/pallas_call | solution.py:50
  208.0 2.2 collective-permute-start
  210.2 1.1 collective-permute-done.theirs
  211.3 0.6 copy-done.3
  211.9 9.3 %shard_map.48 = (f32[16,32,256]{2,1,0:T(8,128)}, f32[8,40,256]{2,1,0:T(8,128)}) custom-call(s32[2]{0:T(128)} %pad_add_fusion.refs_2_.place.refs_1_, bf16[16,256,256]{2,1,0:T(8,128)(2,1)} %get-tuple-element.24.high.refs_1_, bf16[16,256,256]{2,1,0:T(8,128)(2,1)} %get-tuple-element.25.low.refs_2_, f32[16,32,256]{2,1,0:T(8,128)} %source.3, ...), custom_call_target="tpu_custom_call" | custom-call | flops 402653184 | bytes 6750208 | tf_op jit(solution)/shard_map/pallas_call | solution.py:50
  221.2 11.8 %all_to_all.30.ends = f32[8,40,256]{2,1,0:T(8,128)} all-to-all(f32[8,40,256]{2,1,0:T(8,128)} %get-tuple-element.38), channel_id=1, replica_groups=mesh['outer'=8,'mid'=4,'core'=2,'cols'=8] {'mid','core'}, dimensions={0} | all-to-all | bytes 655360 | tf_op jit(solution)/shard_map/all_to_all | solution.py:520
  233.0 5.7 %shard_map.49 = (f32[2,2,16,256]{3,2,1,0:T(8,128)}, f32[8,40,256]{2,1,0:T(8,128)}) custom-call(s32[2]{0:T(128)} %pad_add_fusion.refs_2_.place.refs_1_, f32[8,3,256,256]{3,2,1,0:T(8,128)} %bitcast.16, f32[8,40,256]{2,1,0:T(8,128)} %all_to_all.30.ends), custom_call_target="tpu_custom_call" | custom-call | flops 150994944 | bytes 7012352 | tf_op jit(solution)/shard_map/pallas_call | solution.py:50
  238.7 15.7 %all_to_all.31.ends = f32[8,40,256]{2,1,0:T(8,128)} all-to-all(f32[8,40,256]{2,1,0:T(8,128)} %get-tuple-element.39), channel_id=1, replica_groups=mesh['outer'=8,'mid'=4,'core'=2,'cols'=8] {'outer'}, dimensions={0} | all-to-all | bytes 655360 | tf_op jit(solution)/shard_map/all_to_all | solution.py:520
  254.4 6.3 %shard_map.50 = (f32[2,16,256]{2,1,0:T(8,128)}, f32[2,16,256]{2,1,0:T(8,128)}, f32[8,256]{1,0:T(8,128)}) custom-call(s32[2]{0:T(128)} %pad_add_fusion.1.refs_1_.place, f32[16,3,128,256]{3,2,1,0:T(8,128)} %bitcast.12, f32[8,40,256]{2,1,0:T(8,128)} %all_to_all.31.ends, f32[2,3,256,256]{3,2,1,0:T(8,128)} %shard_map.46.refs_4_.own, ...), custom_call_target="tpu_custom_call" | custom-call | flops 150994944 | bytes 8331264 | tf_op jit(solution)/shard_map/pallas_call | solution.py:50
  260.8 4.8 %collective-permute-start.1 = (f32[2,16,256]{2,1,0:T(8,128)}, f32[2,16,256]{2,1,0:T(8,128)S(1)}, u32[]{:S(2)}, u32[]{:S(2)}) collective-permute-start(f32[2,16,256]{2,1,0:T(8,128)} %get-tuple-element.42), channel_id=1, source_target_pairs={{0,8},{8,0},{1,9},{9,1},{2,10},{10,2},{3,11},{11,3},{4,12},{12,4},... | collective-permute-start | bytes 98312 | tf_op jit(solution)/shard_map/ppermute | solution.py:560
  265.6 0.7 sqrt_bitcast_fusion.1
  266.2 0.7 copy.8.scale
  266.9 0.6 copy-done.2
  267.5 8.8 %shard_map.51 = (f32[16,32,256]{2,1,0:T(8,128)}, f32[8,8,128]{2,1,0:T(8,128)}) custom-call(s32[2]{0:T(128)} %pad_add_fusion.refs_2_.place.refs_1_, bf16[16,256,256]{2,1,0:T(8,128)(2,1)} %get-tuple-element.24.high.refs_1_, bf16[16,256,256]{2,1,0:T(8,128)(2,1)} %get-tuple-element.25.low.refs_2_, f32[16,32,256]{2,1,0:T(8,128)} %get-tuple-element.37.source, ...), custom_call_target="tpu_custom_call" | custom-call | flops 402653184 | bytes 5341312 | tf_op jit(solution)/shard_map/pallas_call | solution.py:50
  276.3 8.0 %all_to_all.32 = f32[8,8,128]{2,1,0:T(8,128)S(1)} all-to-all(f32[8,8,128]{2,1,0:T(8,128)} %get-tuple-element.45), channel_id=1, replica_groups=mesh['outer'=8,'mid'=4,'core'=2,'cols'=8] {'mid','core'}, dimensions={0} | all-to-all | bytes 65536 | tf_op jit(solution)/shard_map/all_to_all | solution.py:520
  284.3 9.2 %all_to_all.33 = f32[8,8,128]{2,1,0:T(8,128)S(1)} all-to-all(f32[8,8,128]{2,1,0:T(8,128)S(1)} %broadcast_in_dim.2), channel_id=1, replica_groups=mesh['outer'=8,'mid'=4,'core'=2,'cols'=8] {'outer'}, dimensions={0} | all-to-all | bytes 65536 | tf_op jit(solution)/shard_map/all_to_all | solution.py:520
  294.0 0.7 copy.9.scale
  294.7 1.9 shard_map.52
  (18 shorter events, 0.7 us)
Async XLA Ops:
  7.2 66.7 %all-gather.6.cloned.1.call-start = ((), (), s32[]{:S(2)}) async-start(), calls=%async_computation.6 | async-start | bytes 4718592 | tf_op jit(solution)/shard_map/all_gather | solution.py:532
  7.9 131.1 %all-gather.8.cloned.1.call-start = ((), (), s32[]{:S(2)}) async-start(), calls=%async_computation.7 | async-start | bytes 7077888 | tf_op jit(solution)/shard_map/all_gather | solution.py:534
  94.7 19.6 %all-to-all-start = ((f32[8,40,256]{2,1,0:T(8,128)}), f32[8,40,256]{2,1,0:T(8,128)S(1)}, u32[]{:S(2)}, u32[]{:S(2)}) async-start(f32[8,40,256]{2,1,0:T(8,128)} %get-tuple-element.30), calls=%async_computation | async-start | bytes 655360 | tf_op jit(solution)/shard_map/all_to_all | solution.py:520
  99.6 102.0 %all-gather.10.cloned.1.call-start = ((), (), s32[]{:S(2)}) async-start(), calls=%async_computation.8 | async-start | bytes 6684672 | tf_op jit(solution)/shard_map/all_gather | solution.py:538
  114.3 24.7 %copy-start.1 = (f32[8,40,256]{2,1,0:T(8,128)}, f32[8,40,256]{2,1,0:T(8,128)S(1)}, u32[]{:S(2)}) copy-start(f32[8,40,256]{2,1,0:T(8,128)S(1)} %all-to-all-done.refs_1_.ends) | copy-start | bytes 983044
  152.7 29.0 %all-to-all-start.1 = ((f32[8,40,256]{2,1,0:T(8,128)}), f32[8,40,256]{2,1,0:T(8,128)S(1)}, u32[]{:S(2)}, u32[]{:S(2)}) async-start(f32[8,40,256]{2,1,0:T(8,128)} %get-tuple-element.33), calls=%async_computation.1 | async-start | bytes 655360 | tf_op jit(solution)/shard_map/all_to_all | solution.py:520
  181.7 19.9 %copy-start = (f32[8,40,256]{2,1,0:T(8,128)}, f32[8,40,256]{2,1,0:T(8,128)S(1)}, u32[]{:S(2)}) copy-start(f32[8,40,256]{2,1,0:T(8,128)S(1)} %all-to-all-done.1.refs_3_) | copy-start | bytes 983044
  208.0 3.3 %collective-permute-start = (f32[2,16,256]{2,1,0:T(8,128)}, f32[2,16,256]{2,1,0:T(8,128)S(1)}, u32[]{:S(2)}, u32[]{:S(2)}) collective-permute-start(f32[2,16,256]{2,1,0:T(8,128)} %get-tuple-element.36), channel_id=1, source_target_pairs={{0,8},{8,0},{1,9},{9,1},{2,10},{10,2},{3,11},{11,3},{4,12},{12,4},... | collective-permute-start | bytes 98312 | tf_op jit(solution)/shard_map/ppermute | solution.py:551
  211.3 0.6 copy-start.3
  260.8 6.2 %collective-permute-start.1 = (f32[2,16,256]{2,1,0:T(8,128)}, f32[2,16,256]{2,1,0:T(8,128)S(1)}, u32[]{:S(2)}, u32[]{:S(2)}) collective-permute-start(f32[2,16,256]{2,1,0:T(8,128)} %get-tuple-element.42), channel_id=1, source_target_pairs={{0,8},{8,0},{1,9},{9,1},{2,10},{10,2},{3,11},{11,3},{4,12},{12,4},... | collective-permute-start | bytes 98312 | tf_op jit(solution)/shard_map/ppermute | solution.py:560
  266.9 0.6 copy-start.2
Sparse Core Ops, SparseCore 0:
  10.1 63.7 all-gather.5
  94.2 44.7 all-gather.7
  146.5 55.1 all-gather.9

commit v7 on v6

--- a/solution.py
+++ b/solution.py
@@ -32,30 +32,61 @@
     )
 
 
-def call(body, out_shapes, scratch, flops, *operands, after=(), position=None):
+class Streamed:
+    def __init__(self, source, buffer, done):
+        self.source, self.buffer, self.done = source, buffer, done
+        self.shape = buffer.shape
+
+    def copy(self, block):
+        return pltpu.make_async_copy(
+            self.source.at[block], self.buffer.at[block], self.done.at[block]
+        )
+
+    def wait(self, block):
+        self.copy(block).wait()
+
+    def __getitem__(self, index):
+        return self.buffer[index]
+
+
+def call(body, out_shapes, scratch, flops, *operands, after=(), position=None, streamed=()):
     vmem = pl.BlockSpec(memory_space=pltpu.VMEM)
+    anywhere = pl.BlockSpec(memory_space=pl.ANY)
     touched = sum(x.size * x.dtype.itemsize for x in (*operands, *out_shapes))
-    specs = [vmem] * len(operands)
+    specs = [anywhere if i in streamed else vmem for i in range(len(operands))]
+    buffers = [pltpu.VMEM(operands[i].shape, operands[i].dtype) for i in streamed]
+    done = [pltpu.SemaphoreType.DMA((operands[i].shape[0],)) for i in streamed]
+    first = 0
     if position is not None:
         specs = [pl.BlockSpec(memory_space=pltpu.SMEM), *specs]
         operands = (position, *operands)
-    kernel = body
-    if after:
-        specs = [pl.BlockSpec(memory_space=pl.ANY)] * len(after) + specs
-        operands = (*after, *operands)
-
-        def kernel(*refs):
-            body(*refs[len(after) :])
+        first = 1
+    specs = [anywhere] * len(after) + specs
+
+    def kernel(*refs):
+        refs = list(refs[len(after) :])
+        ends = len(refs) - 2 * len(streamed)
+        extra = refs[ends:]
+        refs = refs[:ends]
+        arriving = []
+        for k, i in enumerate(streamed):
+            refs[first + i] = Streamed(refs[first + i], extra[k], extra[len(streamed) + k])
+            arriving.append(refs[first + i])
+        if arriving:
+            for block in range(arriving[0].shape[0]):
+                for operand in arriving:
+                    operand.copy(block).start()
+        body(*refs)
 
     return pl.pallas_call(
         kernel,
         out_shape=tuple(out_shapes),
         in_specs=specs,
         out_specs=tuple([vmem] * len(out_shapes)),
-        scratch_shapes=scratch,
+        scratch_shapes=[*scratch, *buffers, *done],
         compiler_params=pltpu.CompilerParams(vmem_limit_bytes=VMEM_BYTES),
         cost_estimate=pl.CostEstimate(flops=flops, bytes_accessed=touched, transcendentals=0),
-    )(*operands)
+    )(*after, *operands)
 
 
 def shape(*dims, dtype=jnp.float32):
@@ -67,6 +98,7 @@
     count = source.shape[1]
 
     def turn(i, _):
+        factors.wait(i)
         high[i], low[i] = split(factors[i].T)
         return 0
 
@@ -132,6 +164,7 @@
         rows * 6 * (2 * count + 3 * width) * width * width,
         factors,
         source,
+        streamed=(0,),
     )
 
 
@@ -217,7 +250,12 @@
 def compose_body(place, spans, half, whole):
     parts = spans.shape[1]
     width = spans.shape[2]
-    level = [tuple(spans[e, part] for part in range(parts)) for e in range(spans.shape[0])]
+
+    def span(e):
+        spans.wait(e)
+        return tuple(spans[e, part] for part in range(parts))
+
+    level = [merge(span(e), span(e + 1)) for e in range(0, spans.shape[0], 2)]
     while len(level) > 1:
         level = [merge(*level[i : i + 2]) for i in range(0, len(level), 2)]
     kept = pl.ds(pl.multiple_of(place[1] * (width // 2), width // 2), width // 2)
@@ -236,6 +274,7 @@
         spans,
         after=after,
         position=place,
+        streamed=(0,),
     )[0]
 
 
@@ -294,12 +333,13 @@
     )[0]
 
 
-def relay(span, ends, states):
+def relay(span, arrive, ends, states):
     members, length, width = ends.shape
     count = (length - 8) // 2
     state = jnp.zeros((count, width), jnp.float32)
     entered = []
     for e in range(members):
+        arrive(e)
         entered.append(state)
         states[0, e] = state
         end = ends[e, :count]
@@ -325,7 +365,7 @@
 
 def near_body(place, spans, ends, entered, messages, states):
     count = entered.shape[2]
-    ahead, behind = relay(functools.partial(row_span, spans), ends, states)
+    ahead, behind = relay(functools.partial(row_span, spans), spans.wait, ends, states)
     message = jnp.concatenate([ahead, behind, total_of(ends)], axis=0)
     for member in range(messages.shape[0]):
         messages[member] = message
@@ -345,11 +385,17 @@
         spans,
         ends,
         position=place,
+        streamed=(0,),
     )
 
 
 def far_body(place, spans, ends, own, inner, mine, theirs, squares, states, entering):
-    relay(functools.partial(far_span, spans), ends, states)
+
+    def arrive(e):
+        spans.wait(2 * e)
+        spans.wait(2 * e + 1)
+
+    relay(functools.partial(far_span, spans), arrive, ends, states)
     ahead, behind = states[0, place[0]], states[1, place[0]]
     for core in range(2):
         entering[core, 0] = apply_split(ahead, *split(own[core, 0])) + inner[core, 0]
@@ -380,6 +426,7 @@
         inner,
         after=after,
         position=place,
+        streamed=(0,),
     )
 
 
@@ -421,6 +468,8 @@
     entering = [both_halves(place, mine, theirs, way) for way in range(2)]
 
     def ahead(i, state):
+        high.wait(i)
+        low.wait(i)
         state = apply_split(state, high[i], low[i]) + source[i]
         forward[i] = state
         return state
@@ -460,6 +509,7 @@
         ahead_ends,
         behind_ends,
         position=place,
+        streamed=(0, 1),
     )
 
 
@@ -469,6 +519,8 @@
     entering = [both_halves(place, mine, theirs, way) for way in range(2)]
 
     def ahead(i, state):
+        high.wait(i)
+        low.wait(i)
         state = apply_split(state, high[i], low[i]) + source[i]
         forward[i] = state
         return state
@@ -505,6 +557,7 @@
         theirs,
         scale,
         position=place,
+        streamed=(0, 1),
     )
 
 

time: 304 us -> 306 us (level)
  no operation moved by 1% of the time
where the time goes in v7:
time: 306 us; the launch traced here: 305 us
  waiting for transfers between devices  112 us (37%)
  Pallas kernels  111 us (36%)
  blocking collectives  44.7 us (15%)
  starting transfers between devices  18.4 us (6%)
  between operations  13.8 us (5%)
    pallas_call x12, Pallas kernels, call(): pl.pallas_call(kernel, out_shape=tuple(out_shapes), in_specs=specs, out_s...  111 us
    all_gather x1, waiting for transfers between devices, shards(): whole = lax.all_gather(factors, 'cols', axis=1, tiled=True)  65.9 us
    all_to_all x4, blocking collectives, swap(): return lax.all_to_all(value, axis, 0, 0, tiled=True)  44.7 us
    all_gather x1, waiting for transfers between devices, shards(): near_spans = lax.all_gather(operators, INNER)  24.7 us
    all_gather x1, waiting for transfers between devices, shards(): far_spans = lax.all_gather(half, ('outer', 'core'))  19.9 us
    all_to_all x2, starting transfers between devices, swap(): return lax.all_to_all(value, axis, 0, 0, tiled=True)  11.4 us
    ppermute x2, starting transfers between devices, shards(): cross_core(theirs)  6.97 us
  transfers between devices with their start and end apart: 7, of which 4 were waited for; matrix products, arithmetic and copies ran while one was open for 1% of the time, Pallas kernels for 14%

profile of v7, /device:TPU:1, one launch (start us, length us, event | category | flops | bytes accessed | tf_op | source)
XLA Modules:
  0.0 305.2 jit_solution(6792024841342456358)
XLA Ops:
  7.2 0.7 all-gather.6.cloned.1.call-update
  7.9 65.9 %all-gather.6.cloned.1.call-done.refs_0_ = f32[16,256,256]{2,1,0:T(8,128)} async-done(((f32[16,32,256]{2,1,0:T(8,128)}), f32[16,256,256]{2,1,0:T(8,128)}) %all-gather.6.cloned.1.call-update) | async-done | bytes 4194320 | tf_op jit(solution)/shard_map/all_gather | solution.py:585
  73.9 20.1 %shard_map.41 = (bf16[16,256,256]{2,1,0:T(8,128)(2,1)}, bf16[16,256,256]{2,1,0:T(8,128)(2,1)}, f32[16,256,256]{2,1,0:T(8,128)}, f32[16,256,256]{2,1,0:T(8,128)},...) custom-call(f32[16,256,256]{2,1,0:T(8,128)} %all-gather.6.cloned.1.call-done.refs_0_, ...), custom_call_target="tpu_custom_call" | custom-call | flops 5234491392 | bytes 18939904 | tf_op jit(solution)/shard_map/pallas_call | solution.py:81
  94.0 0.6 pad_add_fusion.refs_2_.refs_0_.refs_1_
  94.6 4.9 %all-to-all-start = ((f32[8,40,256]{2,1,0:T(8,128)}), f32[8,40,256]{2,1,0:T(8,128)S(1)}, u32[]{:S(2)}, u32[]{:S(2)}) async-start(f32[8,40,256]{2,1,0:T(8,128)} %get-tuple-element.30), calls=%async_computation | async-start | bytes 655360 | tf_op jit(solution)/shard_map/all_to_all | solution.py:573
  99.5 14.6 %shard_map.42 = (f32[16,544,256]{2,1,0:T(8,128)}, f32[544,256]{1,0:T(8,128)}) custom-call(bf16[16,256,256]{2,1,0:T(8,128)(2,1)} %get-tuple-element.24.refs_0_.refs_1_, bf16[16,256,256]{2,1,0:T(8,128)(2,1)} %get-tuple-element.25.refs_1_.refs_2_, f32[16,256,256]{2,1,0:T(8,128)} %get-tuple-element.26.refs_2_, f32[16,256,256]{2,1,0:T(8,128)} %get-tuple-element.27.refs_3_, ...), custom_call_target="tpu_custom_call" | custom-call | flops 3422552064 | bytes 22577152 | tf_op jit(solution)/shard_map/pallas_call | solution.py:81
  114.1 24.7 %all-gather.8.cloned.1.call-done = f32[24,256,256]{2,1,0:T(8,128)} async-done(((f32[3,256,256]{2,1,0:T(8,128)}), f32[24,256,256]{2,1,0:T(8,128)}) %all-gather.8.cloned.1.call-update) | async-done | bytes 6291472 | tf_op jit(solution)/shard_map/all_gather | solution.py:587
  138.9 8.0 %shard_map.43.refs_0_ = f32[3,128,256]{2,1,0:T(8,128)} custom-call(f32[544,256]{1,0:T(8,128)} %get-tuple-element.29.refs_0_.refs_6_, f32[8,40,256]{2,1,0:T(8,128)} %copy-done.1, s32[2]{0:T(128)} %pad_add_fusion.refs_2_.refs_0_.refs_1_, f32[8,3,256,256]{3,2,1,0:T(8,128)} %bitcast.13), custom_call_target="tpu_custom_call" | custom-call | flops 3221225472 | bytes 6684672 | tf_op jit(solution)/shard_map/pallas_call | solution.py:81
  146.9 0.7 pad_add_fusion.1.refs_1_.refs_0_
  147.5 5.9 %shard_map.45 = (f32[2,2,16,256]{3,2,1,0:T(8,128)}, f32[8,40,256]{2,1,0:T(8,128)}) custom-call(s32[2]{0:T(128)} %pad_add_fusion.refs_2_.refs_0_.refs_1_, f32[8,3,256,256]{3,2,1,0:T(8,128)} %bitcast.14, f32[8,40,256]{2,1,0:T(8,128)} %copy-done.1), custom_call_target="tpu_custom_call" | custom-call | flops 150994944 | bytes 7012352 | tf_op jit(solution)/shard_map/pallas_call | solution.py:81
  153.4 6.5 %all-to-all-start.1 = ((f32[8,40,256]{2,1,0:T(8,128)}), f32[8,40,256]{2,1,0:T(8,128)S(1)}, u32[]{:S(2)}, u32[]{:S(2)}) async-start(f32[8,40,256]{2,1,0:T(8,128)} %get-tuple-element.33), calls=%async_computation.1 | async-start | bytes 655360 | tf_op jit(solution)/shard_map/all_to_all | solution.py:573
  159.9 10.4 %shard_map.46.refs_4_.refs_3_ = f32[2,3,256,256]{3,2,1,0:T(8,128)} custom-call(f32[3,128,256]{2,1,0:T(8,128)} %shard_map.43.refs_0_, s32[2]{0:T(128)} %pad_add_fusion.refs_2_.refs_0_.refs_1_, f32[8,3,256,256]{3,2,1,0:T(8,128)} %bitcast.15), custom_call_target="tpu_custom_call" | custom-call | flops 3221225472 | bytes 7864320 | tf_op jit(solution)/shard_map/pallas_call | solution.py:81
  170.3 12.1 %shard_map.44.refs_0_.refs_7_ = f32[544,256]{1,0:T(8,128)} custom-call(f32[3,128,256]{2,1,0:T(8,128)} %shard_map.43.refs_0_, bf16[16,256,256]{2,1,0:T(8,128)(2,1)} %get-tuple-element.24.refs_0_.refs_1_, bf16[16,256,256]{2,1,0:T(8,128)(2,1)} %get-tuple-element.25.refs_1_.refs_2_, f32[16,544,256]{2,1,0:T(8,128)} %get-tuple-element.32.refs_3_), custom_call_target="tpu_custom_call" | custom-call | flops 3422552064 | bytes 13664256 | tf_op jit(solution)/shard_map/pallas_call | solution.py:81
  182.4 19.9 %all-gather.10.cloned.1.call-done = f32[48,128,256]{2,1,0:T(8,128)} async-done(((f32[3,128,256]{2,1,0:T(8,128)}), f32[48,128,256]{2,1,0:T(8,128)}) %all-gather.10.cloned.1.call-update) | async-done | bytes 6291472 | tf_op jit(solution)/shard_map/all_gather | solution.py:591
  202.3 6.5 %shard_map.47 = (f32[2,16,256]{2,1,0:T(8,128)}, f32[2,16,256]{2,1,0:T(8,128)}, f32[8,256]{1,0:T(8,128)}) custom-call(f32[544,256]{1,0:T(8,128)} %shard_map.44.refs_0_.refs_7_, s32[2]{0:T(128)} %pad_add_fusion.1.refs_1_.refs_0_, f32[16,3,128,256]{3,2,1,0:T(8,128)} %bitcast.11, f32[8,40,256]{2,1,0:T(8,128)} %copy-done, ...), custom_call_target="tpu_custom_call" | custom-call | flops 150994944 | bytes 8331264 | tf_op jit(solution)/shard_map/pallas_call | solution.py:81
  208.9 2.2 collective-permute-start
  211.0 1.1 collective-permute-done.refs_5_
  212.2 0.6 copy-done.3
  212.8 9.6 %shard_map.48 = (f32[16,32,256]{2,1,0:T(8,128)}, f32[8,40,256]{2,1,0:T(8,128)}) custom-call(s32[2]{0:T(128)} %pad_add_fusion.refs_2_.refs_0_.refs_1_, bf16[16,256,256]{2,1,0:T(8,128)(2,1)} %get-tuple-element.24.refs_0_.refs_1_, bf16[16,256,256]{2,1,0:T(8,128)(2,1)} %get-tuple-element.25.refs_1_.refs_2_, f32[16,32,256]{2,1,0:T(8,128)} %refs_3_.1, ...), custom_call_target="tpu_custom_call" | custom-call | flops 402653184 | bytes 6750208 | tf_op jit(solution)/shard_map/pallas_call | solution.py:81
  222.4 11.8 %all_to_all.30.refs_2_ = f32[8,40,256]{2,1,0:T(8,128)} all-to-all(f32[8,40,256]{2,1,0:T(8,128)} %get-tuple-element.38), channel_id=1, replica_groups=mesh['outer'=8,'mid'=4,'core'=2,'cols'=8] {'mid','core'}, dimensions={0} | all-to-all | bytes 655360 | tf_op jit(solution)/shard_map/all_to_all | solution.py:573
  234.2 5.9 %shard_map.49 = (f32[2,2,16,256]{3,2,1,0:T(8,128)}, f32[8,40,256]{2,1,0:T(8,128)}) custom-call(s32[2]{0:T(128)} %pad_add_fusion.refs_2_.refs_0_.refs_1_, f32[8,3,256,256]{3,2,1,0:T(8,128)} %bitcast.16, f32[8,40,256]{2,1,0:T(8,128)} %all_to_all.30.refs_2_), custom_call_target="tpu_custom_call" | custom-call | flops 150994944 | bytes 7012352 | tf_op jit(solution)/shard_map/pallas_call | solution.py:81
  240.1 15.7 %all_to_all.31.refs_2_ = f32[8,40,256]{2,1,0:T(8,128)} all-to-all(f32[8,40,256]{2,1,0:T(8,128)} %get-tuple-element.39), channel_id=1, replica_groups=mesh['outer'=8,'mid'=4,'core'=2,'cols'=8] {'outer'}, dimensions={0} | all-to-all | bytes 655360 | tf_op jit(solution)/shard_map/all_to_all | solution.py:573
  255.9 6.5 %shard_map.50 = (f32[2,16,256]{2,1,0:T(8,128)}, f32[2,16,256]{2,1,0:T(8,128)}, f32[8,256]{1,0:T(8,128)}) custom-call(s32[2]{0:T(128)} %pad_add_fusion.1.refs_1_.refs_0_, f32[16,3,128,256]{3,2,1,0:T(8,128)} %bitcast.12, f32[8,40,256]{2,1,0:T(8,128)} %all_to_all.31.refs_2_, f32[2,3,256,256]{3,2,1,0:T(8,128)} %shard_map.46.refs_4_.refs_3_, ...), custom_call_target="tpu_custom_call" | custom-call | flops 150994944 | bytes 8331264 | tf_op jit(solution)/shard_map/pallas_call | solution.py:81
  262.4 4.8 %collective-permute-start.1 = (f32[2,16,256]{2,1,0:T(8,128)}, f32[2,16,256]{2,1,0:T(8,128)S(1)}, u32[]{:S(2)}, u32[]{:S(2)}) collective-permute-start(f32[2,16,256]{2,1,0:T(8,128)} %get-tuple-element.42), channel_id=1, source_target_pairs={{0,8},{8,0},{1,9},{9,1},{2,10},{10,2},{3,11},{11,3},{4,12},{12,4},... | collective-permute-start | bytes 98312 | tf_op jit(solution)/shard_map/ppermute | solution.py:613
  267.2 0.7 sqrt_bitcast_fusion.1
  267.9 0.7 copy.8.refs_6_
  268.6 0.6 copy-done.2
  269.2 9.1 %shard_map.51 = (f32[16,32,256]{2,1,0:T(8,128)}, f32[8,8,128]{2,1,0:T(8,128)}) custom-call(s32[2]{0:T(128)} %pad_add_fusion.refs_2_.refs_0_.refs_1_, bf16[16,256,256]{2,1,0:T(8,128)(2,1)} %get-tuple-element.24.refs_0_.refs_1_, bf16[16,256,256]{2,1,0:T(8,128)(2,1)} %get-tuple-element.25.refs_1_.refs_2_, f32[16,32,256]{2,1,0:T(8,128)} %get-tuple-element.37.refs_3_, ...), custom_call_target="tpu_custom_call" | custom-call | flops 402653184 | bytes 5341312 | tf_op jit(solution)/shard_map/pallas_call | solution.py:81
  278.2 8.0 %all_to_all.32 = f32[8,8,128]{2,1,0:T(8,128)S(1)} all-to-all(f32[8,8,128]{2,1,0:T(8,128)} %get-tuple-element.45), channel_id=1, replica_groups=mesh['outer'=8,'mid'=4,'core'=2,'cols'=8] {'mid','core'}, dimensions={0} | all-to-all | bytes 65536 | tf_op jit(solution)/shard_map/all_to_all | solution.py:573
  286.2 9.2 %all_to_all.33 = f32[8,8,128]{2,1,0:T(8,128)S(1)} all-to-all(f32[8,8,128]{2,1,0:T(8,128)S(1)} %broadcast_in_dim.2), channel_id=1, replica_groups=mesh['outer'=8,'mid'=4,'core'=2,'cols'=8] {'outer'}, dimensions={0} | all-to-all | bytes 65536 | tf_op jit(solution)/shard_map/all_to_all | solution.py:573
  296.0 0.7 copy.9.refs_1_
  296.7 1.9 shard_map.52
  (18 shorter events, 0.7 us)
Async XLA Ops:
  7.2 66.7 %all-gather.6.cloned.1.call-start = ((), (), s32[]{:S(2)}) async-start(), calls=%async_computation.6 | async-start | bytes 4718592 | tf_op jit(solution)/shard_map/all_gather | solution.py:585
  7.9 131.0 %all-gather.8.cloned.1.call-start = ((), (), s32[]{:S(2)}) async-start(), calls=%async_computation.7 | async-start | bytes 7077888 | tf_op jit(solution)/shard_map/all_gather | solution.py:587
  94.6 19.6 %all-to-all-start = ((f32[8,40,256]{2,1,0:T(8,128)}), f32[8,40,256]{2,1,0:T(8,128)S(1)}, u32[]{:S(2)}, u32[]{:S(2)}) async-start(f32[8,40,256]{2,1,0:T(8,128)} %get-tuple-element.30), calls=%async_computation | async-start | bytes 655360 | tf_op jit(solution)/shard_map/all_to_all | solution.py:573
  99.5 102.8 %all-gather.10.cloned.1.call-start = ((), (), s32[]{:S(2)}) async-start(), calls=%async_computation.8 | async-start | bytes 6684672 | tf_op jit(solution)/shard_map/all_gather | solution.py:591
  114.1 24.7 %copy-start.1 = (f32[8,40,256]{2,1,0:T(8,128)}, f32[8,40,256]{2,1,0:T(8,128)S(1)}, u32[]{:S(2)}) copy-start(f32[8,40,256]{2,1,0:T(8,128)S(1)} %all-to-all-done.refs_1_.refs_2_) | copy-start | bytes 983044
  153.4 29.0 %all-to-all-start.1 = ((f32[8,40,256]{2,1,0:T(8,128)}), f32[8,40,256]{2,1,0:T(8,128)S(1)}, u32[]{:S(2)}, u32[]{:S(2)}) async-start(f32[8,40,256]{2,1,0:T(8,128)} %get-tuple-element.33), calls=%async_computation.1 | async-start | bytes 655360 | tf_op jit(solution)/shard_map/all_to_all | solution.py:573
  182.4 19.9 %copy-start = (f32[8,40,256]{2,1,0:T(8,128)}, f32[8,40,256]{2,1,0:T(8,128)S(1)}, u32[]{:S(2)}) copy-start(f32[8,40,256]{2,1,0:T(8,128)S(1)} %all-to-all-done.1.refs_3_) | copy-start | bytes 983044
  208.9 3.3 %collective-permute-start = (f32[2,16,256]{2,1,0:T(8,128)}, f32[2,16,256]{2,1,0:T(8,128)S(1)}, u32[]{:S(2)}, u32[]{:S(2)}) collective-permute-start(f32[2,16,256]{2,1,0:T(8,128)} %get-tuple-element.36), channel_id=1, source_target_pairs={{0,8},{8,0},{1,9},{9,1},{2,10},{10,2},{3,11},{11,3},{4,12},{12,4},... | collective-permute-start | bytes 98312 | tf_op jit(solution)/shard_map/ppermute | solution.py:604
  212.2 0.6 copy-start.3
  262.4 6.2 %collective-permute-start.1 = (f32[2,16,256]{2,1,0:T(8,128)}, f32[2,16,256]{2,1,0:T(8,128)S(1)}, u32[]{:S(2)}, u32[]{:S(2)}) collective-permute-start(f32[2,16,256]{2,1,0:T(8,128)} %get-tuple-element.42), channel_id=1, source_target_pairs={{0,8},{8,0},{1,9},{9,1},{2,10},{10,2},{3,11},{11,3},{4,12},{12,4},... | collective-permute-start | bytes 98312 | tf_op jit(solution)/shard_map/ppermute | solution.py:613
  268.6 0.6 copy-start.2
Sparse Core Ops, SparseCore 0:
  10.1 63.7 all-gather.5
  94.1 44.7 all-gather.7
  147.0 55.3 all-gather.9

commit v8 on v6

--- a/solution.py
+++ b/solution.py
@@ -62,50 +62,38 @@
     return jax.ShapeDtypeStruct(dims, dtype)
 
 
-def prepare_body(factors, source, high, low, suffix, cross, solved, operators, ends, prefix, forward, ahead, behind):
+def prepare_body(factors, source, high, low, prefix, forward, operators, ends, ahead, back, behind):
     rows, width, _ = factors.shape
     count = source.shape[1]
-
-    def turn(i, _):
-        high[i], low[i] = split(factors[i].T)
-        return 0
-
-    lax.fori_loop(0, rows, turn, 0)
-    eye = identity(width)
     ahead[:count] = jnp.zeros((count, width), jnp.float32)
-    ahead[count:] = eye
-    behind[...] = eye
+    ahead[count:] = identity(width)
+    behind[...] = jnp.zeros_like(behind)
+    back[0], back[1] = split(identity(width))
 
     def step(i, _):
-        j = rows - 1 - i
-        moved = apply_split(ahead[...], high[i], low[i])
-        back = apply_split(behind[...], high[j], low[j])
+        turned = split(factors[i].T)
+        high[i], low[i] = turned
+        both = jnp.dot(
+            jnp.concatenate(turned, axis=0), back[0], preferred_element_type=jnp.float32
+        )
+        through = (both[:width] + both[width:]) + jnp.dot(
+            turned[0], back[1], preferred_element_type=jnp.float32
+        )
+        moved = apply_split(ahead[...], *turned)
         state = moved[:count] + source[i]
         forward[i] = state
         prefix[i] = moved[count:]
         ahead[:count] = state
         ahead[count:] = moved[count:]
-        suffix[j] = back
-        behind[...] = back
+        back[0], back[1] = split(through)
+        operators[1] = through
+        behind[...] += apply_split(ahead[...], back[0], back[1])
         return 0
 
-    lax.fori_loop(0, rows, step, 0)
+    lax.fori_loop(0, rows, step, 0, unroll=8)
     operators[0] = ahead[count:]
-    operators[1] = behind[...]
-    ahead[...] = jnp.zeros_like(ahead)
-
-    def back(i, _):
-        j = rows - 1 - i
-        entering = jnp.concatenate([forward[j], prefix[j]], axis=0) + ahead[...]
-        state = apply_split(entering, high[j], low[j])
-        ahead[...] = state
-        solved[j] = state[:count]
-        cross[j] = state[count:]
-        return 0
-
-    lax.fori_loop(0, rows, back, 0)
-    operators[2] = ahead[count:]
-    put_messages(ends, forward[rows - 1], ahead[:count], None)
+    operators[2] = behind[count:]
+    put_messages(ends, ahead[:count], behind[:count], None)
 
 
 def prepare(factors, source, copies):
@@ -117,17 +105,15 @@
         [
             shape(*square, dtype=jnp.bfloat16),
             shape(*square, dtype=jnp.bfloat16),
-            shape(*square),
             shape(*square),
             shape(*source.shape),
             shape(3, width, width),
             shape(copies, count + 8, width),
         ],
         [
-            pltpu.VMEM(square, jnp.float32),
-            pltpu.VMEM(source.shape, jnp.float32),
             pltpu.VMEM((count + width, width), jnp.float32),
-            pltpu.VMEM((width, width), jnp.float32),
+            pltpu.VMEM((2, width, width), jnp.bfloat16),
+            pltpu.VMEM((count + width, width), jnp.float32),
         ],
         rows * 6 * (2 * count + 3 * width) * width * width,
         factors,
@@ -135,13 +121,26 @@
     )
 
 
-def ahead_body(high, low, cross, suffix, solved, rows_out, ends):
-    rows, count, width = solved.shape
+def ahead_body(high, low, prefix, forward, rows_out, ends):
+    rows, count, width = forward.shape
+    zero = jnp.zeros((width, width), jnp.float32)
+    ends[:width] = zero
+    ends[width : 2 * width] = identity(width)
+    ends[2 * width :] = jnp.zeros((count, width), jnp.float32)
+
+    def back(i, _):
+        j = rows - 1 - i
+        source = jnp.concatenate([prefix[j], zero, forward[j]], axis=0)
+        state = apply_split(source + ends[...], high[j], low[j])
+        ends[...] = state
+        rows_out[j] = state
+        return 0
+
+    lax.fori_loop(0, rows, back, 0)
     ends[...] = jnp.zeros_like(ends)
 
     def step(i, _):
-        source = jnp.concatenate([cross[i], suffix[i], solved[i]], axis=0)
-        state = apply_split(ends[...], high[i], low[i]) + source
+        state = apply_split(ends[...], high[i], low[i]) + rows_out[i]
         ends[...] = state
         rows_out[i] = state
         return 0
@@ -161,19 +160,18 @@
     lax.fori_loop(0, rows, step, 0)
 
 
-def respond_ahead(high, low, cross, suffix, solved):
-    rows, count, width = solved.shape
+def respond_ahead(high, low, prefix, forward):
+    rows, count, width = forward.shape
     length = 2 * width + count
     return call(
         ahead_body,
         [shape(rows, length, width), shape(length, width)],
         [],
-        rows * 6 * length * width * width,
+        2 * rows * 6 * length * width * width,
         high,
         low,
-        cross,
-        suffix,
-        solved,
+        prefix,
+        forward,
     )
 
 
@@ -425,7 +423,7 @@
         forward[i] = state
         return state
 
-    lax.fori_loop(0, rows, ahead, entering[0], unroll=2)
+    lax.fori_loop(0, rows, ahead, entering[0], unroll=8)
 
     def behind(i, carry):
         state, total = carry
@@ -435,7 +433,7 @@
         return state, total + state * state
 
     zero = jnp.zeros((count, width), jnp.float32)
-    _, total = lax.fori_loop(0, rows, behind, (entering[1], zero), unroll=2)
+    _, total = lax.fori_loop(0, rows, behind, (entering[1], zero), unroll=8)
     parts = [
         ends[2 * width :]
         + apply_split(entering[0], *split(ends[:width]))
@@ -473,7 +471,7 @@
         forward[i] = state
         return state
 
-    lax.fori_loop(0, rows, ahead, entering[0], unroll=2)
+    lax.fori_loop(0, rows, ahead, entering[0], unroll=8)
 
     def behind(i, carry):
         state, total = carry
@@ -484,7 +482,7 @@
         return state, total + value * value
 
     zero = jnp.zeros((count, width), jnp.float32)
-    _, total = lax.fori_loop(0, rows, behind, (entering[1], zero), unroll=2)
+    _, total = lax.fori_loop(0, rows, behind, (entering[1], zero), unroll=8)
     squares[...] = jnp.zeros(squares.shape, jnp.float32)
     sums = row_sums(total)
     for member in range(squares.shape[0]):
@@ -530,10 +528,10 @@
     cross_core = functools.partial(lax.ppermute, axis_name="core", perm=[(0, 1), (1, 0)])
 
     whole = lax.all_gather(factors, "cols", axis=1, tiled=True)
-    high, low, suffix, cross, solved, operators, ends = prepare(whole, start_vectors, members)
+    high, low, prefix, local, operators, ends = prepare(whole, start_vectors, members)
     near_spans = lax.all_gather(operators, INNER)
     near_ends = swap(ends, INNER)
-    ahead_rows, ahead_ends = respond_ahead(high, low, cross, suffix, solved)
+    ahead_rows, ahead_ends = respond_ahead(high, low, prefix, local)
     half = compose(near_place, near_spans, (ahead_ends, near_ends))
     far_spans = lax.all_gather(half, ("outer", "core"))
     inner, message = near(near_place, near_spans, near_ends, groups)

time: 304 us -> 295 us (0.970)
  waiting for transfers between devices: 112 us -> 107 us
  Pallas kernels: 109 us -> 105 us
    all_gather x1, waiting for transfers between devices: 24.7 us -> 19.5 us  [shards(): near_spans = lax.all_gather(operators, INNER)]
    pallas_call x12, Pallas kernels: 109 us -> 105 us  [call(): pl.pallas_call(kernel, out_shape=tuple(out_shapes), in_specs=specs, out_s...]
  transfers between devices with their start and end apart: 7 -> 7, of which waited for: 4 -> 4; matrix products, arithmetic and copies ran while one was open for 1% -> 1% of each run, Pallas kernels for 14% -> 16%
where the time goes in v8:
time: 295 us
  waiting for transfers between devices  107 us (36%)
  Pallas kernels  105 us (36%)
  blocking collectives  44.7 us (15%)
  starting transfers between devices  18.6 us (6%)
  between operations  13.8 us (5%)
    pallas_call x12, Pallas kernels, call(): pl.pallas_call(kernel, out_shape=tuple(out_shapes), in_specs=specs, out_s...  105 us
    all_gather x1, waiting for transfers between devices, shards(): whole = lax.all_gather(factors, 'cols', axis=1, tiled=True)  65.9 us
    all_to_all x4, blocking collectives, swap(): return lax.all_to_all(value, axis, 0, 0, tiled=True)  44.7 us
    all_gather x1, waiting for transfers between devices, shards(): far_spans = lax.all_gather(half, ('outer', 'core'))  19.9 us
    all_gather x1, waiting for transfers between devices, shards(): near_spans = lax.all_gather(operators, INNER)  19.5 us
    all_to_all x2, starting transfers between devices, swap(): return lax.all_to_all(value, axis, 0, 0, tiled=True)  11.4 us
    ppermute x2, starting transfers between devices, shards(): cross_core(theirs)  7.13 us
  transfers between devices with their start and end apart: 7, of which 4 were waited for; matrix products, arithmetic and copies ran while one was open for 1% of the time, Pallas kernels for 16%

profile of v8, /device:TPU:1, one launch (start us, length us, event | category | flops | bytes accessed | tf_op | source)
XLA Modules:
  0.0 294.6 jit_solution(1996541955065920196)
XLA Ops:
  7.2 0.7 all-gather.6.cloned.1.call-update
  7.9 65.9 %all-gather.6.cloned.1.call-done.factors = f32[16,256,256]{2,1,0:T(8,128)} async-done(((f32[16,32,256]{2,1,0:T(8,128)}), f32[16,256,256]{2,1,0:T(8,128)}) %all-gather.6.cloned.1.call-update) | async-done | bytes 4194320 | tf_op jit(solution)/shard_map/all_gather | solution.py:530
  73.9 12.6 %shard_map.41 = (bf16[16,256,256]{2,1,0:T(8,128)(2,1)}, bf16[16,256,256]{2,1,0:T(8,128)(2,1)}, f32[16,256,256]{2,1,0:T(8,128)}, f32[16,32,256]{2,1,0:T(8,128)}, ...) custom-call(f32[16,256,256]{2,1,0:T(8,128)} %all-gather.6.cloned.1.call-done.factors, f32[16,32,256]{2,1,0:T(8,128)} %source.3), custom_call_target="tpu_custom_call" | custom-call | flops 5234491392 | bytes 14745600 | tf_op jit(solution)/shard_map/pallas_call | solution.py:50
  86.5 0.6 pad_add_fusion.refs_2_.place.refs_1_
  87.1 4.9 %all-to-all-start = ((f32[8,40,256]{2,1,0:T(8,128)}), f32[8,40,256]{2,1,0:T(8,128)S(1)}, u32[]{:S(2)}, u32[]{:S(2)}) async-start(f32[8,40,256]{2,1,0:T(8,128)} %get-tuple-element.28), calls=%async_computation | async-start | bytes 655360 | tf_op jit(solution)/shard_map/all_to_all | solution.py:518
  92.0 19.9 %shard_map.42 = (f32[16,544,256]{2,1,0:T(8,128)}, f32[544,256]{1,0:T(8,128)}) custom-call(bf16[16,256,256]{2,1,0:T(8,128)(2,1)} %get-tuple-element.23.high.refs_1_, bf16[16,256,256]{2,1,0:T(8,128)(2,1)} %get-tuple-element.24.low.refs_2_, f32[16,256,256]{2,1,0:T(8,128)} %get-tuple-element.25.prefix, f32[16,32,256]{2,1,0:T(8,128)} %get-tuple-element.26.forward), custom_call_target="tpu_custom_call" | custom-call | flops 6845104128 | bytes 18382848 | tf_op jit(solution)/shard_map/pallas_call | solution.py:50
  111.9 19.5 %all-gather.8.cloned.1.call-done = f32[24,256,256]{2,1,0:T(8,128)} async-done(((f32[3,256,256]{2,1,0:T(8,128)}), f32[24,256,256]{2,1,0:T(8,128)}) %all-gather.8.cloned.1.call-update) | async-done | bytes 6291472 | tf_op jit(solution)/shard_map/all_gather | solution.py:532
  131.4 7.4 %shard_map.43.refs_0_ = f32[3,128,256]{2,1,0:T(8,128)} custom-call(f32[544,256]{1,0:T(8,128)} %get-tuple-element.27.refs_0_.ahead_ends, f32[8,40,256]{2,1,0:T(8,128)} %copy-done.1, s32[2]{0:T(128)} %pad_add_fusion.refs_2_.place.refs_1_, f32[8,3,256,256]{3,2,1,0:T(8,128)} %bitcast.13), custom_call_target="tpu_custom_call" | custom-call | flops 3221225472 | bytes 6684672 | tf_op jit(solution)/shard_map/pallas_call | solution.py:50
  138.8 0.6 pad_add_fusion.1.refs_1_.place
  139.4 5.7 %shard_map.45 = (f32[2,2,16,256]{3,2,1,0:T(8,128)}, f32[8,40,256]{2,1,0:T(8,128)}) custom-call(s32[2]{0:T(128)} %pad_add_fusion.refs_2_.place.refs_1_, f32[8,3,256,256]{3,2,1,0:T(8,128)} %bitcast.14, f32[8,40,256]{2,1,0:T(8,128)} %copy-done.1), custom_call_target="tpu_custom_call" | custom-call | flops 150994944 | bytes 7012352 | tf_op jit(solution)/shard_map/pallas_call | solution.py:50
  145.1 6.5 %all-to-all-start.1 = ((f32[8,40,256]{2,1,0:T(8,128)}), f32[8,40,256]{2,1,0:T(8,128)S(1)}, u32[]{:S(2)}, u32[]{:S(2)}) async-start(f32[8,40,256]{2,1,0:T(8,128)} %get-tuple-element.31), calls=%async_computation.1 | async-start | bytes 655360 | tf_op jit(solution)/shard_map/all_to_all | solution.py:518
  151.5 10.4 %shard_map.46.refs_4_.own = f32[2,3,256,256]{3,2,1,0:T(8,128)} custom-call(f32[3,128,256]{2,1,0:T(8,128)} %shard_map.43.refs_0_, s32[2]{0:T(128)} %pad_add_fusion.refs_2_.place.refs_1_, f32[8,3,256,256]{3,2,1,0:T(8,128)} %bitcast.15), custom_call_target="tpu_custom_call" | custom-call | flops 3221225472 | bytes 7864320 | tf_op jit(solution)/shard_map/pallas_call | solution.py:50
  161.9 12.1 %shard_map.44.refs_0_.behind_ends = f32[544,256]{1,0:T(8,128)} custom-call(f32[3,128,256]{2,1,0:T(8,128)} %shard_map.43.refs_0_, bf16[16,256,256]{2,1,0:T(8,128)(2,1)} %get-tuple-element.23.high.refs_1_, bf16[16,256,256]{2,1,0:T(8,128)(2,1)} %get-tuple-element.24.low.refs_2_, f32[16,544,256]{2,1,0:T(8,128)} %get-tuple-element.30.refs_3_), custom_call_target="tpu_custom_call" | custom-call | flops 3422552064 | bytes 13664256 | tf_op jit(solution)/shard_map/pallas_call | solution.py:50
  174.0 19.9 %all-gather.10.cloned.1.call-done = f32[48,128,256]{2,1,0:T(8,128)} async-done(((f32[3,128,256]{2,1,0:T(8,128)}), f32[48,128,256]{2,1,0:T(8,128)}) %all-gather.10.cloned.1.call-update) | async-done | bytes 6291472 | tf_op jit(solution)/shard_map/all_gather | solution.py:536
  194.0 6.3 %shard_map.47 = (f32[2,16,256]{2,1,0:T(8,128)}, f32[2,16,256]{2,1,0:T(8,128)}, f32[8,256]{1,0:T(8,128)}) custom-call(f32[544,256]{1,0:T(8,128)} %shard_map.44.refs_0_.behind_ends, s32[2]{0:T(128)} %pad_add_fusion.1.refs_1_.place, f32[16,3,128,256]{3,2,1,0:T(8,128)} %bitcast.11, f32[8,40,256]{2,1,0:T(8,128)} %copy-done, ...), custom_call_target="tpu_custom_call" | custom-call | flops 150994944 | bytes 8331264 | tf_op jit(solution)/shard_map/pallas_call | solution.py:50
  200.3 2.3 collective-permute-start
  202.7 1.0 collective-permute-done.theirs
  203.6 0.6 copy-done.3
  204.2 8.8 %shard_map.48 = (f32[16,32,256]{2,1,0:T(8,128)}, f32[8,40,256]{2,1,0:T(8,128)}) custom-call(s32[2]{0:T(128)} %pad_add_fusion.refs_2_.place.refs_1_, bf16[16,256,256]{2,1,0:T(8,128)(2,1)} %get-tuple-element.23.high.refs_1_, bf16[16,256,256]{2,1,0:T(8,128)(2,1)} %get-tuple-element.24.low.refs_2_, f32[16,32,256]{2,1,0:T(8,128)} %source.3, ...), custom_call_target="tpu_custom_call" | custom-call | flops 402653184 | bytes 6750208 | tf_op jit(solution)/shard_map/pallas_call | solution.py:50
  213.0 11.8 %all_to_all.30.ends = f32[8,40,256]{2,1,0:T(8,128)} all-to-all(f32[8,40,256]{2,1,0:T(8,128)} %get-tuple-element.36), channel_id=1, replica_groups=mesh['outer'=8,'mid'=4,'core'=2,'cols'=8] {'mid','core'}, dimensions={0} | all-to-all | bytes 655360 | tf_op jit(solution)/shard_map/all_to_all | solution.py:518
  224.9 5.7 %shard_map.49 = (f32[2,2,16,256]{3,2,1,0:T(8,128)}, f32[8,40,256]{2,1,0:T(8,128)}) custom-call(s32[2]{0:T(128)} %pad_add_fusion.refs_2_.place.refs_1_, f32[8,3,256,256]{3,2,1,0:T(8,128)} %bitcast.16, f32[8,40,256]{2,1,0:T(8,128)} %all_to_all.30.ends), custom_call_target="tpu_custom_call" | custom-call | flops 150994944 | bytes 7012352 | tf_op jit(solution)/shard_map/pallas_call | solution.py:50
  230.6 15.7 %all_to_all.31.ends = f32[8,40,256]{2,1,0:T(8,128)} all-to-all(f32[8,40,256]{2,1,0:T(8,128)} %get-tuple-element.37), channel_id=1, replica_groups=mesh['outer'=8,'mid'=4,'core'=2,'cols'=8] {'outer'}, dimensions={0} | all-to-all | bytes 655360 | tf_op jit(solution)/shard_map/all_to_all | solution.py:518
  246.3 6.4 %shard_map.50 = (f32[2,16,256]{2,1,0:T(8,128)}, f32[2,16,256]{2,1,0:T(8,128)}, f32[8,256]{1,0:T(8,128)}) custom-call(s32[2]{0:T(128)} %pad_add_fusion.1.refs_1_.place, f32[16,3,128,256]{3,2,1,0:T(8,128)} %bitcast.12, f32[8,40,256]{2,1,0:T(8,128)} %all_to_all.31.ends, f32[2,3,256,256]{3,2,1,0:T(8,128)} %shard_map.46.refs_4_.own, ...), custom_call_target="tpu_custom_call" | custom-call | flops 150994944 | bytes 8331264 | tf_op jit(solution)/shard_map/pallas_call | solution.py:50
  252.6 4.8 %collective-permute-start.1 = (f32[2,16,256]{2,1,0:T(8,128)}, f32[2,16,256]{2,1,0:T(8,128)S(1)}, u32[]{:S(2)}, u32[]{:S(2)}) collective-permute-start(f32[2,16,256]{2,1,0:T(8,128)} %get-tuple-element.40), channel_id=1, source_target_pairs={{0,8},{8,0},{1,9},{9,1},{2,10},{10,2},{3,11},{11,3},{4,12},{12,4},... | collective-permute-start | bytes 98312 | tf_op jit(solution)/shard_map/ppermute | solution.py:558
  257.4 0.7 sqrt_bitcast_fusion.1
  258.1 0.7 copy.8.scale
  258.8 0.6 copy-done.2
  259.4 8.3 %shard_map.51 = (f32[16,32,256]{2,1,0:T(8,128)}, f32[8,8,128]{2,1,0:T(8,128)}) custom-call(s32[2]{0:T(128)} %pad_add_fusion.refs_2_.place.refs_1_, bf16[16,256,256]{2,1,0:T(8,128)(2,1)} %get-tuple-element.23.high.refs_1_, bf16[16,256,256]{2,1,0:T(8,128)(2,1)} %get-tuple-element.24.low.refs_2_, f32[16,32,256]{2,1,0:T(8,128)} %get-tuple-element.35.source, ...), custom_call_target="tpu_custom_call" | custom-call | flops 402653184 | bytes 5341312 | tf_op jit(solution)/shard_map/pallas_call | solution.py:50
  267.7 7.9 %all_to_all.32 = f32[8,8,128]{2,1,0:T(8,128)S(1)} all-to-all(f32[8,8,128]{2,1,0:T(8,128)} %get-tuple-element.43), channel_id=1, replica_groups=mesh['outer'=8,'mid'=4,'core'=2,'cols'=8] {'mid','core'}, dimensions={0} | all-to-all | bytes 65536 | tf_op jit(solution)/shard_map/all_to_all | solution.py:518
  275.7 9.2 %all_to_all.33 = f32[8,8,128]{2,1,0:T(8,128)S(1)} all-to-all(f32[8,8,128]{2,1,0:T(8,128)S(1)} %broadcast_in_dim.2), channel_id=1, replica_groups=mesh['outer'=8,'mid'=4,'core'=2,'cols'=8] {'outer'}, dimensions={0} | all-to-all | bytes 65536 | tf_op jit(solution)/shard_map/all_to_all | solution.py:518
  285.4 0.7 copy.9.scale
  286.1 1.9 shard_map.52
  (18 shorter events, 0.7 us)
Async XLA Ops:
  7.2 66.7 %all-gather.6.cloned.1.call-start = ((), (), s32[]{:S(2)}) async-start(), calls=%async_computation.6 | async-start | bytes 4718592 | tf_op jit(solution)/shard_map/all_gather | solution.py:530
  7.9 123.5 %all-gather.8.cloned.1.call-start = ((), (), s32[]{:S(2)}) async-start(), calls=%async_computation.7 | async-start | bytes 7077888 | tf_op jit(solution)/shard_map/all_gather | solution.py:532
  87.1 24.8 %all-to-all-start = ((f32[8,40,256]{2,1,0:T(8,128)}), f32[8,40,256]{2,1,0:T(8,128)S(1)}, u32[]{:S(2)}, u32[]{:S(2)}) async-start(f32[8,40,256]{2,1,0:T(8,128)} %get-tuple-element.28), calls=%async_computation | async-start | bytes 655360 | tf_op jit(solution)/shard_map/all_to_all | solution.py:518
  92.0 101.9 %all-gather.10.cloned.1.call-start = ((), (), s32[]{:S(2)}) async-start(), calls=%async_computation.8 | async-start | bytes 6684672 | tf_op jit(solution)/shard_map/all_gather | solution.py:536
  111.9 19.5 %copy-start.1 = (f32[8,40,256]{2,1,0:T(8,128)}, f32[8,40,256]{2,1,0:T(8,128)S(1)}, u32[]{:S(2)}) copy-start(f32[8,40,256]{2,1,0:T(8,128)S(1)} %all-to-all-done.refs_1_.ends) | copy-start | bytes 983044
  145.1 29.0 %all-to-all-start.1 = ((f32[8,40,256]{2,1,0:T(8,128)}), f32[8,40,256]{2,1,0:T(8,128)S(1)}, u32[]{:S(2)}, u32[]{:S(2)}) async-start(f32[8,40,256]{2,1,0:T(8,128)} %get-tuple-element.31), calls=%async_computation.1 | async-start | bytes 655360 | tf_op jit(solution)/shard_map/all_to_all | solution.py:518
  174.0 19.9 %copy-start = (f32[8,40,256]{2,1,0:T(8,128)}, f32[8,40,256]{2,1,0:T(8,128)S(1)}, u32[]{:S(2)}) copy-start(f32[8,40,256]{2,1,0:T(8,128)S(1)} %all-to-all-done.1.refs_3_) | copy-start | bytes 983044
  200.3 3.3 %collective-permute-start = (f32[2,16,256]{2,1,0:T(8,128)}, f32[2,16,256]{2,1,0:T(8,128)S(1)}, u32[]{:S(2)}, u32[]{:S(2)}) collective-permute-start(f32[2,16,256]{2,1,0:T(8,128)} %get-tuple-element.34), channel_id=1, source_target_pairs={{0,8},{8,0},{1,9},{9,1},{2,10},{10,2},{3,11},{11,3},{4,12},{12,4},... | collective-permute-start | bytes 98312 | tf_op jit(solution)/shard_map/ppermute | solution.py:549
  203.6 0.6 copy-start.3
  252.6 6.2 %collective-permute-start.1 = (f32[2,16,256]{2,1,0:T(8,128)}, f32[2,16,256]{2,1,0:T(8,128)S(1)}, u32[]{:S(2)}, u32[]{:S(2)}) collective-permute-start(f32[2,16,256]{2,1,0:T(8,128)} %get-tuple-element.40), channel_id=1, source_target_pairs={{0,8},{8,0},{1,9},{9,1},{2,10},{10,2},{3,11},{11,3},{4,12},{12,4},... | collective-permute-start | bytes 98312 | tf_op jit(solution)/shard_map/ppermute | solution.py:558
  258.8 0.6 copy-start.2
Sparse Core Ops, SparseCore 0:
  10.1 63.7 all-gather.5
  86.7 44.7 all-gather.7
  138.9 54.9 all-gather.9

commit v9 on v8

--- a/solution.py
+++ b/solution.py
@@ -461,9 +461,9 @@
     )
 
 
-def second_body(place, high, low, source, mine, theirs, scale, result, squares, forward):
+def second_body(cell_count, place, high, low, source, mine, theirs, first_squares, result, squares, forward):
     rows, count, width = source.shape
-    inverse = 1.0 / scale[...]
+    inverse = 1.0 / upright(scale_of(first_squares[:1, :count], cell_count))
     entering = [both_halves(place, mine, theirs, way) for way in range(2)]
 
     def ahead(i, state):
@@ -489,10 +489,10 @@
         squares[member, :, :count] = sums
 
 
-def second_rows(place, high, low, source, mine, theirs, scale, copies):
+def second_rows(place, high, low, source, mine, theirs, first_squares, cell_count, copies):
     rows, count, width = source.shape
     return call(
-        second_body,
+        functools.partial(second_body, cell_count),
         [shape(*source.shape), shape(copies, 8, 128)],
         [pltpu.VMEM(source.shape, jnp.float32)],
         2 * rows * 6 * count * width * width,
@@ -501,17 +501,43 @@
         source,
         mine,
         theirs,
-        scale,
+        first_squares,
         position=place,
     )
 
 
-def scale_body(vectors, scale, result):
-    result[...] = vectors[...] * (1.0 / scale[...])[None]
-
-
-def rescale(vectors, scale):
-    return call(scale_body, [shape(*vectors.shape)], [], vectors.size, vectors, scale)[0]
+def scale_of(squares, cell_count):
+    return jnp.sqrt(squares / cell_count + eps_value)
+
+
+def upright(row):
+    size = row.shape[1]
+    mine = lax.broadcasted_iota(jnp.int32, (size, size), 0) == lax.broadcasted_iota(
+        jnp.int32, (size, size), 1
+    )
+    spread = jnp.where(mine, jnp.broadcast_to(row, (size, size)), 0.0)
+    return jnp.sum(spread, axis=1, keepdims=True)
+
+
+def scale_body(cell_count, vectors, squares, result, growth):
+    count = vectors.shape[1]
+    total = squares[0]
+    for group in range(1, squares.shape[0]):
+        total = total + squares[group]
+    scale = scale_of(total, cell_count)
+    result[...] = vectors[...] * (1.0 / upright(scale[:1, :count]))[None]
+    growth[...] = jnp.log(scale)
+
+
+def rescale(vectors, squares, cell_count):
+    return call(
+        functools.partial(scale_body, cell_count),
+        [shape(*vectors.shape), shape(*squares.shape[1:])],
+        [],
+        vectors.size,
+        vectors,
+        squares,
+    )
 
 
 def swap(value, axis):
@@ -553,15 +579,13 @@
     )
     inner, message = near(near_place, near_spans, swap(message, INNER), groups)
     mine, theirs, squares = far(far_place, far_spans, swap(message, "outer"), own, inner)
-    scale_one = jnp.sqrt(squares[0, :count] / cell_count + eps_value)
     second, squares = second_rows(
-        near_place, high, low, first_solve, mine, cross_core(theirs), scale_one[:, None], members
+        near_place, high, low, first_solve, mine, cross_core(theirs), squares, cell_count, members
     )
     squares = jnp.sum(swap(squares, INNER), axis=0)
     squares = jnp.broadcast_to(squares[None], (groups, *squares.shape))
-    squares = jnp.sum(swap(squares, "outer"), axis=0)
-    scale_two = jnp.sqrt(squares[0, :count] / cell_count + eps_value)
-    return rescale(second, scale_two[:, None]), jnp.log(scale_two)
+    vectors, growth = rescale(second, swap(squares, "outer"), cell_count)
+    return vectors, growth[0, :count]
 
 
 def solution(mesh):

time: 295 us -> 296 us (level)
  transfers between devices with their start and end apart: 7 -> 7, of which waited for: 4 -> 5; matrix products, arithmetic and copies ran while one was open for 1% -> 0% of each run, Pallas kernels for 16% -> 16%
where the time goes in v9:
time: 296 us; the launch traced here: 295 us
  waiting for transfers between devices  108 us (36%)
  Pallas kernels  105 us (35%)
  blocking collectives  45.7 us (15%)
  starting transfers between devices  18.6 us (6%)
  between operations  13.8 us (5%)
    pallas_call x12, Pallas kernels, call(): pl.pallas_call(kernel, out_shape=tuple(out_shapes), in_specs=specs, out_s...  105 us
    all_gather x1, waiting for transfers between devices, shards(): whole = lax.all_gather(factors, 'cols', axis=1, tiled=True)  65.9 us
    all_to_all x4, blocking collectives, swap(): return lax.all_to_all(value, axis, 0, 0, tiled=True)  45.7 us
    all_gather x1, waiting for transfers between devices, shards(): far_spans = lax.all_gather(half, ('outer', 'core'))  20 us
    all_gather x1, waiting for transfers between devices, shards(): near_spans = lax.all_gather(operators, INNER)  19.5 us
    all_to_all x2, starting transfers between devices, swap(): return lax.all_to_all(value, axis, 0, 0, tiled=True)  11.4 us
    ppermute x2, starting transfers between devices, shards(): cross_core(theirs)  7.13 us
  transfers between devices with their start and end apart: 7, of which 5 were waited for; matrix products, arithmetic and copies ran while one was open for 0% of the time, Pallas kernels for 16%

profile of v9, /device:TPU:1, one launch (start us, length us, event | category | flops | bytes accessed | tf_op | source)
XLA Modules:
  0.0 295.3 jit_solution(17042290722314664433)
XLA Ops:
  7.2 0.7 all-gather.6.cloned.1.call-update
  7.9 0.0 all-gather.8.cloned.1.call-start
  7.9 65.9 %all-gather.6.cloned.1.call-done.factors = f32[16,256,256]{2,1,0:T(8,128)} async-done(((f32[16,32,256]{2,1,0:T(8,128)}), f32[16,256,256]{2,1,0:T(8,128)}) %all-gather.6.cloned.1.call-update) | async-done | bytes 4194320 | tf_op jit(solution)/shard_map/all_gather | solution.py:556
  73.9 12.6 %shard_map.41 = (bf16[16,256,256]{2,1,0:T(8,128)(2,1)}, bf16[16,256,256]{2,1,0:T(8,128)(2,1)}, f32[16,256,256]{2,1,0:T(8,128)}, f32[16,32,256]{2,1,0:T(8,128)}, ...) custom-call(f32[16,256,256]{2,1,0:T(8,128)} %all-gather.6.cloned.1.call-done.factors, f32[16,32,256]{2,1,0:T(8,128)} %source.3), custom_call_target="tpu_custom_call" | custom-call | flops 5234491392 | bytes 14745600 | tf_op jit(solution)/shard_map/pallas_call | solution.py:50
  86.5 0.6 pad_add_fusion.refs_2_.place.refs_1_
  87.1 4.9 %all-to-all-start = ((f32[8,40,256]{2,1,0:T(8,128)}), f32[8,40,256]{2,1,0:T(8,128)S(1)}, u32[]{:S(2)}, u32[]{:S(2)}) async-start(f32[8,40,256]{2,1,0:T(8,128)} %get-tuple-element.30), calls=%async_computation | async-start | bytes 655360 | tf_op jit(solution)/shard_map/all_to_all | solution.py:544
  92.0 19.9 %shard_map.42 = (f32[16,544,256]{2,1,0:T(8,128)}, f32[544,256]{1,0:T(8,128)}) custom-call(bf16[16,256,256]{2,1,0:T(8,128)(2,1)} %get-tuple-element.25.high.refs_1_, bf16[16,256,256]{2,1,0:T(8,128)(2,1)} %get-tuple-element.26.low.refs_2_, f32[16,256,256]{2,1,0:T(8,128)} %get-tuple-element.27.prefix, f32[16,32,256]{2,1,0:T(8,128)} %get-tuple-element.28.forward), custom_call_target="tpu_custom_call" | custom-call | flops 6845104128 | bytes 18382848 | tf_op jit(solution)/shard_map/pallas_call | solution.py:50
  111.9 19.5 %all-gather.8.cloned.1.call-done = f32[24,256,256]{2,1,0:T(8,128)} async-done(((f32[3,256,256]{2,1,0:T(8,128)}), f32[24,256,256]{2,1,0:T(8,128)}) %all-gather.8.cloned.1.call-update) | async-done | bytes 6291472 | tf_op jit(solution)/shard_map/all_gather | solution.py:558
  131.4 7.3 %shard_map.43.refs_0_ = f32[3,128,256]{2,1,0:T(8,128)} custom-call(f32[544,256]{1,0:T(8,128)} %get-tuple-element.29.refs_0_.ahead_ends, f32[8,40,256]{2,1,0:T(8,128)} %copy-done.1, s32[2]{0:T(128)} %pad_add_fusion.refs_2_.place.refs_1_, f32[8,3,256,256]{3,2,1,0:T(8,128)} %bitcast.9), custom_call_target="tpu_custom_call" | custom-call | flops 3221225472 | bytes 6684672 | tf_op jit(solution)/shard_map/pallas_call | solution.py:50
  138.8 0.6 pad_add_fusion.1.refs_1_.place
  139.4 5.7 %shard_map.45 = (f32[2,2,16,256]{3,2,1,0:T(8,128)}, f32[8,40,256]{2,1,0:T(8,128)}) custom-call(s32[2]{0:T(128)} %pad_add_fusion.refs_2_.place.refs_1_, f32[8,3,256,256]{3,2,1,0:T(8,128)} %bitcast.10, f32[8,40,256]{2,1,0:T(8,128)} %copy-done.1), custom_call_target="tpu_custom_call" | custom-call | flops 150994944 | bytes 7012352 | tf_op jit(solution)/shard_map/pallas_call | solution.py:50
  145.1 6.5 %all-to-all-start.1 = ((f32[8,40,256]{2,1,0:T(8,128)}), f32[8,40,256]{2,1,0:T(8,128)S(1)}, u32[]{:S(2)}, u32[]{:S(2)}) async-start(f32[8,40,256]{2,1,0:T(8,128)} %get-tuple-element.33), calls=%async_computation.1 | async-start | bytes 655360 | tf_op jit(solution)/shard_map/all_to_all | solution.py:544
  151.5 10.4 %shard_map.46.refs_4_.own = f32[2,3,256,256]{3,2,1,0:T(8,128)} custom-call(f32[3,128,256]{2,1,0:T(8,128)} %shard_map.43.refs_0_, s32[2]{0:T(128)} %pad_add_fusion.refs_2_.place.refs_1_, f32[8,3,256,256]{3,2,1,0:T(8,128)} %bitcast.11), custom_call_target="tpu_custom_call" | custom-call | flops 3221225472 | bytes 7864320 | tf_op jit(solution)/shard_map/pallas_call | solution.py:50
  161.9 12.1 %shard_map.44.refs_0_.behind_ends = f32[544,256]{1,0:T(8,128)} custom-call(f32[3,128,256]{2,1,0:T(8,128)} %shard_map.43.refs_0_, bf16[16,256,256]{2,1,0:T(8,128)(2,1)} %get-tuple-element.25.high.refs_1_, bf16[16,256,256]{2,1,0:T(8,128)(2,1)} %get-tuple-element.26.low.refs_2_, f32[16,544,256]{2,1,0:T(8,128)} %get-tuple-element.32.refs_3_), custom_call_target="tpu_custom_call" | custom-call | flops 3422552064 | bytes 13664256 | tf_op jit(solution)/shard_map/pallas_call | solution.py:50
  174.0 20.0 %all-gather.10.cloned.1.call-done = f32[48,128,256]{2,1,0:T(8,128)} async-done(((f32[3,128,256]{2,1,0:T(8,128)}), f32[48,128,256]{2,1,0:T(8,128)}) %all-gather.10.cloned.1.call-update) | async-done | bytes 6291472 | tf_op jit(solution)/shard_map/all_gather | solution.py:562
  194.0 6.3 %shard_map.47 = (f32[2,16,256]{2,1,0:T(8,128)}, f32[2,16,256]{2,1,0:T(8,128)}, f32[8,256]{1,0:T(8,128)}) custom-call(f32[544,256]{1,0:T(8,128)} %shard_map.44.refs_0_.behind_ends, s32[2]{0:T(128)} %pad_add_fusion.1.refs_1_.place, f32[16,3,128,256]{3,2,1,0:T(8,128)} %bitcast.7, f32[8,40,256]{2,1,0:T(8,128)} %copy-done, ...), custom_call_target="tpu_custom_call" | custom-call | flops 150994944 | bytes 8331264 | tf_op jit(solution)/shard_map/pallas_call | solution.py:50
  200.3 2.3 collective-permute-start
  202.7 1.0 collective-permute-done.theirs
  203.6 0.6 copy-done.3
  204.2 8.8 %shard_map.48 = (f32[16,32,256]{2,1,0:T(8,128)}, f32[8,40,256]{2,1,0:T(8,128)}) custom-call(s32[2]{0:T(128)} %pad_add_fusion.refs_2_.place.refs_1_, bf16[16,256,256]{2,1,0:T(8,128)(2,1)} %get-tuple-element.25.high.refs_1_, bf16[16,256,256]{2,1,0:T(8,128)(2,1)} %get-tuple-element.26.low.refs_2_, f32[16,32,256]{2,1,0:T(8,128)} %source.3, ...), custom_call_target="tpu_custom_call" | custom-call | flops 402653184 | bytes 6750208 | tf_op jit(solution)/shard_map/pallas_call | solution.py:50
  213.0 11.8 %all_to_all.30.ends = f32[8,40,256]{2,1,0:T(8,128)} all-to-all(f32[8,40,256]{2,1,0:T(8,128)} %get-tuple-element.38), channel_id=1, replica_groups=mesh['outer'=8,'mid'=4,'core'=2,'cols'=8] {'mid','core'}, dimensions={0} | all-to-all | bytes 655360 | tf_op jit(solution)/shard_map/all_to_all | solution.py:544
  224.9 5.7 %shard_map.49 = (f32[2,2,16,256]{3,2,1,0:T(8,128)}, f32[8,40,256]{2,1,0:T(8,128)}) custom-call(s32[2]{0:T(128)} %pad_add_fusion.refs_2_.place.refs_1_, f32[8,3,256,256]{3,2,1,0:T(8,128)} %bitcast.12, f32[8,40,256]{2,1,0:T(8,128)} %all_to_all.30.ends), custom_call_target="tpu_custom_call" | custom-call | flops 150994944 | bytes 7012352 | tf_op jit(solution)/shard_map/pallas_call | solution.py:50
  230.5 15.7 %all_to_all.31.ends = f32[8,40,256]{2,1,0:T(8,128)} all-to-all(f32[8,40,256]{2,1,0:T(8,128)} %get-tuple-element.39), channel_id=1, replica_groups=mesh['outer'=8,'mid'=4,'core'=2,'cols'=8] {'outer'}, dimensions={0} | all-to-all | bytes 655360 | tf_op jit(solution)/shard_map/all_to_all | solution.py:544
  246.2 6.3 %shard_map.50 = (f32[2,16,256]{2,1,0:T(8,128)}, f32[2,16,256]{2,1,0:T(8,128)}, f32[8,256]{1,0:T(8,128)}) custom-call(s32[2]{0:T(128)} %pad_add_fusion.1.refs_1_.place, f32[16,3,128,256]{3,2,1,0:T(8,128)} %bitcast.8, f32[8,40,256]{2,1,0:T(8,128)} %all_to_all.31.ends, f32[2,3,256,256]{3,2,1,0:T(8,128)} %shard_map.46.refs_4_.own, ...), custom_call_target="tpu_custom_call" | custom-call | flops 150994944 | bytes 8331264 | tf_op jit(solution)/shard_map/pallas_call | solution.py:50
  252.6 4.8 %collective-permute-start.1 = (f32[2,16,256]{2,1,0:T(8,128)}, f32[2,16,256]{2,1,0:T(8,128)S(1)}, u32[]{:S(2)}, u32[]{:S(2)}) collective-permute-start(f32[2,16,256]{2,1,0:T(8,128)} %get-tuple-element.42), channel_id=1, source_target_pairs={{0,8},{8,0},{1,9},{9,1},{2,10},{10,2},{3,11},{11,3},{4,12},{12,4},... | collective-permute-start | bytes 98312 | tf_op jit(solution)/shard_map/ppermute | solution.py:583
  257.4 1.0 collective-permute-done.1.theirs
  258.4 0.6 copy-done.2
  259.0 8.3 %shard_map.51 = (f32[16,32,256]{2,1,0:T(8,128)}, f32[8,8,128]{2,1,0:T(8,128)}) custom-call(s32[2]{0:T(128)} %pad_add_fusion.refs_2_.place.refs_1_, bf16[16,256,256]{2,1,0:T(8,128)(2,1)} %get-tuple-element.25.high.refs_1_, bf16[16,256,256]{2,1,0:T(8,128)(2,1)} %get-tuple-element.26.low.refs_2_, f32[16,32,256]{2,1,0:T(8,128)} %get-tuple-element.37.source, ...), custom_call_target="tpu_custom_call" | custom-call | flops 402653184 | bytes 5349376 | tf_op jit(solution)/shard_map/pallas_call | solution.py:50
  267.4 8.3 %all_to_all.32 = f32[8,8,128]{2,1,0:T(8,128)S(1)} all-to-all(f32[8,8,128]{2,1,0:T(8,128)} %get-tuple-element.45), channel_id=1, replica_groups=mesh['outer'=8,'mid'=4,'core'=2,'cols'=8] {'mid','core'}, dimensions={0} | all-to-all | bytes 65536 | tf_op jit(solution)/shard_map/all_to_all | solution.py:544
  275.7 9.9 %all_to_all.33.squares = f32[8,8,128]{2,1,0:T(8,128)} all-to-all(f32[8,8,128]{2,1,0:T(8,128)S(1)} %broadcast_in_dim.2), channel_id=1, replica_groups=mesh['outer'=8,'mid'=4,'core'=2,'cols'=8] {'outer'}, dimensions={0} | all-to-all | bytes 65536 | tf_op jit(solution)/shard_map/all_to_all | solution.py:544
  285.6 2.0 shard_map.52
  287.6 1.2 slice_bitcast_fusion
  (14 shorter events, 0.1 us)
Async XLA Ops:
  7.2 66.7 %all-gather.6.cloned.1.call-start = ((), (), s32[]{:S(2)}) async-start(), calls=%async_computation.6 | async-start | bytes 4718592 | tf_op jit(solution)/shard_map/all_gather | solution.py:556
  7.9 123.5 %all-gather.8.cloned.1.call-start = ((), (), s32[]{:S(2)}) async-start(), calls=%async_computation.7 | async-start | bytes 7077888 | tf_op jit(solution)/shard_map/all_gather | solution.py:558
  87.1 24.8 %all-to-all-start = ((f32[8,40,256]{2,1,0:T(8,128)}), f32[8,40,256]{2,1,0:T(8,128)S(1)}, u32[]{:S(2)}, u32[]{:S(2)}) async-start(f32[8,40,256]{2,1,0:T(8,128)} %get-tuple-element.30), calls=%async_computation | async-start | bytes 655360 | tf_op jit(solution)/shard_map/all_to_all | solution.py:544
  92.0 101.9 %all-gather.10.cloned.1.call-start = ((), (), s32[]{:S(2)}) async-start(), calls=%async_computation.8 | async-start | bytes 6684672 | tf_op jit(solution)/shard_map/all_gather | solution.py:562
  111.9 19.5 %copy-start.1 = (f32[8,40,256]{2,1,0:T(8,128)}, f32[8,40,256]{2,1,0:T(8,128)S(1)}, u32[]{:S(2)}) copy-start(f32[8,40,256]{2,1,0:T(8,128)S(1)} %all-to-all-done.refs_1_.ends) | copy-start | bytes 983044
  145.1 28.9 %all-to-all-start.1 = ((f32[8,40,256]{2,1,0:T(8,128)}), f32[8,40,256]{2,1,0:T(8,128)S(1)}, u32[]{:S(2)}, u32[]{:S(2)}) async-start(f32[8,40,256]{2,1,0:T(8,128)} %get-tuple-element.33), calls=%async_computation.1 | async-start | bytes 655360 | tf_op jit(solution)/shard_map/all_to_all | solution.py:544
  174.0 20.0 %copy-start = (f32[8,40,256]{2,1,0:T(8,128)}, f32[8,40,256]{2,1,0:T(8,128)S(1)}, u32[]{:S(2)}) copy-start(f32[8,40,256]{2,1,0:T(8,128)S(1)} %all-to-all-done.1.refs_3_) | copy-start | bytes 983044
  200.3 3.3 %collective-permute-start = (f32[2,16,256]{2,1,0:T(8,128)}, f32[2,16,256]{2,1,0:T(8,128)S(1)}, u32[]{:S(2)}, u32[]{:S(2)}) collective-permute-start(f32[2,16,256]{2,1,0:T(8,128)} %get-tuple-element.36), channel_id=1, source_target_pairs={{0,8},{8,0},{1,9},{9,1},{2,10},{10,2},{3,11},{11,3},{4,12},{12,4},... | collective-permute-start | bytes 98312 | tf_op jit(solution)/shard_map/ppermute | solution.py:575
  203.6 0.6 copy-start.3
  252.6 5.8 %collective-permute-start.1 = (f32[2,16,256]{2,1,0:T(8,128)}, f32[2,16,256]{2,1,0:T(8,128)S(1)}, u32[]{:S(2)}, u32[]{:S(2)}) collective-permute-start(f32[2,16,256]{2,1,0:T(8,128)} %get-tuple-element.42), channel_id=1, source_target_pairs={{0,8},{8,0},{1,9},{9,1},{2,10},{10,2},{3,11},{11,3},{4,12},{12,4},... | collective-permute-start | bytes 98312 | tf_op jit(solution)/shard_map/ppermute | solution.py:583
  258.4 0.6 copy-start.2
Sparse Core Ops, SparseCore 0:
  10.1 63.7 all-gather.5
  86.7 44.7 all-gather.7
  138.9 55.0 all-gather.9
